TPU v7x, 32 devices: a whole 2x2x4 slice. The times are simulated.
32 devices in a mesh: dp: 8 (over z, x), seq: 4 (over y, core).
Axes of the slice: x: 2, y: 2, z: 4, core: 2. Of those that a mesh axis runs over, the one named last changes fastest.
Arguments:
- inputs: float32 [64, 1024, 256], P('dp', 'seq'), may hold values from -5 to 5
- encoded: float32 [64, 128, 256], P('dp'), may hold values from -5 to 5
- durations: int32 [64, 128], P('dp'), may hold values from 1 to 14
- lengths: int32 [64], P('dp'), may hold values from 512 to 1024, as said below
- time_embed: float32 [64, 1024], P('dp'), may hold values from -6 to 6
- cotangent: float32 [64, 1024, 256], P('dp', 'seq'), may hold values from -12 to 12
- res_master: float32 [722944], P(('dp', 'seq')), may hold values from -2 to 2
- res_moment: float32 [722944], P(('dp', 'seq'))
- res_average: float32 [722944], P(('dp', 'seq')), may hold values from -2 to 2
- tf_master: float32 [659968], P(('dp', 'seq')), may hold values from -2 to 2
- tf_moment: float32 [659968], P(('dp', 'seq'))
- tf_average: float32 [659968], P(('dp', 'seq')), may hold values from -2 to 2
Outputs:
- outputs: float32 [64, 1024, 256], P('dp', 'seq')
- grad_inputs: float32 [64, 1024, 256], P('dp', 'seq')
- res_grad: float32 [722944], P(('dp', 'seq'))
- tf_grad: float32 [659968], P(('dp', 'seq'))
- res_new: float32 [722944], P(('dp', 'seq'))
- tf_new: float32 [659968], P(('dp', 'seq'))
- res_moment_new: float32 [722944], P(('dp', 'seq'))
- tf_moment_new: float32 [659968], P(('dp', 'seq'))
- res_average_new: float32 [722944], P(('dp', 'seq'))
- tf_average_new: float32 [659968], P(('dp', 'seq'))
- res_low: bfloat16 [722944], P(('dp', 'seq'))
- tf_low: bfloat16 [659968], P(('dp', 'seq'))
Inputs may be any that keep to these rules, and one draw needn't show every extreme that they name: `lengths`: valid frames of an utterance; in every draw some utterance has all 1024 frames valid.
All inputs are finite; a program needn't handle non-finite values.
Results may differ from a plain program's by a relative error of at most 0.014.
The roundings to bfloat16 on the way count: a program that leaves them out, or rounds other values in their place, can miss the bound.
Values may be sent and summed in bfloat16 or wider, within the bound.
A program may use at most 192 MiB of HBM per device.

v0:
```python
import math

import jax
import jax.numpy as jnp
from jax import lax
from jax.sharding import PartitionSpec as P

C = 256
GROUPS = 8
TE = 1024
HEADS = 2
HD = 64
F = 1024


EPSILON = 1e-05
SCORE_SCALE = 0.125
MOMENTUM = 0.9
AVERAGE_DECAY = 0.99
LEARN_BASE = 0.015
MASK_FILL = -1e30


def extended(cells, sides, width):
    for axis, dim in sides:
        count = lax.axis_size(axis)
        ends = count - 1
        head = lax.slice_in_dim(cells, 0, width, axis=dim)
        tail = lax.slice_in_dim(cells, cells.shape[dim] - width, cells.shape[dim], axis=dim)
        cells = jnp.concatenate(
            [
                lax.ppermute(tail, axis, [(i, (i + 1) % count) for i in range(ends)]),
                cells,
                lax.ppermute(head, axis, [((i + 1) % count, i) for i in range(ends)]),
            ],
            axis=dim,
        )
    return cells


def soft_plus(signal):
    return jnp.log1p(jnp.exp(-jnp.abs(signal))) + jnp.maximum(signal, 0.0)


def mish_fn(signal):
    return signal * jnp.tanh(soft_plus(signal))


def snake_fn(signal, alpha_row, beta_row):
    return signal + jnp.sin(signal * jnp.exp(alpha_row)) ** 2 / (jnp.exp(beta_row) + 1e-09)


def layer_norm(signal, gain_row, shift_row):
    center = signal - jnp.mean(signal, axis=-1, keepdims=True)
    spread = jnp.mean(center * center, axis=-1, keepdims=True)
    return center * lax.rsqrt(spread + EPSILON) * gain_row + shift_row


def unpack_res(flat):
    square = C * C
    conv_one = flat[0 : 3 * square].reshape(3, C, C)
    conv_two = flat[3 * square : 6 * square].reshape(3, C, C)
    res_weight = flat[6 * square : 7 * square].reshape(C, C)
    time_weight = flat[7 * square : 7 * square + TE * C].reshape(TE, C)
    offset = 7 * square + TE * C
    small_rows = flat[offset : offset + 8 * C].reshape(8, C)
    return (conv_one, conv_two, res_weight, time_weight, small_rows)


def unpack_tf(flat):
    inner = HEADS * HD
    qkv_weight = flat[0 : 3 * C * inner].reshape(C, 3 * inner)
    offset = 3 * C * inner
    out_weight = flat[offset : offset + inner * C].reshape(inner, C)
    offset = offset + inner * C
    up_weight = flat[offset : offset + C * F].reshape(C, F)
    offset = offset + C * F
    down_weight = flat[offset : offset + F * C].reshape(F, C)
    offset = offset + F * C
    small_rows = flat[offset : offset + 6 * C].reshape(6, C)
    offset = offset + 6 * C
    wide_rows = flat[offset : offset + 3 * F].reshape(3, F)
    return (qkv_weight, out_weight, up_weight, down_weight, small_rows, wide_rows)


def take_rows(phone_table, phone_rows):
    return phone_table[phone_rows]


def rim_pad(signal):
    return extended(signal, (("seq", 1),), 1)


def conv_apply(padded, weight):
    length_here = padded.shape[1] - 2
    result = jnp.dot(padded[:, 0:length_here], weight[0], preferred_element_type=jnp.float32)
    result = result + jnp.dot(
        padded[:, 1 : length_here + 1], weight[1], preferred_element_type=jnp.float32
    )
    return result + jnp.dot(padded[:, 2:], weight[2], preferred_element_type=jnp.float32)


def conv_weight_grad(padded, grad_low):
    length_here = grad_low.shape[1]
    return jnp.stack(
        [
            jnp.einsum(
                "utc,utd->cd",
                padded[:, tap_index : tap_index + length_here],
                grad_low,
                preferred_element_type=jnp.float32,
            )
            for tap_index in range(3)
        ]
    )


def conv_input_grad(grad_low, weight):
    padded = extended(grad_low, (("seq", 1),), 1)
    length_here = grad_low.shape[1]
    result = jnp.einsum("utd,cd->utc", padded[:, 2:], weight[0], preferred_element_type=jnp.float32)
    result = result + jnp.einsum(
        "utd,cd->utc", padded[:, 1 : length_here + 1], weight[1], preferred_element_type=jnp.float32
    )
    return result + jnp.einsum(
        "utd,cd->utc", padded[:, 0:length_here], weight[2], preferred_element_type=jnp.float32
    )


def norm_forward(signal, frame_mask, valid_count, gain_row, shift_row):
    width = C // GROUPS
    shape_now = signal.shape
    grouped = (signal * frame_mask[:, :, None]).reshape(shape_now[0], shape_now[1], GROUPS, width)
    total = jnp.sum(grouped, axis=(1, 3))
    squares = jnp.sum(grouped * grouped, axis=(1, 3))
    total, squares = lax.psum((total, squares), "seq")
    number = valid_count[:, None] * width
    mean_now = total / number
    inv_std = lax.rsqrt(squares / number - mean_now * mean_now + EPSILON)
    mean_wide = jnp.repeat(mean_now, width, axis=1)[:, None, :]
    inv_wide = jnp.repeat(inv_std, width, axis=1)[:, None, :]
    normed = (signal - mean_wide) * inv_wide
    return (normed * gain_row + shift_row, normed, inv_wide)


def norm_backward(grad_out, normed, inv_wide, frame_mask, valid_count, gain_row):
    width = C // GROUPS
    shape_now = grad_out.shape
    grad_norm = grad_out * gain_row
    first_sum = jnp.sum(grad_norm.reshape(shape_now[0], shape_now[1], GROUPS, width), axis=(1, 3))
    second_sum = jnp.sum(
        (grad_norm * normed).reshape(shape_now[0], shape_now[1], GROUPS, width), axis=(1, 3)
    )
    first_sum, second_sum = lax.psum((first_sum, second_sum), "seq")
    number = valid_count[:, None] * width
    first_wide = jnp.repeat(first_sum / number, width, axis=1)[:, None, :]
    second_wide = jnp.repeat(second_sum / number, width, axis=1)[:, None, :]
    grad_signal = inv_wide * (
        grad_norm - frame_mask[:, :, None] * (first_wide + normed * second_wide)
    )
    grad_gain = jnp.sum(grad_out * normed, axis=(0, 1))
    grad_shift = jnp.sum(grad_out, axis=(0, 1))
    return (grad_signal, grad_gain, grad_shift)


def update(master, moment, average, grad, rate):
    moment_new = MOMENTUM * moment + grad
    master_new = master - rate * (grad + MOMENTUM * moment_new)
    average_new = AVERAGE_DECAY * average + (1.0 - AVERAGE_DECAY) * master_new
    return (master_new, moment_new, average_new, master_new.astype(jnp.bfloat16))


def per_device(
    inputs,
    encoded,
    durations,
    lengths,
    time_embed,
    cotangent,
    res_master,
    res_moment,
    res_average,
    tf_master,
    tf_moment,
    tf_average,
):
    utt_count, local_len, _ = inputs.shape
    key_total = local_len * lax.axis_size("seq")
    inner = HEADS * HD
    seq_index = lax.axis_index("seq")
    frame_ids = seq_index * local_len + jnp.arange(local_len, dtype=jnp.int32)
    frame_mask = (frame_ids[None, :] < lengths[:, None]).astype(jnp.float32)
    wide_mask = frame_mask[:, :, None]
    key_mask = jnp.arange(key_total, dtype=jnp.int32)[None, :] < lengths[:, None]
    valid_count = lengths.astype(jnp.float32)
    boundary = jnp.cumsum(durations, axis=1)
    phone = jnp.sum((boundary[:, None, :] <= frame_ids[None, :, None]).astype(jnp.int32), axis=2)
    phone = jnp.minimum(phone, durations.shape[1] - 1)
    start_state = inputs + jax.vmap(take_rows)(encoded, phone)
    res_whole = lax.all_gather(res_master.astype(jnp.bfloat16), ("dp", "seq"), axis=0, tiled=True)
    conv_one, conv_two, res_weight, time_weight, res_rows = unpack_res(res_whole)
    res_small = res_rows.astype(jnp.float32)
    masked_in = (start_state * wide_mask).astype(jnp.bfloat16)
    padded_one = rim_pad(masked_in)
    z_one = conv_apply(padded_one, conv_one) + res_small[0]
    norm_one, normed_one, inv_one = norm_forward(
        z_one, frame_mask, valid_count, res_small[1], res_small[2]
    )
    act_one = mish_fn(norm_one) * wide_mask
    time_act = mish_fn(time_embed).astype(jnp.bfloat16)
    time_proj = jnp.dot(time_act, time_weight, preferred_element_type=jnp.float32) + res_small[7]
    masked_two = ((act_one + time_proj[:, None, :]) * wide_mask).astype(jnp.bfloat16)
    padded_two = rim_pad(masked_two)
    z_two = conv_apply(padded_two, conv_two) + res_small[3]
    norm_two, normed_two, inv_two = norm_forward(
        z_two, frame_mask, valid_count, res_small[4], res_small[5]
    )
    act_two = mish_fn(norm_two) * wide_mask
    skip_out = jnp.dot(masked_in, res_weight, preferred_element_type=jnp.float32) + res_small[6]
    block_out = act_two + skip_out
    tf_whole = lax.all_gather(tf_master.astype(jnp.bfloat16), ("dp", "seq"), axis=0, tiled=True)
    qkv_weight, out_weight, up_weight, down_weight, tf_rows, wide_rows = unpack_tf(tf_whole)
    tf_small = tf_rows.astype(jnp.float32)
    wide_small = wide_rows.astype(jnp.float32)
    attn_in = layer_norm(block_out, tf_small[0], tf_small[1]).astype(jnp.bfloat16)
    qkv_all = jnp.dot(attn_in, qkv_weight, preferred_element_type=jnp.float32).astype(jnp.bfloat16)
    queries = qkv_all[:, :, :inner].reshape(utt_count, local_len, HEADS, HD)
    kv_whole = lax.all_gather(qkv_all[:, :, inner:], "seq", axis=1, tiled=True)
    keys = kv_whole[:, :, :inner].reshape(utt_count, key_total, HEADS, HD)
    values = kv_whole[:, :, inner:].reshape(utt_count, key_total, HEADS, HD)
    scores = (
        jnp.einsum("uqhd,ukhd->uhqk", queries, keys, preferred_element_type=jnp.float32)
        * SCORE_SCALE
    )
    scores = jnp.where(key_mask[:, None, None, :], scores, MASK_FILL)
    top_score = jnp.max(scores, axis=-1, keepdims=True)
    expo = jnp.exp(scores - top_score)
    row_total = jnp.sum(expo, axis=-1, keepdims=True)
    log_total = top_score + jnp.log(row_total)
    probs_low = (expo / row_total).astype(jnp.bfloat16)
    attn_vals = jnp.einsum("uhqk,ukhd->uqhd", probs_low, values, preferred_element_type=jnp.float32)
    attn_vals = attn_vals.reshape(utt_count, local_len, inner).astype(jnp.bfloat16)
    attn_out = jnp.dot(attn_vals, out_weight, preferred_element_type=jnp.float32) + tf_small[2]
    mid_state = block_out + attn_out
    ff_in = layer_norm(mid_state, tf_small[3], tf_small[4]).astype(jnp.bfloat16)
    up_out = jnp.dot(ff_in, up_weight, preferred_element_type=jnp.float32) + wide_small[0]
    snake_out = snake_fn(up_out, wide_small[1], wide_small[2]).astype(jnp.bfloat16)
    ff_out = jnp.dot(snake_out, down_weight, preferred_element_type=jnp.float32) + tf_small[5]
    final = (mid_state + ff_out) * wide_mask
    tf_back = lax.all_gather(tf_master.astype(jnp.bfloat16), ("dp", "seq"), axis=0, tiled=True)
    qkv_weight, out_weight, up_weight, down_weight, tf_rows, wide_rows = unpack_tf(tf_back)
    grad_final = cotangent * wide_mask
    grad_ff = grad_final.astype(jnp.bfloat16)
    grad_down_w = jnp.einsum("utf,utc->fc", snake_out, grad_ff, preferred_element_type=jnp.float32)
    grad_down_b = jnp.sum(grad_ff, axis=(0, 1), dtype=jnp.float32)
    grad_snake = jnp.einsum("utc,fc->utf", grad_ff, down_weight, preferred_element_type=jnp.float32)
    snake_value, snake_pull = jax.vjp(snake_fn, up_out, wide_small[1], wide_small[2])
    grad_up_f, grad_alpha, grad_beta = snake_pull(grad_snake)
    grad_up = grad_up_f.astype(jnp.bfloat16)
    grad_up_w = jnp.einsum("utc,utf->cf", ff_in, grad_up, preferred_element_type=jnp.float32)
    grad_up_b = jnp.sum(grad_up, axis=(0, 1), dtype=jnp.float32)
    grad_ff_in = jnp.einsum("utf,cf->utc", grad_up, up_weight, preferred_element_type=jnp.float32)
    norm_value, norm_pull = jax.vjp(layer_norm, mid_state, tf_small[3], tf_small[4])
    grad_mid_ln, grad_ln3_g, grad_ln3_b = norm_pull(grad_ff_in)
    grad_mid = grad_final + grad_mid_ln
    grad_attn = grad_mid.astype(jnp.bfloat16)
    grad_out_w = jnp.einsum("uti,utc->ic", attn_vals, grad_attn, preferred_element_type=jnp.float32)
    grad_out_b = jnp.sum(grad_attn, axis=(0, 1), dtype=jnp.float32)
    grad_vals = jnp.einsum("utc,ic->uti", grad_attn, out_weight, preferred_element_type=jnp.float32)
    grad_vals = grad_vals.astype(jnp.bfloat16).reshape(utt_count, local_len, HEADS, HD)
    scores = (
        jnp.einsum("uqhd,ukhd->uhqk", queries, keys, preferred_element_type=jnp.float32)
        * SCORE_SCALE
    )
    scores = jnp.where(key_mask[:, None, None, :], scores, MASK_FILL)
    probs = jnp.exp(scores - log_total)
    probs_low = probs.astype(jnp.bfloat16)
    grad_probs = jnp.einsum(
        "uqhd,ukhd->uhqk", grad_vals, values, preferred_element_type=jnp.float32
    )
    row_dot = jnp.sum(probs * grad_probs, axis=-1, keepdims=True)
    grad_scores = (probs * (grad_probs - row_dot)).astype(jnp.bfloat16)
    grad_query = (
        jnp.einsum("uhqk,ukhd->uqhd", grad_scores, keys, preferred_element_type=jnp.float32)
        * SCORE_SCALE
    )
    grad_key = (
        jnp.einsum("uhqk,uqhd->ukhd", grad_scores, queries, preferred_element_type=jnp.float32)
        * SCORE_SCALE
    )
    grad_value = jnp.einsum(
        "uhqk,uqhd->ukhd", probs_low, grad_vals, preferred_element_type=jnp.float32
    )
    grad_kv = jnp.concatenate(
        [
            grad_key.reshape(utt_count, key_total, inner),
            grad_value.reshape(utt_count, key_total, inner),
        ],
        axis=2,
    )
    grad_kv_local = lax.psum_scatter(grad_kv, "seq", scatter_dimension=1, tiled=True)
    grad_qkv = jnp.concatenate(
        [grad_query.reshape(utt_count, local_len, inner), grad_kv_local], axis=2
    ).astype(jnp.bfloat16)
    grad_qkv_w = jnp.einsum("utc,utd->cd", attn_in, grad_qkv, preferred_element_type=jnp.float32)
    grad_attn_in = jnp.einsum(
        "utd,cd->utc", grad_qkv, qkv_weight, preferred_element_type=jnp.float32
    )
    block_value, block_pull = jax.vjp(layer_norm, block_out, tf_small[0], tf_small[1])
    grad_block_ln, grad_ln1_g, grad_ln1_b = block_pull(grad_attn_in)
    grad_block = grad_mid + grad_block_ln
    tf_grad_local = jnp.concatenate(
        [
            grad_qkv_w.reshape(-1),
            grad_out_w.reshape(-1),
            grad_up_w.reshape(-1),
            grad_down_w.reshape(-1),
            jnp.stack(
                [grad_ln1_g, grad_ln1_b, grad_out_b, grad_ln3_g, grad_ln3_b, grad_down_b]
            ).reshape(-1),
            jnp.stack([grad_up_b, grad_alpha, grad_beta]).reshape(-1),
        ]
    )
    tf_share = lax.psum_scatter(tf_grad_local, ("dp", "seq"), scatter_dimension=0, tiled=True)
    res_back = lax.all_gather(res_master.astype(jnp.bfloat16), ("dp", "seq"), axis=0, tiled=True)
    conv_one, conv_two, res_weight, time_weight, res_rows = unpack_res(res_back)
    grad_skip = grad_block.astype(jnp.bfloat16)
    grad_res_w = jnp.einsum("utc,utd->cd", masked_in, grad_skip, preferred_element_type=jnp.float32)
    grad_res_b = jnp.sum(grad_skip, axis=(0, 1), dtype=jnp.float32)
    grad_masked_in = jnp.einsum(
        "utd,cd->utc", grad_skip, res_weight, preferred_element_type=jnp.float32
    )
    mish_two, mish_pull_two = jax.vjp(mish_fn, norm_two)
    (grad_norm_two,) = mish_pull_two(grad_block * wide_mask)
    grad_z_two, grad_gn2_g, grad_gn2_b = norm_backward(
        grad_norm_two, normed_two, inv_two, frame_mask, valid_count, res_small[4]
    )
    grad_z_two = grad_z_two.astype(jnp.bfloat16)
    grad_conv_two = conv_weight_grad(padded_two, grad_z_two)
    grad_conv_two_b = jnp.sum(grad_z_two, axis=(0, 1), dtype=jnp.float32)
    grad_hidden = conv_input_grad(grad_z_two, conv_two) * wide_mask
    grad_time_proj = jnp.sum(grad_hidden, axis=1)
    grad_time_w = jnp.dot(
        time_act.astype(jnp.float32).T, grad_time_proj, precision=lax.Precision.HIGHEST
    )
    grad_time_b = jnp.sum(grad_time_proj, axis=0)
    mish_one, mish_pull_one = jax.vjp(mish_fn, norm_one)
    (grad_norm_one,) = mish_pull_one(grad_hidden * wide_mask)
    grad_z_one, grad_gn1_g, grad_gn1_b = norm_backward(
        grad_norm_one, normed_one, inv_one, frame_mask, valid_count, res_small[1]
    )
    grad_z_one = grad_z_one.astype(jnp.bfloat16)
    grad_conv_one = conv_weight_grad(padded_one, grad_z_one)
    grad_conv_one_b = jnp.sum(grad_z_one, axis=(0, 1), dtype=jnp.float32)
    grad_masked_in = grad_masked_in + conv_input_grad(grad_z_one, conv_one)
    grad_inputs = grad_masked_in * wide_mask
    res_grad_local = jnp.concatenate(
        [
            grad_conv_one.reshape(-1),
            grad_conv_two.reshape(-1),
            grad_res_w.reshape(-1),
            grad_time_w.reshape(-1),
            jnp.stack(
                [
                    grad_conv_one_b,
                    grad_gn1_g,
                    grad_gn1_b,
                    grad_conv_two_b,
                    grad_gn2_g,
                    grad_gn2_b,
                    grad_res_b,
                    grad_time_b,
                ]
            ).reshape(-1),
        ]
    )
    res_share = lax.psum_scatter(res_grad_local, ("dp", "seq"), scatter_dimension=0, tiled=True)
    tokens_total = utt_count * key_total * lax.axis_size("dp")
    rate = LEARN_BASE / math.sqrt(tokens_total)
    res_new, res_moment_new, res_average_new, res_low = update(
        res_master, res_moment, res_average, res_share, rate
    )
    tf_new, tf_moment_new, tf_average_new, tf_low = update(
        tf_master, tf_moment, tf_average, tf_share, rate
    )
    return (
        final,
        grad_inputs,
        res_share,
        tf_share,
        res_new,
        tf_new,
        res_moment_new,
        tf_moment_new,
        res_average_new,
        tf_average_new,
        res_low,
        tf_low,
    )


def solution(mesh):
    placed = (
        P("dp", "seq", None),
        P("dp", None, None),
        P("dp", None),
        P("dp"),
        P("dp", None),
        P("dp", "seq", None),
        P(("dp", "seq")),
        P(("dp", "seq")),
        P(("dp", "seq")),
        P(("dp", "seq")),
        P(("dp", "seq")),
        P(("dp", "seq")),
    )
    return jax.shard_map(
        per_device,
        mesh=mesh,
        in_specs=placed,
        out_specs=(
            P("dp", "seq", None),
            P("dp", "seq", None),
            P(("dp", "seq")),
            P(("dp", "seq")),
            P(("dp", "seq")),
            P(("dp", "seq")),
            P(("dp", "seq")),
            P(("dp", "seq")),
            P(("dp", "seq")),
            P(("dp", "seq")),
            P(("dp", "seq")),
            P(("dp", "seq")),
        ),
        check_vma=False,
    )
```

profile of v0, /device:TPU:0, one launch (start us, length us, event | category | flops | bytes accessed | tf_op | source)
XLA Modules:
  0.0 690.7 jit_solution(5647994302986426264)
XLA Ops:
  14.5 14.1 %gather_fusion = f32[2048,256]{1,0:T(8,128)S(1)} fusion(f32[8,128,256]{2,1,0:T(8,128)S(1)} %copy-done, s32[2048]{0:T(1024)S(1)} %bitcast.147), kind=kCustom, calls=%fused_computation | custom fusion | bytes 4210688 | tf_op jit(solution)/shard_map/vmap()/gather | solution.py:87
  32.6 3.6 collective-permute-start
  37.5 116.1 %all-reduce.15.cloned.1.call-done = (bf16[722944]{0:T(1024)(128)(2,1)}, bf16[659968]{0:T(1024)(128)(2,1)}) async-done(((bf16[722944]{0:T(1024)(128)(2,1)}, bf16[659968]{0:T(1024)(128)(2,1)}), (bf16[722944]{0:T(1024)(128)(2,1)}, bf16[659968]{0:T(1024)(128)(2,1)})) %all-reduce.15.cloned.1.call-update) | async-done | bytes 2765840
  168.6 4.4 multiply_reduce_fusion.16
  174.8 6.4 all-reduce.8
  183.5 4.8 convert_reduce_fusion.1
  202.0 8.4 %all-reduce.7 = (f32[8,8]{1,0:T(8,128)S(1)}, f32[8,8]{1,0:T(8,128)S(1)}) all-reduce(f32[8,8]{1,0:T(8,128)S(1)} %reduce_sum.457, f32[8,8]{1,0:T(8,128)S(1)} %reduce_sum.454), channel_id=1, replica_groups=mesh['dp'=8,'seq'=4] {'seq'}, use_global_device_ids=true, to_apply=%region_13.14 | all-reduce | flops 128 | bytes 1024 | tf_op jit(solution)/shard_map/psum | solution.py:136
  224.4 5.9 fusion.68
  233.2 18.4 %all-gather.2.cloned.1.call-done = bf16[8,1024,256]{2,1,0:T(8,128)(2,1)} async-done(((bf16[8,256,256]{2,1,0:T(8,128)(2,1)}), bf16[8,1024,256]{2,1,0:T(8,128)(2,1)}) %all-gather.2.cloned.1.call-update) | async-done | bytes 4194320 | tf_op jit(solution)/shard_map/all_gather | solution.py:228
  251.7 4.0 fusion.54
  255.6 4.3 copy.80
  262.5 4.6 fusion.64
  267.2 3.7 fusion
  270.9 4.3 fusion.7
  277.4 40.5 %multiply_reduce_fusion.2 = (f32[1024]{0:T(1024)}, f32[1024]{0:T(1024)}, f32[1024]{0:T(1024)}, bf16[8,256,1024]{2,1,0:T(8,128)(2,1)S(1)}, bf16[8,256,1024]{2,1,0:T(8,128)(2,1)}) fusion(f32[1024]{0:T(1024)S(1)} %copy-done.124, f32[1024]{0:T(1024)S(1)} %copy-done.123, f32[8,256,1024]{2,1,0:T(8,128)} %fusion.68, f32[1024]{0:T(1024)S(1)} %copy-done.122, ...), kind=kOutput, calls=%fused_computation.12 | convolution fusion | flops 1118303232 | bytes 19445760 | tf_op jit(solution)/shard_map/dot_general | solution.py:246
  326.9 4.3 fusion.2
  331.3 21.6 %multiply_reduce_fusion = (f32[8,2,256]{2,1,0:T(2,128)}, f32[8,2,256,1024]{3,2,1,0:T(8,128)}) fusion(f32[8,2,256,1024]{3,2,1,0:T(8,128)S(1)} %get-tuple-element.134, f32[8,2,256]{2,1,0:T(2,128)} %bitcast.172, bf16[8,256,2,64]{1,3,2,0:T(8,128)(2,1)} %bitcast.158, bf16[8,1024,2,64]{1,3,2,0:T(8,128)(2,1)} %bitcast.153), kind=kOutput, calls=%fused_computation.2 | convolution fusion | flops 549449728 | bytes 36208640 | tf_op jit(solution)/shard_map/uqhd,ukhd->uhqk/dot_general | solution.py:278
  352.9 5.3 copy.83
  358.2 11.8 %multiply_convert_fusion = bf16[8,2,256,1024]{3,2,1,0:T(8,128)(2,1)S(1)} fusion(f32[8,2,256,1024]{3,2,1,0:T(8,128)} %get-tuple-element.139, f32[8,2,256,1024]{3,2,1,0:T(8,128)} %copy-done.2, f32[8,2,256]{2,1,0:T(2,128)S(1)} %copy-done.91, f32[8,2,256]{2,1,0:T(2,128)S(1)} %bitcast.173), kind=kLoop, calls=%fused_computation.1 | loop fusion | flops 16777216 | bytes 41975808 | tf_op jit(solution)/shard_map/convert_element_type | solution.py:282
  370.1 4.1 convolution_multiply_fusion
  374.6 5.3 copy.82
  379.9 7.3 %pad_maximum_fusion = f32[8,1024,256]{2,1,0:T(8,128)} fusion(f32[8,1024,128]{2,1,0:T(8,128)} %copy.83, f32[8,1024,128]{2,1,0:T(8,128)} %copy.82), kind=kLoop, calls=%fused_computation.10 | loop fusion | flops 2097152 | bytes 16777216 | tf_op jit(solution)/shard_map/concatenate | solution.py:294
  394.3 5.3 convolution_bitcast_fusion.1
  403.0 6.9 fusion.6
  412.2 46.5 %reduce-scatter.2.cloned.1.call-done = f32[8,256,256]{2,1,0:T(8,128)} async-done(((f32[8,1024,256]{2,1,0:T(8,128)}), f32[8,256,256]{2,1,0:T(8,128)}) %reduce-scatter.2.cloned.1.call-update) | async-done | bytes 2097168 | tf_op jit(solution)/shard_map/reduce_scatter | solution.py:301
  466.9 5.3 multiply_reduce_fusion.5
  472.5 6.1 all-reduce.6
  479.0 3.7 convert_reduce_fusion.4
  500.8 5.8 fusion.49
  506.9 8.0 %all-reduce.5 = (f32[8,8]{1,0:T(8,128)S(1)}, f32[8,8]{1,0:T(8,128)S(1)}) all-reduce(f32[8,8]{1,0:T(8,128)S(1)} %reduce_sum.479, f32[8,8]{1,0:T(8,128)S(1)} %reduce_sum.476), channel_id=1, replica_groups=mesh['dp'=8,'seq'=4] {'seq'}, use_global_device_ids=true, to_apply=%region_37.38 | all-reduce | flops 128 | bytes 1024 | tf_op jit(solution)/shard_map/psum | solution.py:154
  529.2 5.0 add_multiply_fusion.2
  543.6 135.6 %all-reduce.13.cloned.1.call-done = (f32[722944]{0:T(1024)}, f32[659968]{0:T(1024)}) async-done(((f32[722944]{0:T(1024)}, f32[659968]{0:T(1024)}), (f32[722944]{0:T(1024)}, f32[659968]{0:T(1024)})) %all-reduce.13.cloned.1.call-update) | async-done | bytes 5531664
  (461 shorter events, 143.8 us)
Async XLA Ops:
  7.2 146.3 %all-reduce.15.cloned.1.call-start = ((), (), s32[]{:S(2)}) async-start(), calls=%async_computation.4 | async-start | bytes 5533696
  13.7 238.0 %all-gather.2.cloned.1.call-start = ((), (), s32[]{:S(2)}) async-start(), calls=%async_computation.1 | async-start | bytes 5242880 | tf_op jit(solution)/shard_map/all_gather | solution.py:228
  31.3 137.3 %collective-permute-start.1 = (bf16[8,1,256]{2,1,0:T(2,128)(2,1)}, bf16[8,1,256]{2,1,0:T(2,128)(2,1)}, u32[]{:S(2)}, u32[]{:S(2)}) collective-permute-start(bf16[8,1,256]{2,1,0:T(2,128)(2,1)} %get-tuple-element.98), channel_id=1, source_target_pairs={{1,0},{2,1},{3,2},{5,4},{6,5},{7,6},{9,8},{10,9},{11,10},{13,12},{... | collective-permute-start | bytes 12296 | tf_op jit(solution)/shard_map/ppermute | solution.py:34
  32.6 127.3 %collective-permute-start = (bf16[8,1,256]{2,1,0:T(2,128)(2,1)}, bf16[8,1,256]{2,1,0:T(2,128)(2,1)}, u32[]{:S(2)}, u32[]{:S(2)}) collective-permute-start(bf16[8,1,256]{2,1,0:T(2,128)(2,1)} %get-tuple-element.99), channel_id=1, source_target_pairs={{0,1},{1,2},{2,3},{4,5},{5,6},{6,7},{8,9},{9,10},{10,11},{12,13},{... | collective-permute-start | bytes 12296 | tf_op jit(solution)/shard_map/ppermute | solution.py:32
  158.9 24.6 %copy-start.95 = (f32[256]{0:T(256)}, f32[256]{0:T(256)S(1)}, u32[]{:S(2)}) copy-start(f32[256]{0:T(256)S(1)} %get-tuple-element.119) | copy-start | bytes 3076
  167.6 22.1 %copy-start.42 = (bf16[256,256,1]{1,0,2:T(8,128)(2,1)}, bf16[256,256,1]{1,0,2:T(8,128)(2,1)S(1)}, u32[]{:S(2)}) copy-start(bf16[256,256,1]{1,0,2:T(8,128)(2,1)S(1)} %reshape.515) | copy-start | bytes 393220
  188.3 8.0 %collective-permute-start.2 = (bf16[8,1,256]{2,1,0:T(2,128)(2,1)S(1)}, bf16[8,1,256]{2,1,0:T(2,128)(2,1)S(1)}, u32[]{:S(2)}, u32[]{:S(2)}) collective-permute-start(bf16[8,1,256]{2,1,0:T(2,128)(2,1)S(1)} %get-tuple-element.97), channel_id=1, source_target_pairs={{0,1},{1,2},{2,3},{4,5},{5,6},{6,7},{8,9},{9,10},{10,11},{12,13},{... | collective-permute-start | bytes 12296 | tf_op jit(solution)/shard_map/ppermute | solution.py:32
  192.1 23.0 %copy-start.98 = (f32[256]{0:T(256)}, f32[256]{0:T(256)S(1)}, u32[]{:S(2)}) copy-start(f32[256]{0:T(256)S(1)} %get-tuple-element.112) | copy-start | bytes 3076
  192.1 23.1 %copy-start.114 = (f32[256]{0:T(256)}, f32[256]{0:T(256)S(1)}, u32[]{:S(2)}) copy-start(f32[256]{0:T(256)S(1)} %get-tuple-element.111) | copy-start | bytes 3076
  194.9 4.5 collective-permute-start.3
  217.3 241.4 %reduce-scatter.2.cloned.1.call-start = ((), (), s32[]{:S(2)}) async-start(), calls=%async_computation.2 | async-start | bytes 10485760 | tf_op jit(solution)/shard_map/reduce_scatter | solution.py:301
  267.1 64.1 %copy-start.2 = (f32[8,2,256,1024]{3,2,1,0:T(8,128)}, f32[8,2,256,1024]{3,2,1,0:T(8,128)S(1)}, u32[]{:S(2)}) copy-start(f32[8,2,256,1024]{3,2,1,0:T(8,128)S(1)} %get-tuple-element.134) | copy-start | bytes 50331652
  276.0 45.9 %copy-start.7 = (f32[8,256,256]{2,1,0:T(8,128)}, f32[8,256,256]{2,1,0:T(8,128)S(1)}, u32[]{:S(2)}) copy-start(f32[8,256,256]{2,1,0:T(8,128)S(1)} %get-tuple-element.136) | copy-start | bytes 6291460
  276.1 45.9 %copy-start.69 = (f32[8,256]{1,0:T(8,128)}, f32[8,256]{1,0:T(8,128)S(1)}, u32[]{:S(2)}) copy-start(f32[8,256]{1,0:T(8,128)S(1)} %broadcast_multiply_fusion) | copy-start | bytes 24580
  276.7 45.2 %copy-start.89 = (f32[8,256]{1,0:T(8,128)}, f32[8,256]{1,0:T(8,128)S(1)}, u32[]{:S(2)}) copy-start(f32[8,256]{1,0:T(8,128)S(1)} %fusion.29) | copy-start | bytes 24580
  387.2 291.9 %all-reduce.13.cloned.1.call-start = ((), (), s32[]{:S(2)}) async-start(), calls=%async_computation.3 | async-start | bytes 11067392
  409.8 50.6 %copy-start.6 = (f32[8,256,256]{2,1,0:T(8,128)S(1)}, f32[8,256,256]{2,1,0:T(8,128)}, u32[]{:S(2)}) copy-start(f32[8,256,256]{2,1,0:T(8,128)} %copy-done.4) | copy-start | bytes 6291460
  409.8 50.6 %copy-start.67 = (f32[8,256]{1,0:T(8,128)S(1)}, f32[8,256]{1,0:T(8,128)}, u32[]{:S(2)}) copy-start(f32[8,256]{1,0:T(8,128)} %copy-done.66) | copy-start | bytes 24580
  409.8 50.6 %copy-start.86 = (f32[8,256]{1,0:T(8,128)S(1)}, f32[8,256]{1,0:T(8,128)}, u32[]{:S(2)}) copy-start(f32[8,256]{1,0:T(8,128)} %copy-done.85) | copy-start | bytes 24580
  409.8 50.6 %copy-start.99 = (f32[256]{0:T(256)S(1)}, f32[256]{0:T(256)}, u32[]{:S(2)}) copy-start(f32[256]{0:T(256)} %copy-done.98) | copy-start | bytes 3076
  409.8 50.6 %copy-start.115 = (f32[256]{0:T(256)S(1)}, f32[256]{0:T(256)}, u32[]{:S(2)}) copy-start(f32[256]{0:T(256)} %copy-done.114) | copy-start | bytes 3076
  489.9 9.4 %collective-permute-start.5 = (bf16[8,1,256]{2,1,0:T(2,128)(2,1)}, bf16[8,1,256]{2,1,0:T(2,128)(2,1)S(1)}, u32[]{:S(2)}, u32[]{:S(2)}) collective-permute-start(bf16[8,1,256]{2,1,0:T(2,128)(2,1)} %get-tuple-element.94), channel_id=1, source_target_pairs={{0,1},{1,2},{2,3},{4,5},{5,6},{6,7},{8,9},{9,10},{10,11},{12,13},{... | collective-permute-start | bytes 12296 | tf_op jit(solution)/shard_map/ppermute | solution.py:32
  491.7 7.1 %collective-permute-start.4 = (bf16[8,1,256]{2,1,0:T(2,128)(2,1)}, bf16[8,1,256]{2,1,0:T(2,128)(2,1)S(1)}, u32[]{:S(2)}, u32[]{:S(2)}) collective-permute-start(bf16[8,1,256]{2,1,0:T(2,128)(2,1)} %get-tuple-element.95), channel_id=1, source_target_pairs={{1,0},{2,1},{3,2},{5,4},{6,5},{7,6},{9,8},{10,9},{11,10},{13,12},{... | collective-permute-start | bytes 12296 | tf_op jit(solution)/shard_map/ppermute | solution.py:34
  535.6 5.1 collective-permute-start.6
  537.5 4.0 collective-permute-start.7
  541.2 137.9 %copy-start.60 = (f32[22592]{0:T(1024)S(1)}, f32[22592]{0:T(1024)}, u32[]{:S(2)}) copy-start(f32[22592]{0:T(1024)} %param.18) | copy-start | bytes 271108
  541.2 137.9 %copy-start.72 = (f32[22592]{0:T(1024)S(1)}, f32[22592]{0:T(1024)}, u32[]{:S(2)}) copy-start(f32[22592]{0:T(1024)} %param.19) | copy-start | bytes 271108
  541.2 139.6 %copy-start.71 = (f32[22592]{0:T(1024)S(1)}, f32[22592]{0:T(1024)}, u32[]{:S(2)}) copy-start(f32[22592]{0:T(1024)} %param.20) | copy-start | bytes 271108
  541.2 140.2 %copy-start.62 = (f32[20624]{0:T(1024)S(1)}, f32[20624]{0:T(1024)}, u32[]{:S(2)}) copy-start(f32[20624]{0:T(1024)} %param.21) | copy-start | bytes 247492
  541.2 140.2 %copy-start.75 = (f32[20624]{0:T(1024)S(1)}, f32[20624]{0:T(1024)}, u32[]{:S(2)}) copy-start(f32[20624]{0:T(1024)} %param.22) | copy-start | bytes 247492
  541.2 141.9 %copy-start.76 = (f32[20624]{0:T(1024)S(1)}, f32[20624]{0:T(1024)}, u32[]{:S(2)}) copy-start(f32[20624]{0:T(1024)} %param.23) | copy-start | bytes 247492
  541.5 142.3 %copy-start.1 = (f32[8,128,256]{2,1,0:T(8,128)S(1)}, f32[8,128,256]{2,1,0:T(8,128)}, u32[]{:S(2)}) copy-start(f32[8,128,256]{2,1,0:T(8,128)} %param.13) | copy-start | bytes 3145732
  (119 other events, 476.1 us)
Sparse Core Ops, SparseCore 0:
  14.2 139.3 all-reduce.14
  217.4 34.1 all-gather.1
  387.3 71.2 reduce-scatter.1
  527.8 151.2 all-reduce.12
where the time goes:
time: 700 us; the launch traced here: 691 us
  waiting for transfers between devices  319 us (46%)
  matrix products  150 us (21%)
  local copies, waits for them, and re-layouts  96.6 us (14%)
  other arithmetic  64.5 us (9%)
  blocking collectives  28.8 us (4%)
  between operations  15.9 us (2%)
  starting transfers between devices  15.5 us (2%)
    unnamed x6, waiting for transfers between devices  252 us
    reduce_scatter x1, waiting for transfers between devices, per_device(): lax.psum_scatter(grad_kv, 'seq', scatter_dimension=1, tiled=True)  46.5 us
    dot_general x1, matrix products, per_device(): jnp.dot(ff_in, up_weight, preferred_element_type=jnp.float32)  40.5 us
    unnamed x300, local copies, waits for them, and re-layouts  26.9 us
    dot_general x1, matrix products, per_device(): jnp.einsum('uqhd,ukhd->uhqk', grad_vals, values, preferred_element_type=j...  21.6 us
    all_gather x1, waiting for transfers between devices, per_device(): kv_whole = lax.all_gather(qkv_all[:, :, inner:], 'seq', axis=1, tiled=True)  18.4 us
    psum x2, blocking collectives, norm_forward(): total, squares = lax.psum((total, squares), 'seq')  14.8 us
    gather x1, local copies, waits for them, and re-layouts, take_rows(): return phone_table[phone_rows]  14.1 us
  transfers between devices with their start and end apart: 12, of which 6 were waited for; matrix products, arithmetic and copies ran while one was open for 13% of the time, Pallas kernels for 0%

commit v1 on v0

--- a/solution.py
+++ b/solution.py
@@ -19,23 +19,6 @@
 AVERAGE_DECAY = 0.99
 LEARN_BASE = 0.015
 MASK_FILL = -1e30
-
-
-def extended(cells, sides, width):
-    for axis, dim in sides:
-        count = lax.axis_size(axis)
-        ends = count - 1
-        head = lax.slice_in_dim(cells, 0, width, axis=dim)
-        tail = lax.slice_in_dim(cells, cells.shape[dim] - width, cells.shape[dim], axis=dim)
-        cells = jnp.concatenate(
-            [
-                lax.ppermute(tail, axis, [(i, (i + 1) % count) for i in range(ends)]),
-                cells,
-                lax.ppermute(head, axis, [((i + 1) % count, i) for i in range(ends)]),
-            ],
-            axis=dim,
-        )
-    return cells
 
 
 def soft_plus(signal):
@@ -88,7 +71,7 @@
 
 
 def rim_pad(signal):
-    return extended(signal, (("seq", 1),), 1)
+    return jnp.pad(signal, ((0, 0), (1, 1), (0, 0)))
 
 
 def conv_apply(padded, weight):
@@ -116,7 +99,7 @@
 
 
 def conv_input_grad(grad_low, weight):
-    padded = extended(grad_low, (("seq", 1),), 1)
+    padded = rim_pad(grad_low)
     length_here = grad_low.shape[1]
     result = jnp.einsum("utd,cd->utc", padded[:, 2:], weight[0], preferred_element_type=jnp.float32)
     result = result + jnp.einsum(
@@ -133,7 +116,6 @@
     grouped = (signal * frame_mask[:, :, None]).reshape(shape_now[0], shape_now[1], GROUPS, width)
     total = jnp.sum(grouped, axis=(1, 3))
     squares = jnp.sum(grouped * grouped, axis=(1, 3))
-    total, squares = lax.psum((total, squares), "seq")
     number = valid_count[:, None] * width
     mean_now = total / number
     inv_std = lax.rsqrt(squares / number - mean_now * mean_now + EPSILON)
@@ -151,7 +133,6 @@
     second_sum = jnp.sum(
         (grad_norm * normed).reshape(shape_now[0], shape_now[1], GROUPS, width), axis=(1, 3)
     )
-    first_sum, second_sum = lax.psum((first_sum, second_sum), "seq")
     number = valid_count[:, None] * width
     first_wide = jnp.repeat(first_sum / number, width, axis=1)[:, None, :]
     second_wide = jnp.repeat(second_sum / number, width, axis=1)[:, None, :]
@@ -168,6 +149,40 @@
     master_new = master - rate * (grad + MOMENTUM * moment_new)
     average_new = AVERAGE_DECAY * average + (1.0 - AVERAGE_DECAY) * master_new
     return (master_new, moment_new, average_new, master_new.astype(jnp.bfloat16))
+
+
+def pad_width(length_now):
+    return -(-length_now // 1024) * 1024
+
+
+def gather_weights(res_master, tf_master):
+    res_len, tf_len = res_master.shape[0], tf_master.shape[0]
+    width = pad_width(res_len + tf_len)
+    flat = jnp.concatenate([res_master, tf_master]).astype(jnp.bfloat16)
+    flat = jnp.pad(flat, (0, width - res_len - tf_len))
+    whole = lax.all_gather(flat, ("dp", "seq"), axis=0, tiled=True).reshape(-1, width)
+    return (whole[:, :res_len].reshape(-1), whole[:, res_len : res_len + tf_len].reshape(-1))
+
+
+def scatter_grads(res_grad, tf_grad):
+    count = lax.axis_size("dp") * lax.axis_size("seq")
+    res_grad, tf_grad = res_grad.reshape(count, -1), tf_grad.reshape(count, -1)
+    res_len, tf_len = res_grad.shape[1], tf_grad.shape[1]
+    width = pad_width(res_len + tf_len)
+    rows = jnp.concatenate(
+        [res_grad, tf_grad, jnp.zeros((count, width - res_len - tf_len), jnp.float32)], axis=1
+    )
+    share = lax.psum_scatter(rows.reshape(-1), ("dp", "seq"), scatter_dimension=0, tiled=True)
+    return (share[:res_len], share[res_len : res_len + tf_len])
+
+
+def to_utts(cells):
+    return lax.all_to_all(cells, "seq", split_axis=0, concat_axis=1, tiled=True)
+
+
+def to_frames(cells):
+    low = cells.astype(jnp.bfloat16)
+    return lax.all_to_all(low, "seq", split_axis=1, concat_axis=0, tiled=True).astype(jnp.float32)
 
 
 def per_device(
@@ -184,23 +199,29 @@
     tf_moment,
     tf_average,
 ):
-    utt_count, local_len, _ = inputs.shape
-    key_total = local_len * lax.axis_size("seq")
+    utts_here, local_len, _ = inputs.shape
+    seq_size = lax.axis_size("seq")
+    key_total = local_len * seq_size
+    utt_count = utts_here // seq_size
     inner = HEADS * HD
     seq_index = lax.axis_index("seq")
     frame_ids = seq_index * local_len + jnp.arange(local_len, dtype=jnp.int32)
-    frame_mask = (frame_ids[None, :] < lengths[:, None]).astype(jnp.float32)
-    wide_mask = frame_mask[:, :, None]
-    key_mask = jnp.arange(key_total, dtype=jnp.int32)[None, :] < lengths[:, None]
-    valid_count = lengths.astype(jnp.float32)
+    local_mask = (frame_ids[None, :] < lengths[:, None]).astype(jnp.float32)[:, :, None]
     boundary = jnp.cumsum(durations, axis=1)
     phone = jnp.sum((boundary[:, None, :] <= frame_ids[None, :, None]).astype(jnp.int32), axis=2)
     phone = jnp.minimum(phone, durations.shape[1] - 1)
     start_state = inputs + jax.vmap(take_rows)(encoded, phone)
-    res_whole = lax.all_gather(res_master.astype(jnp.bfloat16), ("dp", "seq"), axis=0, tiled=True)
+    res_whole, tf_whole = gather_weights(res_master, tf_master)
+    masked_in = to_utts((start_state * local_mask).astype(jnp.bfloat16))
+    grad_ff = to_utts((cotangent * local_mask).astype(jnp.bfloat16))
+    lengths = lax.dynamic_slice_in_dim(lengths, seq_index * utt_count, utt_count)
+    time_embed = lax.dynamic_slice_in_dim(time_embed, seq_index * utt_count, utt_count)
+    frame_mask = (jnp.arange(key_total)[None, :] < lengths[:, None]).astype(jnp.float32)
+    wide_mask = frame_mask[:, :, None]
+    key_mask = jnp.arange(key_total, dtype=jnp.int32)[None, :] < lengths[:, None]
+    valid_count = lengths.astype(jnp.float32)
     conv_one, conv_two, res_weight, time_weight, res_rows = unpack_res(res_whole)
     res_small = res_rows.astype(jnp.float32)
-    masked_in = (start_state * wide_mask).astype(jnp.bfloat16)
     padded_one = rim_pad(masked_in)
     z_one = conv_apply(padded_one, conv_one) + res_small[0]
     norm_one, normed_one, inv_one = norm_forward(
@@ -218,14 +239,13 @@
     act_two = mish_fn(norm_two) * wide_mask
     skip_out = jnp.dot(masked_in, res_weight, preferred_element_type=jnp.float32) + res_small[6]
     block_out = act_two + skip_out
-    tf_whole = lax.all_gather(tf_master.astype(jnp.bfloat16), ("dp", "seq"), axis=0, tiled=True)
     qkv_weight, out_weight, up_weight, down_weight, tf_rows, wide_rows = unpack_tf(tf_whole)
     tf_small = tf_rows.astype(jnp.float32)
     wide_small = wide_rows.astype(jnp.float32)
     attn_in = layer_norm(block_out, tf_small[0], tf_small[1]).astype(jnp.bfloat16)
     qkv_all = jnp.dot(attn_in, qkv_weight, preferred_element_type=jnp.float32).astype(jnp.bfloat16)
-    queries = qkv_all[:, :, :inner].reshape(utt_count, local_len, HEADS, HD)
-    kv_whole = lax.all_gather(qkv_all[:, :, inner:], "seq", axis=1, tiled=True)
+    queries = qkv_all[:, :, :inner].reshape(utt_count, key_total, HEADS, HD)
+    kv_whole = qkv_all[:, :, inner:]
     keys = kv_whole[:, :, :inner].reshape(utt_count, key_total, HEADS, HD)
     values = kv_whole[:, :, inner:].reshape(utt_count, key_total, HEADS, HD)
     scores = (
@@ -239,7 +259,7 @@
     log_total = top_score + jnp.log(row_total)
     probs_low = (expo / row_total).astype(jnp.bfloat16)
     attn_vals = jnp.einsum("uhqk,ukhd->uqhd", probs_low, values, preferred_element_type=jnp.float32)
-    attn_vals = attn_vals.reshape(utt_count, local_len, inner).astype(jnp.bfloat16)
+    attn_vals = attn_vals.reshape(utt_count, key_total, inner).astype(jnp.bfloat16)
     attn_out = jnp.dot(attn_vals, out_weight, preferred_element_type=jnp.float32) + tf_small[2]
     mid_state = block_out + attn_out
     ff_in = layer_norm(mid_state, tf_small[3], tf_small[4]).astype(jnp.bfloat16)
@@ -247,10 +267,7 @@
     snake_out = snake_fn(up_out, wide_small[1], wide_small[2]).astype(jnp.bfloat16)
     ff_out = jnp.dot(snake_out, down_weight, preferred_element_type=jnp.float32) + tf_small[5]
     final = (mid_state + ff_out) * wide_mask
-    tf_back = lax.all_gather(tf_master.astype(jnp.bfloat16), ("dp", "seq"), axis=0, tiled=True)
-    qkv_weight, out_weight, up_weight, down_weight, tf_rows, wide_rows = unpack_tf(tf_back)
-    grad_final = cotangent * wide_mask
-    grad_ff = grad_final.astype(jnp.bfloat16)
+    grad_final = grad_ff.astype(jnp.float32)
     grad_down_w = jnp.einsum("utf,utc->fc", snake_out, grad_ff, preferred_element_type=jnp.float32)
     grad_down_b = jnp.sum(grad_ff, axis=(0, 1), dtype=jnp.float32)
     grad_snake = jnp.einsum("utc,fc->utf", grad_ff, down_weight, preferred_element_type=jnp.float32)
@@ -267,7 +284,7 @@
     grad_out_w = jnp.einsum("uti,utc->ic", attn_vals, grad_attn, preferred_element_type=jnp.float32)
     grad_out_b = jnp.sum(grad_attn, axis=(0, 1), dtype=jnp.float32)
     grad_vals = jnp.einsum("utc,ic->uti", grad_attn, out_weight, preferred_element_type=jnp.float32)
-    grad_vals = grad_vals.astype(jnp.bfloat16).reshape(utt_count, local_len, HEADS, HD)
+    grad_vals = grad_vals.astype(jnp.bfloat16).reshape(utt_count, key_total, HEADS, HD)
     scores = (
         jnp.einsum("uqhd,ukhd->uhqk", queries, keys, preferred_element_type=jnp.float32)
         * SCORE_SCALE
@@ -298,9 +315,9 @@
         ],
         axis=2,
     )
-    grad_kv_local = lax.psum_scatter(grad_kv, "seq", scatter_dimension=1, tiled=True)
+    grad_kv_local = grad_kv
     grad_qkv = jnp.concatenate(
-        [grad_query.reshape(utt_count, local_len, inner), grad_kv_local], axis=2
+        [grad_query.reshape(utt_count, key_total, inner), grad_kv_local], axis=2
     ).astype(jnp.bfloat16)
     grad_qkv_w = jnp.einsum("utc,utd->cd", attn_in, grad_qkv, preferred_element_type=jnp.float32)
     grad_attn_in = jnp.einsum(
@@ -321,9 +338,6 @@
             jnp.stack([grad_up_b, grad_alpha, grad_beta]).reshape(-1),
         ]
     )
-    tf_share = lax.psum_scatter(tf_grad_local, ("dp", "seq"), scatter_dimension=0, tiled=True)
-    res_back = lax.all_gather(res_master.astype(jnp.bfloat16), ("dp", "seq"), axis=0, tiled=True)
-    conv_one, conv_two, res_weight, time_weight, res_rows = unpack_res(res_back)
     grad_skip = grad_block.astype(jnp.bfloat16)
     grad_res_w = jnp.einsum("utc,utd->cd", masked_in, grad_skip, preferred_element_type=jnp.float32)
     grad_res_b = jnp.sum(grad_skip, axis=(0, 1), dtype=jnp.float32)
@@ -374,8 +388,8 @@
             ).reshape(-1),
         ]
     )
-    res_share = lax.psum_scatter(res_grad_local, ("dp", "seq"), scatter_dimension=0, tiled=True)
-    tokens_total = utt_count * key_total * lax.axis_size("dp")
+    res_share, tf_share = scatter_grads(res_grad_local, tf_grad_local)
+    tokens_total = utts_here * key_total * lax.axis_size("dp")
     rate = LEARN_BASE / math.sqrt(tokens_total)
     res_new, res_moment_new, res_average_new, res_low = update(
         res_master, res_moment, res_average, res_share, rate
@@ -384,8 +398,8 @@
         tf_master, tf_moment, tf_average, tf_share, rate
     )
     return (
-        final,
-        grad_inputs,
+        to_frames(final),
+        to_frames(grad_inputs),
         res_share,
         tf_share,
         res_new,

time: 700 us -> 515 us (0.74)
  waiting for transfers between devices: 319 us -> 147 us
  local copies, waits for them, and re-layouts: 96.6 us -> 123 us
  matrix products: 150 us -> 136 us
  other arithmetic: 64.5 us -> 55.4 us
  blocking collectives: 28.8 us -> 19.8 us
    unnamed x6 -> x3, waiting for transfers between devices: 252 us -> 99.8 us
    reduce_scatter x1 -> x0, waiting for transfers between devices: 46.5 us -> none  [per_device(): lax.psum_scatter(grad_kv, 'seq', scatter_dimension=1, tiled=True)]
    all_to_all x0 -> x3, waiting for transfers between devices: none -> 46 us  [the longest x2 27 us: to_frames(): lax.all_to_all(low, 'seq', split_axis=1, concat_axis=0, tiled=True)]
    psum x4 -> x0, blocking collectives: 28.8 us -> none  [the longest x2 14.8 us: norm_forward(): total, squares = lax.psum((total, squares), 'seq')]
    unnamed x300 -> x114, local copies, waits for them, and re-layouts: 26.9 us -> 49.1 us
    all_to_all x0 -> x1, blocking collectives: none -> 19.8 us  [to_utts(): return lax.all_to_all(cells, 'seq', split_axis=0, concat_axis=1, tiled=True)]
    all_gather x1, waiting for transfers between devices: 18.4 us -> 1.15 us  [gather_weights(): lax.all_gather(flat, ('dp', 'seq'), axis=0, tiled=True).reshape(-1, width)]
    reshape x1 -> x5, local copies, waits for them, and re-layouts: 2.33 us -> 19.4 us  [the longest x1 4.82 us: scatter_grads(): tf_grad.reshape(count, -1)]
  transfers between devices with their start and end apart: 12 -> 5, of which waited for: 6 -> 5; matrix products, arithmetic and copies ran while one was open for 13% -> 8% of each run, Pallas kernels for 0% -> 0%
where the time goes in v1:
time: 515 us; the launch traced here: 507 us
  waiting for transfers between devices  147 us (29%)
  matrix products  136 us (26%)
  local copies, waits for them, and re-layouts  123 us (24%)
  other arithmetic  55.4 us (11%)
  blocking collectives  19.8 us (4%)
  between operations  15.1 us (3%)
  starting transfers between devices  10.6 us (2%)
    unnamed x3, waiting for transfers between devices  99.8 us
    unnamed x114, local copies, waits for them, and re-layouts  49.1 us
    dot_general x1, matrix products, per_device(): jnp.dot(ff_in, up_weight, preferred_element_type=jnp.float32)  36.9 us
    all_to_all x2, waiting for transfers between devices, to_frames(): lax.all_to_all(low, 'seq', split_axis=1, concat_axis=0, tiled=True)  27 us
    all_to_all x1, blocking collectives, to_utts(): return lax.all_to_all(cells, 'seq', split_axis=0, concat_axis=1, tiled=True)  19.8 us
    all_to_all x1, waiting for transfers between devices, to_utts(): return lax.all_to_all(cells, 'seq', split_axis=0, concat_axis=1, tiled=True)  19 us
    gather x1, local copies, waits for them, and re-layouts, take_rows(): return phone_table[phone_rows]  14.1 us
  transfers between devices with their start and end apart: 5, of which 5 were waited for; matrix products, arithmetic and copies ran while one was open for 8% of the time, Pallas kernels for 0%

profile of v1, /device:TPU:0, one launch (start us, length us, event | category | flops | bytes accessed | tf_op | source)
XLA Modules:
  0.0 506.8 jit_solution(15145667915792458925)
XLA Ops:
  11.3 14.1 %gather_fusion = f32[2048,256]{1,0:T(8,128)S(1)} fusion(f32[8,128,256]{2,1,0:T(8,128)S(1)} %copy-done, s32[2048]{0:T(1024)S(1)} %bitcast.212), kind=kCustom, calls=%fused_computation | custom fusion | bytes 4210688 | tf_op jit(solution)/shard_map/vmap()/gather | solution.py:70
  25.5 3.7 multiply_convert_fusion.4
  29.2 19.8 %all_to_all.54 = bf16[8,256,256]{2,1,0:T(8,128)(2,1)S(1)} all-to-all(bf16[8,256,256]{2,1,0:T(8,128)(2,1)S(1)} %get-tuple-element.80), channel_id=1, replica_groups=mesh['dp'=8,'seq'=4] {'seq'}, dimensions={0} | all-to-all | bytes 2097152 | tf_op jit(solution)/shard_map/all_to_all | solution.py:180
  48.9 3.5 all-to-all-start
  52.8 19.0 %all-to-all-done = bf16[8,256,256]{2,1,0:T(8,128)(2,1)S(1)} async-done(((bf16[8,256,256]{2,1,0:T(8,128)(2,1)}), bf16[8,256,256]{2,1,0:T(8,128)(2,1)S(1)}, u32[]{:S(2)}, u32[]{:S(2)}) %all-to-all-start) | async-done | bytes 1048608 | tf_op jit(solution)/shard_map/all_to_all | solution.py:180
  76.1 4.6 reshape.420
  86.0 4.4 reshape.421
  98.0 3.7 reshape.480
  101.7 3.5 slice.201
  125.8 4.4 multiply_reduce_fusion.13
  130.9 3.6 fusion.78
  142.8 3.9 fusion
  146.8 5.1 %fusion.13 = bf16[2,2,64,1024]{3,2,1,0:T(8,128)(2,1)} fusion(bf16[2,1024,2,64]{1,3,2,0:T(8,128)(2,1)S(1)} %bitcast.244, f32[2,2,1024]{2,1,0:T(2,128)S(1)} %fusion, f32[2,2,1024]{2,1,0:T(2,128)S(1)} %get-tuple-element.106, f32[2,2,1024,1024]{2,3,1,0:T(8,128)S(1)} %get-tuple-element.107, pred[2,1024]{1,0:T(4,128)(4,1)S(1)} %get-tuple-element.100), kind=kOutput, calls=%fused_computation.83 | convolution fusion | flops 558104576 | bytes 17860608 | tf_op jit(solution)/shard_map/uhqk,ukhd->uqhd/dot_general | solution.py:261
  155.0 36.9 %multiply_reduce_fusion.2 = (f32[1024]{0:T(1024)S(1)}, f32[1024]{0:T(1024)S(1)}, f32[1024]{0:T(1024)S(1)}, bf16[2,1024,1024]{2,1,0:T(8,128)(2,1)S(1)}, bf16[2,1024,1024]{2,1,0:T(8,128)(2,1)}) fusion(f32[1024]{0:T(1024)S(1)} %get-tuple-element.79, f32[1024]{0:T(1024)S(1)} %get-tuple-element.78, f32[2,1024,1024]{2,1,0:T(8,128)S(1)} %fusion.28, ...), kind=kOutput, calls=%fused_computation.11 | convolution fusion | flops 1118303232 | bytes 19445760 | tf_op jit(solution)/shard_map/dot_general | solution.py:266
  201.9 5.2 %fusion.8 = bf16[2,2,64,1024]{3,2,1,0:T(8,128)(2,1)} fusion(bf16[2,1024,2,64]{1,3,2,0:T(8,128)(2,1)S(1)} %bitcast.242, f32[2,2,1024]{2,1,0:T(2,128)S(1)} %log_add_fusion, f32[2,2,1024,1024]{2,3,1,0:T(8,128)S(1)} %get-tuple-element.107, pred[2,1024]{1,0:T(4,128)(4,1)S(1)} %get-tuple-element.100), kind=kOutput, calls=%fused_computation.79 | convolution fusion | flops 553910272 | bytes 17844224 | tf_op jit(solution)/shard_map/uhqk,uqhd->ukhd/dot_general | solution.py:308
  207.1 8.2 %multiply_reduce_fusion = (f32[2,2,1024]{2,1,0:T(2,128)S(1)}, f32[2,2,1024,1024]{2,3,1,0:T(8,128)}) fusion(f32[2,2,1024]{2,1,0:T(2,128)S(1)} %log_add_fusion, f32[2,2,1024,1024]{2,3,1,0:T(8,128)S(1)} %get-tuple-element.107, pred[2,1024]{1,0:T(4,128)(4,1)S(1)} %get-tuple-element.100, bf16[2,1024,2,64]{1,3,2,0:T(8,128)(2,1)S(1)} %bitcast.243, ...), kind=kOutput, calls=%fused_computation.2 | convolution fusion | flops 557838336 | bytes 34637824 | tf_op jit(solution)/shard_map/uqhd,ukhd->uhqk/dot_general | solution.py:295
  215.3 8.7 %multiply_convert_fusion = bf16[2,2,1024,1024]{2,3,1,0:T(8,128)(2,1)S(1)} fusion(f32[2,2,1024,1024]{2,3,1,0:T(8,128)} %get-tuple-element.112, f32[2,2,1024]{2,1,0:T(2,128)S(1)} %get-tuple-element.111, f32[2,2,1024]{2,1,0:T(2,128)S(1)} %log_add_fusion, f32[2,2,1024,1024]{2,3,1,0:T(8,128)S(1)} %get-tuple-element.107, pred[2,1024]{1,0:T(4,128)(4,1)S(1)} %get-tuple-element.100), kind=kLoop, calls=%fused_computation.1 | loop fusion | flops 25165824 | bytes 41977856 | tf_op jit(solution)/shard_map/convert_element_type | solution.py:299
  236.2 3.7 convolution_bitcast_fusion.3
  248.1 4.9 multiply_reduce_fusion.5
  263.3 7.0 %fusion.70 = (f32[256]{0:T(256)}, f32[2,256]{1,0:T(2,128)}, f32[256]{0:T(256)}, f32[2,256]{1,0:T(2,128)S(1)}, f32[2,256]{1,0:T(2,128)S(1)}, /*index=5*/f32[256]{0:T(256)}, f32[2,1024,256]{2,1,0:T(8,128)}) fusion(f32[256]{0:T(256)S(1)} %bitcast.279, f32[256]{0:T(256)S(1)} %bitcast.269, f32[2,256]{1,0:T(2,128)S(1)} %mul.522, ...), kind=kOutput, calls=%fused_computation.217 | convolution fusion | flops 290977536 | bytes 9591808 | tf_op jit(solution)/shard_map/utd,cd->utc/dot_general | solution.py:108
  271.0 3.5 convert_reduce_fusion.5
  299.9 3.6 reshape.436
  310.7 4.8 reshape.443
  315.5 8.7 %dynamic-update-slice = f32[32,44032]{1,0:T(8,128)} dynamic-update-slice(f32[32,44032]{1,0:T(8,128)} %custom-call.2, f32[32,22592]{1,0:T(8,128)} %reshape.436, s32[]{} %constant.101, s32[]{} %constant.101) | dynamic-update-slice | bytes 5783556
  324.1 9.2 %dynamic-update-slice.1 = f32[32,44032]{1,0:T(8,128)} dynamic-update-slice(f32[32,44032]{1,0:T(8,128)} %dynamic-update-slice, f32[32,20624]{1,0:T(8,128)} %reshape.443, s32[]{} %constant.101, s32[]{} %constant.102) | dynamic-update-slice | bytes 5279748
  335.3 6.0 %copy.146 = f32[4,344,8,128]{3,1,2,0:T(8,128)} copy(f32[4,344,8,128]{3,2,1,0:T(8,128)} %bitcast.227) | data formatting | bytes 11272192
  342.0 4.3 multiply_convert_fusion.5
  348.4 3.5 all-to-all-start.1
  360.0 11.0 %all-to-all-done.1 = bf16[2,1024,256]{2,0,1:T(2,128)(2,1)S(1)} async-done(((bf16[2,1024,256]{2,0,1:T(2,128)(2,1)}), bf16[2,1024,256]{2,0,1:T(2,128)(2,1)S(1)}, u32[]{:S(2)}, u32[]{:S(2)}) %all-to-all-start.1) | async-done | bytes 1048608 | tf_op jit(solution)/shard_map/all_to_all | solution.py:185
  371.1 3.5 all-to-all-start.3
  376.8 16.0 %all-to-all-done.3 = bf16[2,1024,256]{2,0,1:T(2,128)(2,1)S(1)} async-done(((bf16[2,1024,256]{2,0,1:T(2,128)(2,1)}), bf16[2,1024,256]{2,0,1:T(2,128)(2,1)S(1)}, u32[]{:S(2)}, u32[]{:S(2)}) %all-to-all-start.3) | async-done | bytes 1048608 | tf_op jit(solution)/shard_map/all_to_all | solution.py:185
  395.2 99.8 %all-reduce.8.cloned.1.call-done = f32[1409024]{0:T(1024)} async-done(((f32[1409024]{0:T(1024)}), f32[1409024]{0:T(1024)}) %all-reduce.8.cloned.1.call-update) | async-done | bytes 5636112
  (255 shorter events, 149.7 us)
Async XLA Ops:
  7.2 4.1 copy-start
  7.2 68.9 %all-gather.2.cloned.1.call-start = ((), (), s32[]{:S(2)}) async-start(), calls=%async_computation.4 | async-start | bytes 2906112 | tf_op jit(solution)/shard_map/all_gather | solution.py:163
  11.3 14.1 %copy-start.44 = (s32[8]{0:T(128)S(1)}, s32[8]{0:T(128)}, u32[]{:S(2)}) copy-start(s32[8]{0:T(128)} %param.15) | copy-start | bytes 100
  48.9 22.8 %all-to-all-start = ((bf16[8,256,256]{2,1,0:T(8,128)(2,1)}), bf16[8,256,256]{2,1,0:T(8,128)(2,1)S(1)}, u32[]{:S(2)}, u32[]{:S(2)}) async-start(bf16[8,256,256]{2,1,0:T(8,128)(2,1)} %get-tuple-element.81), calls=%async_computation | async-start | bytes 2097152 | tf_op jit(solution)/shard_map/all_to_all | solution.py:180
  52.5 442.5 %all-reduce.8.cloned.1.call-start = ((), (), s32[]{:S(2)}) async-start(), calls=%async_computation.5 | async-start | bytes 11272192
  52.8 146.2 %copy-start.13 = (bf16[4,2,256,256]{3,2,0,1:T(8,128)(2,1)}, bf16[4,2,256,256]{3,2,0,1:T(8,128)(2,1)S(1)}, u32[]{:S(2)}) copy-start(bf16[4,2,256,256]{3,2,0,1:T(8,128)(2,1)S(1)} %copy.101) | copy-start | bytes 3145732
  116.9 8.9 %copy-start.4 = (bf16[2,1024,256]{2,1,0:T(8,128)(2,1)}, bf16[2,1024,256]{2,1,0:T(8,128)(2,1)S(1)}, u32[]{:S(2)}) copy-start(bf16[2,1024,256]{2,1,0:T(8,128)(2,1)S(1)} %multiply_convert_fusion.6) | copy-start | bytes 3145732
  134.5 17.4 %copy-start.2 = (f32[2,1024,256]{2,1,0:T(8,128)}, f32[2,1024,256]{2,1,0:T(8,128)S(1)}, u32[]{:S(2)}) copy-start(f32[2,1024,256]{2,1,0:T(8,128)S(1)} %get-tuple-element.105) | copy-start | bytes 6291460
  136.8 9.9 %copy-start.24 = (bf16[2,1024,128]{1,2,0:T(8,128)(2,1)}, bf16[2,1024,128]{1,2,0:T(8,128)(2,1)S(1)}, u32[]{:S(2)}) copy-start(bf16[2,1024,128]{1,2,0:T(8,128)(2,1)S(1)} %get-tuple-element.73) | copy-start | bytes 1572868
  153.6 43.7 %copy-start.6 = (f32[2,1024,256]{2,1,0:T(8,128)}, f32[2,1024,256]{2,1,0:T(8,128)S(1)}, u32[]{:S(2)}) copy-start(f32[2,1024,256]{2,1,0:T(8,128)S(1)} %get-tuple-element.109) | copy-start | bytes 6291460
  201.9 5.2 %copy-start.25 = (bf16[2,1024,128]{1,2,0:T(8,128)(2,1)S(1)}, bf16[2,1024,128]{1,2,0:T(8,128)(2,1)}, u32[]{:S(2)}) copy-start(bf16[2,1024,128]{1,2,0:T(8,128)(2,1)} %copy-done.24) | copy-start | bytes 1572868
  215.3 8.7 %copy-start.19 = (bf16[2,1024,128]{1,2,0:T(8,128)(2,1)S(1)}, bf16[2,1024,128]{1,2,0:T(8,128)(2,1)}, u32[]{:S(2)}) copy-start(bf16[2,1024,128]{1,2,0:T(8,128)(2,1)} %copy-done.18) | copy-start | bytes 1572868
  224.1 3.5 copy-start.17
  229.9 6.3 %copy-start.3 = (f32[2,1024,256]{2,1,0:T(8,128)S(1)}, f32[2,1024,256]{2,1,0:T(8,128)}, u32[]{:S(2)}) copy-start(f32[2,1024,256]{2,1,0:T(8,128)} %copy-done.2) | copy-start | bytes 6291460
  236.2 3.8 copy-start.30
  236.2 3.8 copy-start.31
  236.2 3.8 copy-start.32
  236.2 3.8 copy-start.37
  245.7 7.4 %copy-start.7 = (f32[2,1024,256]{2,1,0:T(8,128)}, f32[2,1024,256]{2,1,0:T(8,128)S(1)}, u32[]{:S(2)}) copy-start(f32[2,1024,256]{2,1,0:T(8,128)S(1)} %get-tuple-element.48) | copy-start | bytes 6291460
  285.3 6.8 %copy-start.27 = (f32[1,256,256]{2,1,0:T(8,128)S(1)}, f32[1,256,256]{2,1,0:T(8,128)}, u32[]{:S(2)}) copy-start(f32[1,256,256]{2,1,0:T(8,128)} %convolution_bitcast_fusion.8) | copy-start | bytes 786436
  299.9 6.0 %copy-start.21 = (f32[32,8,8,128]{3,1,2,0:T(8,128)S(1)}, f32[32,8,8,128]{3,1,2,0:T(8,128)}, u32[]{:S(2)}) copy-start(f32[32,8,8,128]{3,1,2,0:T(8,128)} %copy.144) | copy-start | bytes 3145732
  305.9 3.4 copy-start.42
  348.4 22.7 %all-to-all-start.1 = ((bf16[2,1024,256]{2,0,1:T(2,128)(2,1)}), bf16[2,1024,256]{2,0,1:T(2,128)(2,1)S(1)}, u32[]{:S(2)}, u32[]{:S(2)}) async-start(bf16[2,1024,256]{2,0,1:T(2,128)(2,1)} %copy.99), calls=%async_computation.1 | async-start | bytes 2097152 | tf_op jit(solution)/shard_map/all_to_all | solution.py:185
  371.1 21.8 %all-to-all-start.3 = ((bf16[2,1024,256]{2,0,1:T(2,128)(2,1)}), bf16[2,1024,256]{2,0,1:T(2,128)(2,1)S(1)}, u32[]{:S(2)}, u32[]{:S(2)}) async-start(bf16[2,1024,256]{2,0,1:T(2,128)(2,1)} %copy.108), calls=%async_computation.3 | async-start | bytes 2097152 | tf_op jit(solution)/shard_map/all_to_all | solution.py:185
  392.8 106.8 %copy-start.1 = (f32[8,128,256]{2,1,0:T(8,128)S(1)}, f32[8,128,256]{2,1,0:T(8,128)}, u32[]{:S(2)}) copy-start(f32[8,128,256]{2,1,0:T(8,128)} %param.13) | copy-start | bytes 3145732
  393.6 101.4 %copy-start.35 = (f32[20624]{0:T(1024)S(1)}, f32[20624]{0:T(1024)}, u32[]{:S(2)}) copy-start(f32[20624]{0:T(1024)} %param.21) | copy-start | bytes 247492
  393.6 101.4 %copy-start.40 = (f32[20624]{0:T(1024)S(1)}, f32[20624]{0:T(1024)}, u32[]{:S(2)}) copy-start(f32[20624]{0:T(1024)} %param.22) | copy-start | bytes 247492
  393.6 103.0 %copy-start.41 = (f32[20624]{0:T(1024)S(1)}, f32[20624]{0:T(1024)}, u32[]{:S(2)}) copy-start(f32[20624]{0:T(1024)} %param.23) | copy-start | bytes 247492
  393.6 103.7 %copy-start.33 = (f32[22592]{0:T(1024)S(1)}, f32[22592]{0:T(1024)}, u32[]{:S(2)}) copy-start(f32[22592]{0:T(1024)} %param.18) | copy-start | bytes 271108
  393.6 103.7 %copy-start.39 = (f32[22592]{0:T(1024)S(1)}, f32[22592]{0:T(1024)}, u32[]{:S(2)}) copy-start(f32[22592]{0:T(1024)} %param.19) | copy-start | bytes 271108
  393.6 105.4 %copy-start.38 = (f32[22592]{0:T(1024)S(1)}, f32[22592]{0:T(1024)}, u32[]{:S(2)}) copy-start(f32[22592]{0:T(1024)} %param.20) | copy-start | bytes 271108
  496.6 3.0 copy-start.36
  (19 other events, 36.4 us)
Sparse Core Ops, SparseCore 0:
  11.4 64.5 all-gather.1
  341.5 153.4 all-reduce.7

commit v2 on v1

--- a/solution.py
+++ b/solution.py
@@ -1,8 +1,11 @@
+import functools
 import math
 
 import jax
 import jax.numpy as jnp
 from jax import lax
+from jax.experimental import pallas as pl
+from jax.experimental.pallas import tpu as pltpu
 from jax.sharding import PartitionSpec as P
 
 C = 256
@@ -37,33 +40,6 @@
     center = signal - jnp.mean(signal, axis=-1, keepdims=True)
     spread = jnp.mean(center * center, axis=-1, keepdims=True)
     return center * lax.rsqrt(spread + EPSILON) * gain_row + shift_row
-
-
-def unpack_res(flat):
-    square = C * C
-    conv_one = flat[0 : 3 * square].reshape(3, C, C)
-    conv_two = flat[3 * square : 6 * square].reshape(3, C, C)
-    res_weight = flat[6 * square : 7 * square].reshape(C, C)
-    time_weight = flat[7 * square : 7 * square + TE * C].reshape(TE, C)
-    offset = 7 * square + TE * C
-    small_rows = flat[offset : offset + 8 * C].reshape(8, C)
-    return (conv_one, conv_two, res_weight, time_weight, small_rows)
-
-
-def unpack_tf(flat):
-    inner = HEADS * HD
-    qkv_weight = flat[0 : 3 * C * inner].reshape(C, 3 * inner)
-    offset = 3 * C * inner
-    out_weight = flat[offset : offset + inner * C].reshape(inner, C)
-    offset = offset + inner * C
-    up_weight = flat[offset : offset + C * F].reshape(C, F)
-    offset = offset + C * F
-    down_weight = flat[offset : offset + F * C].reshape(F, C)
-    offset = offset + F * C
-    small_rows = flat[offset : offset + 6 * C].reshape(6, C)
-    offset = offset + 6 * C
-    wide_rows = flat[offset : offset + 3 * F].reshape(3, F)
-    return (qkv_weight, out_weight, up_weight, down_weight, small_rows, wide_rows)
 
 
 def take_rows(phone_table, phone_rows):
@@ -151,29 +127,314 @@
     return (master_new, moment_new, average_new, master_new.astype(jnp.bfloat16))
 
 
-def pad_width(length_now):
-    return -(-length_now // 1024) * 1024
-
-
-def gather_weights(res_master, tf_master):
-    res_len, tf_len = res_master.shape[0], tf_master.shape[0]
-    width = pad_width(res_len + tf_len)
-    flat = jnp.concatenate([res_master, tf_master]).astype(jnp.bfloat16)
-    flat = jnp.pad(flat, (0, width - res_len - tf_len))
-    whole = lax.all_gather(flat, ("dp", "seq"), axis=0, tiled=True).reshape(-1, width)
-    return (whole[:, :res_len].reshape(-1), whole[:, res_len : res_len + tf_len].reshape(-1))
-
-
-def scatter_grads(res_grad, tf_grad):
-    count = lax.axis_size("dp") * lax.axis_size("seq")
-    res_grad, tf_grad = res_grad.reshape(count, -1), tf_grad.reshape(count, -1)
-    res_len, tf_len = res_grad.shape[1], tf_grad.shape[1]
-    width = pad_width(res_len + tf_len)
-    rows = jnp.concatenate(
-        [res_grad, tf_grad, jnp.zeros((count, width - res_len - tf_len), jnp.float32)], axis=1
-    )
-    share = lax.psum_scatter(rows.reshape(-1), ("dp", "seq"), scatter_dimension=0, tiled=True)
-    return (share[:res_len], share[res_len : res_len + tf_len])
+def axis_bits(mesh_sizes):
+    bits = []
+    for name, size in mesh_sizes:
+        weight = size // 2
+        while weight >= 1:
+            bits.append((name, weight))
+            weight //= 2
+    return bits
+
+
+def part_orders(mesh_sizes):
+    first = axis_bits(mesh_sizes)
+    second = list(first)
+    if len(second) >= 3:
+        second[-3], second[-2] = second[-2], second[-3]
+    return (first, second)
+
+
+def owner_place(order, mesh_sizes, owner):
+    strides, stride = {}, 1
+    for name, size in reversed(mesh_sizes):
+        strides[name] = (stride, size)
+        stride *= size
+    place = 0
+    for step, (name, weight) in enumerate(order):
+        base, size = strides[name]
+        place += ((owner // base) % size // weight % 2) << step
+    return place
+
+
+def window_rows(length_now, count):
+    most = max((i * length_now) % 128 + length_now for i in range(count))
+    return -(-most // (128 * 16)) * 16
+
+
+def bit_of(name, weight):
+    return (lax.axis_index(name) // weight) % 2
+
+
+def partner_of(name, weight):
+    return {name: lax.axis_index(name) + (1 - 2 * bit_of(name, weight)) * weight}
+
+
+def greet(orders):
+    barrier = pltpu.get_barrier_semaphore()
+    for name, weight in orders[0]:
+        pl.semaphore_signal(
+            barrier,
+            inc=1,
+            device_id=partner_of(name, weight),
+            device_id_type=pl.DeviceIdType.MESH,
+        )
+    pl.semaphore_wait(barrier, len(orders[0]))
+
+
+def gather_kernel(orders, in_a, in_b, out_a, out_b, local_sem, send_sem, recv_sem):
+    ins, outs = (in_a, in_b), (out_a, out_b)
+    stage_count = len(orders[0])
+    offsets = []
+    for part in range(2):
+        offset = 0
+        for step, (name, weight) in enumerate(orders[part]):
+            offset = offset + bit_of(name, weight) * (1 << step)
+        offsets.append(offset)
+    locals_now = [
+        pltpu.make_async_copy(ins[part], outs[part].at[offsets[part]], local_sem.at[part])
+        for part in range(2)
+    ]
+    for copy in locals_now:
+        copy.start()
+    greet(orders)
+    for copy in locals_now:
+        copy.wait()
+    copies = []
+    for step in range(stage_count):
+        held = 1 << step
+        for part in range(2):
+            name, weight = orders[part][step]
+            start = offsets[part]
+            block = outs[part].at[pl.ds(start, held)]
+            copy = pltpu.make_async_remote_copy(
+                src_ref=block,
+                dst_ref=block,
+                send_sem=send_sem.at[part, step],
+                recv_sem=recv_sem.at[part, step],
+                device_id=partner_of(name, weight),
+                device_id_type=pl.DeviceIdType.MESH,
+            )
+            copy.start()
+            copies.append(copy)
+        for part in range(2):
+            copies[2 * step + part].wait_recv()
+            name, weight = orders[part][step]
+            offsets[part] = offsets[part] - bit_of(name, weight) * held
+    for copy in copies:
+        copy.wait_send()
+
+
+def gather_windows(orders, win_a, win_b):
+    count = 1 << len(orders[0])
+    stages = len(orders[0])
+    return pl.pallas_call(
+        functools.partial(gather_kernel, orders),
+        out_shape=(
+            jax.ShapeDtypeStruct((count,) + win_a.shape, win_a.dtype),
+            jax.ShapeDtypeStruct((count,) + win_b.shape, win_b.dtype),
+        ),
+        in_specs=[pl.BlockSpec(memory_space=pltpu.VMEM)] * 2,
+        out_specs=[pl.BlockSpec(memory_space=pltpu.VMEM)] * 2,
+        scratch_shapes=[
+            pltpu.SemaphoreType.DMA((2,)),
+            pltpu.SemaphoreType.DMA((2, stages)),
+            pltpu.SemaphoreType.DMA((2, stages)),
+        ],
+        compiler_params=pltpu.CompilerParams(
+            collective_id=0, has_side_effects=True, vmem_limit_bytes=32 * 1024 * 1024
+        ),
+    )(win_a, win_b)
+
+
+def reduce_kernel(orders, in_a, in_b, out_a, out_b, land_a, land_b, send_sem, recv_sem):
+    ins, outs, lands = (in_a, in_b), (out_a, out_b), (land_a, land_b)
+    stage_count = len(orders[0])
+    greet(orders)
+    copies = []
+
+    def source(part, step, keep):
+        name, weight = orders[part][stage_count - 1 - step]
+        held = 1 << (stage_count - 1 - step)
+        side = bit_of(name, weight)
+        side = side if keep else 1 - side
+        if step == 0:
+            return ins[part].at[pl.ds(side * held, held)]
+        base = (1 << stage_count) - (1 << (stage_count - step + 1))
+        return lands[part].at[pl.ds(base + side * held, held)]
+
+    for step in range(stage_count):
+        held = 1 << (stage_count - 1 - step)
+        base = (1 << stage_count) - (1 << (stage_count - step))
+        for part in range(2):
+            name, weight = orders[part][stage_count - 1 - step]
+            copy = pltpu.make_async_remote_copy(
+                src_ref=source(part, step, False),
+                dst_ref=lands[part].at[pl.ds(base, held)],
+                send_sem=send_sem.at[part, step],
+                recv_sem=recv_sem.at[part, step],
+                device_id=partner_of(name, weight),
+                device_id_type=pl.DeviceIdType.MESH,
+            )
+            copy.start()
+            copies.append(copy)
+        for part in range(2):
+            copies[2 * step + part].wait_recv()
+            mine = source(part, step, True)
+            if step == stage_count - 1:
+                outs[part][...] = mine[0].astype(jnp.float32) + lands[part][base].astype(
+                    jnp.float32
+                )
+            else:
+
+                def add_one(index, carry, mine=mine, part=part, base=base):
+                    land = lands[part].at[base + index]
+                    total = mine[index].astype(jnp.float32) + land[...].astype(jnp.float32)
+                    land[...] = total.astype(land.dtype)
+                    return carry
+
+                lax.fori_loop(0, held, add_one, 0)
+    for copy in copies:
+        copy.wait_send()
+
+
+def reduce_windows(orders, rows_a, rows_b):
+    count = 1 << len(orders[0])
+    stages = len(orders[0])
+    return pl.pallas_call(
+        functools.partial(reduce_kernel, orders),
+        out_shape=(
+            jax.ShapeDtypeStruct(rows_a.shape[1:], jnp.float32),
+            jax.ShapeDtypeStruct(rows_b.shape[1:], jnp.float32),
+        ),
+        in_specs=[pl.BlockSpec(memory_space=pltpu.VMEM)] * 2,
+        out_specs=[pl.BlockSpec(memory_space=pltpu.VMEM)] * 2,
+        scratch_shapes=[
+            pltpu.VMEM((count - 1,) + rows_a.shape[1:], rows_a.dtype),
+            pltpu.VMEM((count - 1,) + rows_b.shape[1:], rows_b.dtype),
+            pltpu.SemaphoreType.DMA((2, stages)),
+            pltpu.SemaphoreType.DMA((2, stages)),
+        ],
+        compiler_params=pltpu.CompilerParams(
+            collective_id=1, has_side_effects=True, vmem_limit_bytes=32 * 1024 * 1024
+        ),
+    )(rows_a, rows_b)
+
+
+RES_SQUARES = 7 * C * C
+RES_ROWS = (RES_SQUARES + TE * C + 8 * C) // 128
+INNER = HEADS * HD
+TF_SIZES = (3 * C * INNER, INNER * C, C * F, F * C, 6 * C, 3 * F)
+TF_ROWS = sum(TF_SIZES) // 128
+
+
+def place_maps(orders, mesh_sizes):
+    count = 1 << len(orders[0])
+    return [[owner_place(orders[part], mesh_sizes, i) for i in range(count)] for part in range(2)]
+
+
+def matrix_views():
+    views = []
+    row = 0
+    for rows, width in ((6 * C, C), (C, C), (TE, C), (8, C)):
+        views.append((0, row, rows, width))
+        row += rows * width // 128
+    row = 0
+    for rows, width in ((C, 3 * INNER), (INNER, C), (C, F), (F, C), (6, C), (3, F)):
+        views.append((1, row, rows, width))
+        row += rows * width // 128
+    return views
+
+
+def assemble_kernel(places, lengths_now, in_a, in_b, *refs):
+    outs, flats = refs[:10], refs[10:12]
+    count = len(places[0])
+    for part, ref in enumerate((in_a, in_b)):
+        flat = flats[part]
+        for i in range(count):
+            start, lead = divmod(i * lengths_now[part], 128)
+            rows = -(-(lead + lengths_now[part]) // 128)
+            if lead:
+                edge = flat[start : start + 1, :]
+            flat[start : start + rows, :] = ref[places[part][i]].astype(jnp.float32)[:rows]
+            if lead:
+                flat[start : start + 1, :] = flat[start : start + 1, :] + edge
+    for out, (part, row, rows, width) in zip(outs, matrix_views()):
+        stride = width // 128
+        for lane in range(stride):
+            piece = flats[part][pl.ds(row + lane, rows, stride=stride), :]
+            out[:, lane * 128 : (lane + 1) * 128] = piece.astype(out.dtype)
+
+
+def assemble_weights(places, lengths_now, win_a, win_b):
+    shapes = []
+    for index, (part, row, rows, width) in enumerate(matrix_views()):
+        kind = jnp.float32 if index in (3, 8, 9) else jnp.bfloat16
+        shapes.append(jax.ShapeDtypeStruct((rows, width), kind))
+    return pl.pallas_call(
+        functools.partial(assemble_kernel, places, lengths_now),
+        out_shape=shapes,
+        in_specs=[pl.BlockSpec(memory_space=pltpu.VMEM)] * 2,
+        out_specs=[pl.BlockSpec(memory_space=pltpu.VMEM)] * 10,
+        scratch_shapes=[
+            pltpu.VMEM((RES_ROWS + 8, 128), jnp.float32),
+            pltpu.VMEM((TF_ROWS + 12, 128), jnp.float32),
+        ],
+        compiler_params=pltpu.CompilerParams(vmem_limit_bytes=32 * 1024 * 1024),
+    )(win_a, win_b)
+
+
+def cut_kernel(places, lengths_now, *refs):
+    ins, outs, flats = refs[:10], refs[10:12], refs[12:14]
+    count = len(places[0])
+    for ref, (part, row, rows, width) in zip(ins, matrix_views()):
+        stride = width // 128
+        for lane in range(stride):
+            flats[part][pl.ds(row + lane, rows, stride=stride), :] = ref[
+                :, lane * 128 : (lane + 1) * 128
+            ]
+    for part in range(2):
+        for i in range(count):
+            start, lead = divmod(i * lengths_now[part], 128)
+            rows = outs[part].shape[1]
+            outs[part][places[part][i]] = flats[part][start : start + rows, :].astype(
+                outs[part].dtype
+            )
+
+
+def cut_grads(places, lengths_now, window_sizes, grads):
+    count = len(places[0])
+    return pl.pallas_call(
+        functools.partial(cut_kernel, places, lengths_now),
+        out_shape=[
+            jax.ShapeDtypeStruct((count, rows, 128), jnp.bfloat16) for rows in window_sizes
+        ],
+        in_specs=[pl.BlockSpec(memory_space=pltpu.VMEM)] * 10,
+        out_specs=[pl.BlockSpec(memory_space=pltpu.VMEM)] * 2,
+        scratch_shapes=[
+            pltpu.VMEM((RES_ROWS + 24, 128), jnp.float32),
+            pltpu.VMEM((TF_ROWS + 28, 128), jnp.float32),
+        ],
+        compiler_params=pltpu.CompilerParams(vmem_limit_bytes=40 * 1024 * 1024),
+    )(*grads)
+
+
+def flat_index(mesh_sizes):
+    index = 0
+    for name, size in mesh_sizes:
+        index = index * size + lax.axis_index(name)
+    return index
+
+
+def to_window(master, rows, owner):
+    lead = (owner * master.shape[0]) % 128
+    window = jnp.zeros((rows * 128,), jnp.bfloat16)
+    return lax.dynamic_update_slice(window, master.astype(jnp.bfloat16), (lead,)).reshape(rows, 128)
+
+
+def from_window(window, length_now, owner):
+    lead = (owner * length_now) % 128
+    return lax.dynamic_slice(window.reshape(-1), (lead,), (length_now,))
 
 
 def to_utts(cells):
@@ -211,7 +472,31 @@
     phone = jnp.sum((boundary[:, None, :] <= frame_ids[None, :, None]).astype(jnp.int32), axis=2)
     phone = jnp.minimum(phone, durations.shape[1] - 1)
     start_state = inputs + jax.vmap(take_rows)(encoded, phone)
-    res_whole, tf_whole = gather_weights(res_master, tf_master)
+    mesh_sizes = [(name, lax.axis_size(name)) for name in ("dp", "seq")]
+    orders = part_orders(mesh_sizes)
+    places = place_maps(orders, mesh_sizes)
+    owner = flat_index(mesh_sizes)
+    shard_lengths = (res_master.shape[0], tf_master.shape[0])
+    window_sizes = [window_rows(size, len(places[0])) for size in shard_lengths]
+    gathered = gather_windows(
+        orders,
+        to_window(res_master, window_sizes[0], owner),
+        to_window(tf_master, window_sizes[1], owner),
+    )
+    (
+        convs,
+        res_weight,
+        time_weight,
+        res_small,
+        qkv_weight,
+        out_weight,
+        up_weight,
+        down_weight,
+        tf_small,
+        wide_small,
+    ) = assemble_weights(places, shard_lengths, *gathered)
+    conv_one = convs[: 3 * C].reshape(3, C, C)
+    conv_two = convs[3 * C :].reshape(3, C, C)
     masked_in = to_utts((start_state * local_mask).astype(jnp.bfloat16))
     grad_ff = to_utts((cotangent * local_mask).astype(jnp.bfloat16))
     lengths = lax.dynamic_slice_in_dim(lengths, seq_index * utt_count, utt_count)
@@ -220,8 +505,6 @@
     wide_mask = frame_mask[:, :, None]
     key_mask = jnp.arange(key_total, dtype=jnp.int32)[None, :] < lengths[:, None]
     valid_count = lengths.astype(jnp.float32)
-    conv_one, conv_two, res_weight, time_weight, res_rows = unpack_res(res_whole)
-    res_small = res_rows.astype(jnp.float32)
     padded_one = rim_pad(masked_in)
     z_one = conv_apply(padded_one, conv_one) + res_small[0]
     norm_one, normed_one, inv_one = norm_forward(
@@ -239,9 +522,6 @@
     act_two = mish_fn(norm_two) * wide_mask
     skip_out = jnp.dot(masked_in, res_weight, preferred_element_type=jnp.float32) + res_small[6]
     block_out = act_two + skip_out
-    qkv_weight, out_weight, up_weight, down_weight, tf_rows, wide_rows = unpack_tf(tf_whole)
-    tf_small = tf_rows.astype(jnp.float32)
-    wide_small = wide_rows.astype(jnp.float32)
     attn_in = layer_norm(block_out, tf_small[0], tf_small[1]).astype(jnp.bfloat16)
     qkv_all = jnp.dot(attn_in, qkv_weight, preferred_element_type=jnp.float32).astype(jnp.bfloat16)
     queries = qkv_all[:, :, :inner].reshape(utt_count, key_total, HEADS, HD)
@@ -326,18 +606,6 @@
     block_value, block_pull = jax.vjp(layer_norm, block_out, tf_small[0], tf_small[1])
     grad_block_ln, grad_ln1_g, grad_ln1_b = block_pull(grad_attn_in)
     grad_block = grad_mid + grad_block_ln
-    tf_grad_local = jnp.concatenate(
-        [
-            grad_qkv_w.reshape(-1),
-            grad_out_w.reshape(-1),
-            grad_up_w.reshape(-1),
-            grad_down_w.reshape(-1),
-            jnp.stack(
-                [grad_ln1_g, grad_ln1_b, grad_out_b, grad_ln3_g, grad_ln3_b, grad_down_b]
-            ).reshape(-1),
-            jnp.stack([grad_up_b, grad_alpha, grad_beta]).reshape(-1),
-        ]
-    )
     grad_skip = grad_block.astype(jnp.bfloat16)
     grad_res_w = jnp.einsum("utc,utd->cd", masked_in, grad_skip, preferred_element_type=jnp.float32)
     grad_res_b = jnp.sum(grad_skip, axis=(0, 1), dtype=jnp.float32)
@@ -368,27 +636,32 @@
     grad_conv_one_b = jnp.sum(grad_z_one, axis=(0, 1), dtype=jnp.float32)
     grad_masked_in = grad_masked_in + conv_input_grad(grad_z_one, conv_one)
     grad_inputs = grad_masked_in * wide_mask
-    res_grad_local = jnp.concatenate(
-        [
-            grad_conv_one.reshape(-1),
-            grad_conv_two.reshape(-1),
-            grad_res_w.reshape(-1),
-            grad_time_w.reshape(-1),
-            jnp.stack(
-                [
-                    grad_conv_one_b,
-                    grad_gn1_g,
-                    grad_gn1_b,
-                    grad_conv_two_b,
-                    grad_gn2_g,
-                    grad_gn2_b,
-                    grad_res_b,
-                    grad_time_b,
-                ]
-            ).reshape(-1),
-        ]
-    )
-    res_share, tf_share = scatter_grads(res_grad_local, tf_grad_local)
+    grads = (
+        jnp.concatenate([grad_conv_one.reshape(-1, C), grad_conv_two.reshape(-1, C)]),
+        grad_res_w,
+        grad_time_w,
+        jnp.stack(
+            [
+                grad_conv_one_b,
+                grad_gn1_g,
+                grad_gn1_b,
+                grad_conv_two_b,
+                grad_gn2_g,
+                grad_gn2_b,
+                grad_res_b,
+                grad_time_b,
+            ]
+        ),
+        grad_qkv_w,
+        grad_out_w,
+        grad_up_w,
+        grad_down_w,
+        jnp.stack([grad_ln1_g, grad_ln1_b, grad_out_b, grad_ln3_g, grad_ln3_b, grad_down_b]),
+        jnp.stack([grad_up_b, grad_alpha, grad_beta]),
+    )
+    summed = reduce_windows(orders, *cut_grads(places, shard_lengths, window_sizes, grads))
+    res_share = from_window(summed[0], shard_lengths[0], owner)
+    tf_share = from_window(summed[1], shard_lengths[1], owner)
     tokens_total = utts_here * key_total * lax.axis_size("dp")
     rate = LEARN_BASE / math.sqrt(tokens_total)
     res_new, res_moment_new, res_average_new, res_low = update(

time: 515 us -> 337 us (0.65)
  waiting for transfers between devices: 147 us -> 18.8 us
  local copies, waits for them, and re-layouts: 123 us -> 48.3 us
  Pallas kernels: 0 us -> 70.7 us
  blocking collectives: 19.8 us -> 0 us
  matrix products: 136 us -> 120 us
  between operations: 15.1 us -> 2.02 us
  starting transfers between devices: 10.6 us -> 17 us
    unnamed x3 -> x0, waiting for transfers between devices: 99.8 us -> none
    pallas_call x0 -> x4, Pallas kernels: none -> 70.7 us  [the longest x1 34.5 us: gather_windows(): pl.pallas_call(functools.partial(gather_kernel, orders), out_shape=(jax.S...]
    unnamed x114 -> x175, local copies, waits for them, and re-layouts: 49.1 us -> 9.65 us
    reshape x10 -> x0, local copies, waits for them, and re-layouts: 22 us -> none  [the longest x1 4.82 us: scatter_grads(): tf_grad.reshape(count, -1)]
    all_to_all x1 -> x0, blocking collectives: 19.8 us -> none  [to_utts(): return lax.all_to_all(cells, 'seq', split_axis=0, concat_axis=1, tiled=True)]
    all_to_all x2, waiting for transfers between devices: 27 us -> 10.3 us  [to_frames(): lax.all_to_all(low, 'seq', split_axis=1, concat_axis=0, tiled=True)]
    slice x7 -> x0, local copies, waits for them, and re-layouts: 14.9 us -> none  [the longest x1 3.54 us: conv_apply(): weight[0]]
    all_to_all x1 -> x2, waiting for transfers between devices: 19 us -> 8.5 us  [to_utts(): return lax.all_to_all(cells, 'seq', split_axis=0, concat_axis=1, tiled=True)]
  transfers between devices with their start and end apart: 5 -> 4, of which waited for: 5 -> 2; matrix products, arithmetic and copies ran while one was open for 8% -> 7% of each run, Pallas kernels for 0% -> 21%
where the time goes in v2:
time: 337 us; the launch traced here: 332 us
  matrix products  120 us (36%)
  Pallas kernels  70.7 us (21%)
  other arithmetic  55.2 us (16%)
  local copies, waits for them, and re-layouts  48.3 us (14%)
  waiting for transfers between devices  18.8 us (6%)
  starting transfers between devices  17 us (5%)
    dot_general x1, matrix products, per_device(): jnp.dot(ff_in, up_weight, preferred_element_type=jnp.float32)  37.9 us
    pallas_call x1, Pallas kernels, gather_windows(): pl.pallas_call(functools.partial(gather_kernel, orders), out_shape=(jax.S...  34.5 us
    pallas_call x1, Pallas kernels, reduce_windows(): pl.pallas_call(functools.partial(reduce_kernel, orders), out_shape=(jax.S...  34.3 us
    gather x1, local copies, waits for them, and re-layouts, take_rows(): return phone_table[phone_rows]  14.1 us
    convert_element_type x1, other arithmetic, per_device(): grad_scores = (probs * (grad_probs - row_dot)).astype(jnp.bfloat16)  12.4 us
    dot_general x1, matrix products, per_device(): jnp.einsum('uqhd,ukhd->uhqk', grad_vals, values, preferred_element_type=j...  11.5 us
    all_to_all x2, waiting for transfers between devices, to_frames(): lax.all_to_all(low, 'seq', split_axis=1, concat_axis=0, tiled=True)  10.3 us
    unnamed x175, local copies, waits for them, and re-layouts  9.65 us
  transfers between devices with their start and end apart: 4, of which 2 were waited for; matrix products, arithmetic and copies ran while one was open for 7% of the time, Pallas kernels for 21%

profile of v2, /device:TPU:0, one launch (start us, length us, event | category | flops | bytes accessed | tf_op | source)
XLA Modules:
  0.0 332.1 jit_solution(14483148692756588839)
XLA Ops:
  2.9 14.1 %gather_fusion = f32[2048,256]{1,0:T(8,128)S(1)} fusion(f32[8,128,256]{2,1,0:T(8,128)S(1)} %copy-done, s32[2048]{0:T(1024)S(1)} %bitcast.227), kind=kCustom, calls=%fused_computation | custom fusion | bytes 4210688 | tf_op jit(solution)/shard_map/vmap()/gather | solution.py:46
  17.0 4.0 %multiply_convert_fusion.4 = (bf16[8,256,256]{2,1,0:T(8,128)(2,1)}, bf16[8,256,256]{2,1,0:T(8,128)(2,1)}) fusion(f32[8,256,256]{2,1,0:T(8,128)} %param.17, f32[8,256]{1,0:T(8,128)S(1)} %compare_convert_fusion, f32[8,256,256]{2,1,0:T(8,128)} %param.12, f32[8,256,256]{2,1,0:T(8,128)S(1)} %bitcast.238), kind=kLoop, calls=%fused_computation.45 | loop fusion | flops 2621440 | bytes 8396800 | tf_op jit(solution)/shard_map/convert_element_type | solution.py:501
  21.0 4.4 %all-to-all-start.2 = ((bf16[8,256,256]{2,1,0:T(8,128)(2,1)}), bf16[8,256,256]{2,1,0:T(8,128)(2,1)}, u32[]{:S(2)}, u32[]{:S(2)}) async-start(bf16[8,256,256]{2,1,0:T(8,128)(2,1)} %get-tuple-element.111), calls=%async_computation.2 | async-start | bytes 2097152 | tf_op jit(solution)/shard_map/all_to_all | solution.py:441
  26.7 34.5 %shard_map.211 = (bf16[32,192,128]{2,1,0:T(8,128)(2,1)S(1)}, bf16[32,176,128]{2,1,0:T(8,128)(2,1)S(1)}) custom-call(bf16[192,128]{1,0:T(8,128)(2,1)S(1)} %bitcast.223, bf16[176,128]{1,0:T(8,128)(2,1)S(1)} %bitcast.224), custom_call_target="tpu_custom_call" | custom-call | tf_op jit(solution)/shard_map/pallas_call | solution.py:231
  62.9 4.4 %all-to-all-start = ((bf16[8,256,256]{2,1,0:T(8,128)(2,1)}), bf16[8,256,256]{2,1,0:T(8,128)(2,1)}, u32[]{:S(2)}, u32[]{:S(2)}) async-start(bf16[8,256,256]{2,1,0:T(8,128)(2,1)} %get-tuple-element.112), calls=%async_computation | async-start | bytes 2097152 | tf_op jit(solution)/shard_map/all_to_all | solution.py:441
  69.0 2.3 copy.101
  73.4 8.5 %all-to-all-done = bf16[8,256,256]{2,1,0:T(8,128)(2,1)} async-done(((bf16[8,256,256]{2,1,0:T(8,128)(2,1)}), bf16[8,256,256]{2,1,0:T(8,128)(2,1)}, u32[]{:S(2)}, u32[]{:S(2)}) %all-to-all-start) | async-done | bytes 1048608 | tf_op jit(solution)/shard_map/all_to_all | solution.py:441
  84.0 2.2 multiply_reduce_fusion.14
  87.0 3.2 multiply_convert_fusion.6
  94.1 3.9 %fusion.110 = (f32[2,1024]{1,0:T(2,128)S(1)}, f32[2,1024,256]{2,1,0:T(8,128)S(1)}) fusion(f32[256]{0:T(256)S(1)} %bitcast.306, bf16[2,1024,256]{2,1,0:T(8,128)(2,1)} %bitcast.231, bf16[256,256]{1,0:T(8,128)(2,1)S(1)} %get-tuple-element.33, f32[2,1024]{1,0:T(2,128)S(1)} %get-tuple-element.132, f32[256]{0:T(256)S(1)} %bitcast.294, f32[256]{0:T(256)S(1)} %bitcast.274, ...), kind=kOutput, calls=%fused_computation.232 | convolution fusion | flops 275249152 | bytes 5397504 | tf_op jit(solution)/shard_map/dot_general | solution.py:523
  100.3 3.3 fusion.6
  103.6 3.7 %fusion = f32[2,2,1024]{2,1,0:T(2,128)S(1)} fusion(f32[2,2,1024]{2,1,0:T(2,128)S(1)} %get-tuple-element.137, f32[2,2,1024,1024]{2,3,1,0:T(8,128)S(1)} %get-tuple-element.138, pred[2,1024]{1,0:T(4,128)(4,1)S(1)} %get-tuple-element.131), kind=kLoop, calls=%fused_computation.7 | loop fusion | flops 16773120 | bytes 16812032 | tf_op jit(solution)/shard_map/reduce_sum | solution.py:538
  107.3 4.6 %fusion.13 = bf16[2,2,64,1024]{3,2,1,0:T(8,128)(2,1)S(1)} fusion(bf16[2,1024,2,64]{1,3,2,0:T(8,128)(2,1)S(1)} %bitcast.248, f32[2,2,1024]{2,1,0:T(2,128)S(1)} %fusion, f32[2,2,1024]{2,1,0:T(2,128)S(1)} %get-tuple-element.137, f32[2,2,1024,1024]{2,3,1,0:T(8,128)S(1)} %get-tuple-element.138, pred[2,1024]{1,0:T(4,128)(4,1)S(1)} %get-tuple-element.131), kind=kOutput, calls=%fused_computation.83 | convolution fusion | flops 558104576 | bytes 17860608 | tf_op jit(solution)/shard_map/uhqk,ukhd->uqhd/dot_general | solution.py:541
  115.9 37.9 %multiply_reduce_fusion.2 = (f32[1024]{0:T(1024)}, f32[1024]{0:T(1024)}, f32[1024]{0:T(1024)}, bf16[2,1024,1024]{2,1,0:T(8,128)(2,1)S(1)}, bf16[2,1024,1024]{2,1,0:T(8,128)(2,1)}) fusion(f32[1024]{0:T(1024)S(1)} %bitcast.291, f32[1024]{0:T(1024)S(1)} %bitcast.292, f32[2,1024,1024]{2,1,0:T(8,128)S(1)} %fusion.27, f32[1024]{0:T(1024)S(1)} %bitcast.258, ...), kind=kOutput, calls=%fused_computation.11 | convolution fusion | flops 1118303232 | bytes 19445760 | tf_op jit(solution)/shard_map/dot_general | solution.py:546
  155.7 2.5 multiply_reduce_fusion.3
  161.7 5.2 %fusion.8 = bf16[2,2,64,1024]{3,2,1,0:T(8,128)(2,1)} fusion(bf16[2,1024,2,64]{1,3,2,0:T(8,128)(2,1)S(1)} %bitcast.246, f32[2,2,1024]{2,1,0:T(2,128)S(1)} %log_add_fusion, f32[2,2,1024,1024]{2,3,1,0:T(8,128)S(1)} %get-tuple-element.138, pred[2,1024]{1,0:T(4,128)(4,1)S(1)} %get-tuple-element.131), kind=kOutput, calls=%fused_computation.79 | convolution fusion | flops 553910272 | bytes 17844224 | tf_op jit(solution)/shard_map/uhqk,uqhd->ukhd/dot_general | solution.py:588
  166.9 11.5 %multiply_reduce_fusion = (f32[2,2,1024]{2,1,0:T(2,128)S(1)}, f32[2,2,1024,1024]{2,3,1,0:T(8,128)}) fusion(f32[2,2,1024]{2,1,0:T(2,128)S(1)} %log_add_fusion, f32[2,2,1024,1024]{2,3,1,0:T(8,128)} %copy-done.12, pred[2,1024]{1,0:T(4,128)(4,1)S(1)} %get-tuple-element.131, bf16[2,1024,2,64]{1,3,2,0:T(8,128)(2,1)S(1)} %bitcast.247, ...), kind=kOutput, calls=%fused_computation.2 | convolution fusion | flops 557838336 | bytes 34637824 | tf_op jit(solution)/shard_map/uqhd,ukhd->uhqk/dot_general | solution.py:575
  178.4 12.4 %multiply_convert_fusion = bf16[2,2,1024,1024]{2,3,1,0:T(8,128)(2,1)S(1)} fusion(f32[2,2,1024,1024]{2,3,1,0:T(8,128)} %get-tuple-element.143, f32[2,2,1024]{2,1,0:T(2,128)S(1)} %get-tuple-element.142, f32[2,2,1024]{2,1,0:T(2,128)S(1)} %log_add_fusion, f32[2,2,1024,1024]{2,3,1,0:T(8,128)} %copy-done.12, pred[2,1024]{1,0:T(4,128)(4,1)S(1)} %get-tuple-element.131), kind=kLoop, calls=%fused_computation.1 | loop fusion | flops 25165824 | bytes 41977856 | tf_op jit(solution)/shard_map/convert_element_type | solution.py:579
  190.8 2.7 fusion.12
  193.4 2.4 fusion.11
  201.0 4.4 %convolution_bitcast_fusion.2.refs_4_ = f32[256,384]{1,0:T(8,128)} fusion(bf16[2,1024,128]{2,1,0:T(8,128)(2,1)} %copy.107, bf16[2,1024,128]{2,1,0:T(8,128)(2,1)} %copy.106, bf16[2,1024,128]{2,1,0:T(8,128)(2,1)} %copy.105, f32[2,1024,256]{2,1,0:T(8,128)} %copy-done.16, f32[256]{0:T(256)S(1)} %bitcast.282, f32[256]{0:T(256)S(1)} %bitcast.261, ...), kind=kOutput, calls=%fused_computation.84 | convolution fusion | flops 409993216 | bytes 4081664 | tf_op jit(solution)/shard_map/utc,utd->cd/dot_general | solution.py:602
  208.8 2.5 convert_reduce_fusion.3
  214.3 5.2 %multiply_reduce_fusion.5 = (f32[256]{0:T(256)}, f32[2,256]{1,0:T(2,128)S(1)}, f32[2,256]{1,0:T(2,128)S(1)}, f32[256]{0:T(256)}, f32[2,1024,256]{2,1,0:T(8,128)}) fusion(f32[2,1024,256]{2,1,0:T(8,128)S(1)} %copy-done.25, f32[2,256]{1,0:T(2,128)S(1)} %copy-done.62, f32[2,256]{1,0:T(2,128)S(1)} %copy-done.64, f32[256]{0:T(256)S(1)} %bitcast.276, ...), kind=kLoop, calls=%fused_computation.29 | loop fusion | flops 19921408 | bytes 6311936 | tf_op jit(solution)/shard_map/reduce_sum | solution.py:118
  221.4 3.6 %convert_reduce_fusion.4 = (f32[256]{0:T(256)}, bf16[2,1024,256]{2,1,0:T(8,128)(2,1)S(1)}) fusion(f32[2,256]{1,0:T(2,128)} %mul.600, f32[2,1024,256]{2,1,0:T(8,128)} %get-tuple-element.134, f32[2,256]{1,0:T(2,128)} %copy-done.63, f32[2,256]{1,0:T(2,128)} %add.404, f32[2,1024]{1,0:T(2,128)S(1)} %get-tuple-element.132, f32[2,1024,256]{2,1,0:T(8,128)} %get-tuple-element.86, ...), kind=kLoop, calls=%fused_computation.30 | loop fusion | flops 5766912 | bytes 5261312 | tf_op jit(solution)/shard_map/reduce_sum | solution.py:622
  230.6 5.9 %fusion.101 = (f32[256]{0:T(256)}, f32[2,256]{1,0:T(2,128)}, f32[256]{0:T(256)}, f32[2,256]{1,0:T(2,128)S(1)}, f32[2,256]{1,0:T(2,128)S(1)}, /*index=5*/f32[256]{0:T(256)}, f32[2,1024,256]{2,1,0:T(8,128)}) fusion(f32[256]{0:T(256)S(1)} %bitcast.280, f32[256]{0:T(256)S(1)} %bitcast.271, f32[2,256]{1,0:T(2,128)S(1)} %mul.530, ...), kind=kOutput, calls=%fused_computation.224 | convolution fusion | flops 290977536 | bytes 9591808 | tf_op jit(solution)/shard_map/utd,cd->utc/dot_general | solution.py:84
  238.4 3.5 %convert_reduce_fusion.5 = (f32[256]{0:T(256)}, bf16[2,1024,256]{2,1,0:T(8,128)(2,1)S(1)}) fusion(f32[2,256]{1,0:T(2,128)} %mul.615, f32[2,1024,256]{2,1,0:T(8,128)} %get-tuple-element.133, f32[2,256]{1,0:T(2,128)S(1)} %copy-done.60, f32[2,256]{1,0:T(2,128)} %add.411, f32[2,1024]{1,0:T(2,128)S(1)} %get-tuple-element.132, ...), kind=kLoop, calls=%fused_computation.32 | loop fusion | flops 5766912 | bytes 5261312 | tf_op jit(solution)/shard_map/reduce_sum | solution.py:636
  249.1 2.3 convolution_bitcast_fusion.refs_7_
  254.8 4.7 %all-to-all-start.1 = ((bf16[2,1024,256]{2,0,1:T(2,128)(2,1)}), bf16[2,1024,256]{2,0,1:T(2,128)(2,1)}, u32[]{:S(2)}, u32[]{:S(2)}) async-start(bf16[2,1024,256]{2,0,1:T(2,128)(2,1)} %copy.99), calls=%async_computation.1 | async-start | bytes 2097152 | tf_op jit(solution)/shard_map/all_to_all | solution.py:446
  259.5 2.5 fusion.99.refs_2_
  272.2 34.3 %shard_map.214 = (f32[192,128]{1,0:T(8,128)S(1)}, f32[176,128]{1,0:T(8,128)S(1)}) custom-call(bf16[32,192,128]{2,1,0:T(8,128)(2,1)S(1)} %get-tuple-element.40.in_a, bf16[32,176,128]{2,1,0:T(8,128)(2,1)S(1)} %get-tuple-element.41.in_b), custom_call_target="tpu_custom_call" | custom-call | tf_op jit(solution)/shard_map/pallas_call | solution.py:304
  311.7 3.5 %all-to-all-start.3 = ((bf16[2,1024,256]{2,0,1:T(2,128)(2,1)}), bf16[2,1024,256]{2,0,1:T(2,128)(2,1)S(1)}, u32[]{:S(2)}, u32[]{:S(2)}) async-start(bf16[2,1024,256]{2,0,1:T(2,128)(2,1)} %copy.108), calls=%async_computation.3 | async-start | bytes 2097152 | tf_op jit(solution)/shard_map/all_to_all | solution.py:446
  319.4 10.3 %all-to-all-done.3 = bf16[2,1024,256]{2,0,1:T(2,128)(2,1)S(1)} async-done(((bf16[2,1024,256]{2,0,1:T(2,128)(2,1)}), bf16[2,1024,256]{2,0,1:T(2,128)(2,1)S(1)}, u32[]{:S(2)}, u32[]{:S(2)}) %all-to-all-start.3) | async-done | bytes 1048608 | tf_op jit(solution)/shard_map/all_to_all | solution.py:446
  (296 shorter events, 80.0 us)
Async XLA Ops:
  21.0 41.9 %all-to-all-start.2 = ((bf16[8,256,256]{2,1,0:T(8,128)(2,1)}), bf16[8,256,256]{2,1,0:T(8,128)(2,1)}, u32[]{:S(2)}, u32[]{:S(2)}) async-start(bf16[8,256,256]{2,1,0:T(8,128)(2,1)} %get-tuple-element.111), calls=%async_computation.2 | async-start | bytes 2097152 | tf_op jit(solution)/shard_map/all_to_all | solution.py:441
  25.4 36.8 %copy-start.84 = (s32[8]{0:T(128)S(1)}, s32[8]{0:T(128)}, u32[]{:S(2)}) copy-start(s32[8]{0:T(128)} %param.15) | copy-start | bytes 100
  62.3 53.6 %copy-start.10 = (bf16[256,1024]{1,0:T(8,128)(2,1)}, bf16[256,1024]{1,0:T(8,128)(2,1)S(1)}, u32[]{:S(2)}) copy-start(bf16[256,1024]{1,0:T(8,128)(2,1)S(1)} %get-tuple-element.37) | copy-start | bytes 1572868
  62.4 31.3 %copy-start.67 = (f32[2]{0:T(128)}, f32[2]{0:T(128)S(1)}, u32[]{:S(2)}) copy-start(f32[2]{0:T(128)S(1)} %get-tuple-element.93) | copy-start | bytes 28
  62.5 188.9 %copy-start.43 = (f32[2,1024]{1,0:T(2,128)}, f32[2,1024]{1,0:T(2,128)S(1)}, u32[]{:S(2)}) copy-start(f32[2,1024]{1,0:T(2,128)S(1)} %get-tuple-element.132) | copy-start | bytes 24580
  62.9 18.9 %all-to-all-start = ((bf16[8,256,256]{2,1,0:T(8,128)(2,1)}), bf16[8,256,256]{2,1,0:T(8,128)(2,1)}, u32[]{:S(2)}, u32[]{:S(2)}) async-start(bf16[8,256,256]{2,1,0:T(8,128)(2,1)} %get-tuple-element.112), calls=%async_computation | async-start | bytes 2097152 | tf_op jit(solution)/shard_map/all_to_all | solution.py:441
  68.0 19.0 %copy-start.70 = (f32[1,256]{1,0:T(1,128)}, f32[1,256]{1,0:T(1,128)S(1)}, u32[]{:S(2)}) copy-start(f32[1,256]{1,0:T(1,128)S(1)} %get-tuple-element.146) | copy-start | bytes 3076
  68.0 19.0 %copy-start.74 = (f32[1,256]{1,0:T(1,128)}, f32[1,256]{1,0:T(1,128)S(1)}, u32[]{:S(2)}) copy-start(f32[1,256]{1,0:T(1,128)S(1)} %get-tuple-element.147) | copy-start | bytes 3076
  68.0 26.1 %copy-start.72 = (f32[1,256]{1,0:T(1,128)}, f32[1,256]{1,0:T(1,128)S(1)}, u32[]{:S(2)}) copy-start(f32[1,256]{1,0:T(1,128)S(1)} %get-tuple-element.152) | copy-start | bytes 3076
  68.0 26.1 %copy-start.81 = (f32[1,256]{1,0:T(1,128)}, f32[1,256]{1,0:T(1,128)S(1)}, u32[]{:S(2)}) copy-start(f32[1,256]{1,0:T(1,128)S(1)} %get-tuple-element.150) | copy-start | bytes 3076
  68.0 30.7 %copy-start.65 = (f32[1,256]{1,0:T(1,128)}, f32[1,256]{1,0:T(1,128)S(1)}, u32[]{:S(2)}) copy-start(f32[1,256]{1,0:T(1,128)S(1)} %get-tuple-element.118) | copy-start | bytes 3076
  68.0 30.7 %copy-start.76 = (f32[1,256]{1,0:T(1,128)}, f32[1,256]{1,0:T(1,128)S(1)}, u32[]{:S(2)}) copy-start(f32[1,256]{1,0:T(1,128)S(1)} %get-tuple-element.117) | copy-start | bytes 3076
  97.9 14.0 %copy-start.16 = (f32[2,1024,256]{2,1,0:T(8,128)}, f32[2,1024,256]{2,1,0:T(8,128)S(1)}, u32[]{:S(2)}) copy-start(f32[2,1024,256]{2,1,0:T(8,128)S(1)} %get-tuple-element.136) | copy-start | bytes 6291460
  103.6 58.1 %copy-start.12 = (f32[2,2,1024,1024]{2,3,1,0:T(8,128)}, f32[2,2,1024,1024]{2,3,1,0:T(8,128)S(1)}, u32[]{:S(2)}) copy-start(f32[2,2,1024,1024]{2,3,1,0:T(8,128)S(1)} %get-tuple-element.138) | copy-start | bytes 50331652
  112.6 45.6 %copy-start.22 = (f32[2,1024,256]{2,1,0:T(8,128)}, f32[2,1024,256]{2,1,0:T(8,128)S(1)}, u32[]{:S(2)}) copy-start(f32[2,1024,256]{2,1,0:T(8,128)S(1)} %get-tuple-element.140) | copy-start | bytes 6291460
  254.8 7.2 %copy-start.9 = (f32[3,1024]{1,0:T(4,128)S(1)}, f32[3,1024]{1,0:T(4,128)}, u32[]{:S(2)}) copy-start(f32[3,1024]{1,0:T(4,128)} %copy-done.8) | copy-start | bytes 36868
  254.8 7.2 %copy-start.80 = (f32[1024]{0:T(1024)S(1)}, f32[1024]{0:T(1024)}, u32[]{:S(2)}) copy-start(f32[1024]{0:T(1024)} %get-tuple-element.44) | copy-start | bytes 12292
  254.8 7.2 %copy-start.34 = (f32[1,256,256]{2,1,0:T(8,128)S(1)}, f32[1,256,256]{2,1,0:T(8,128)}, u32[]{:S(2)}) copy-start(f32[1,256,256]{2,1,0:T(8,128)} %convolution_bitcast_fusion.4) | copy-start | bytes 786436
  254.8 7.2 %copy-start.35 = (f32[1,256,256]{2,1,0:T(8,128)S(1)}, f32[1,256,256]{2,1,0:T(8,128)}, u32[]{:S(2)}) copy-start(f32[1,256,256]{2,1,0:T(8,128)} %convolution_bitcast_fusion.5) | copy-start | bytes 786436
  254.8 7.2 %copy-start.36 = (f32[1,256,256]{2,1,0:T(8,128)S(1)}, f32[1,256,256]{2,1,0:T(8,128)}, u32[]{:S(2)}) copy-start(f32[1,256,256]{2,1,0:T(8,128)} %convolution_bitcast_fusion.6) | copy-start | bytes 786436
  254.8 7.3 %copy-start.37 = (f32[1,256,256]{2,1,0:T(8,128)S(1)}, f32[1,256,256]{2,1,0:T(8,128)}, u32[]{:S(2)}) copy-start(f32[1,256,256]{2,1,0:T(8,128)} %convolution_bitcast_fusion.7) | copy-start | bytes 786436
  254.8 7.3 %copy-start.38 = (f32[1,256,256]{2,1,0:T(8,128)S(1)}, f32[1,256,256]{2,1,0:T(8,128)}, u32[]{:S(2)}) copy-start(f32[1,256,256]{2,1,0:T(8,128)} %convolution_bitcast_fusion.8) | copy-start | bytes 786436
  254.8 56.9 %all-to-all-start.1 = ((bf16[2,1024,256]{2,0,1:T(2,128)(2,1)}), bf16[2,1024,256]{2,0,1:T(2,128)(2,1)}, u32[]{:S(2)}, u32[]{:S(2)}) async-start(bf16[2,1024,256]{2,0,1:T(2,128)(2,1)} %copy.99), calls=%async_computation.1 | async-start | bytes 2097152 | tf_op jit(solution)/shard_map/all_to_all | solution.py:446
  271.3 35.2 %copy-start.49 = (f32[20624]{0:T(1024)S(1)}, f32[20624]{0:T(1024)}, u32[]{:S(2)}) copy-start(f32[20624]{0:T(1024)} %param.21) | copy-start | bytes 247492
  271.3 35.2 %copy-start.55 = (f32[20624]{0:T(1024)S(1)}, f32[20624]{0:T(1024)}, u32[]{:S(2)}) copy-start(f32[20624]{0:T(1024)} %param.22) | copy-start | bytes 247492
  271.3 36.7 %copy-start.32 = (f32[2,1024,256]{2,1,0:T(8,128)S(1)}, f32[2,1024,256]{2,1,0:T(8,128)}, u32[]{:S(2)}) copy-start(f32[2,1024,256]{2,1,0:T(8,128)} %fusion.50) | copy-start | bytes 6291460
  271.3 36.7 %copy-start.33 = (f32[2,1024,256]{2,1,0:T(8,128)S(1)}, f32[2,1024,256]{2,1,0:T(8,128)}, u32[]{:S(2)}) copy-start(f32[2,1024,256]{2,1,0:T(8,128)} %fusion.15) | copy-start | bytes 6291460
  272.2 35.1 %copy-start.56 = (f32[20624]{0:T(1024)S(1)}, f32[20624]{0:T(1024)}, u32[]{:S(2)}) copy-start(f32[20624]{0:T(1024)} %param.23) | copy-start | bytes 247492
  272.2 35.8 %copy-start.21 = (bf16[2,1024,256]{2,1,0:T(8,128)(2,1)S(1)}, bf16[2,1024,256]{2,1,0:T(8,128)(2,1)}, u32[]{:S(2)}) copy-start(bf16[2,1024,256]{2,1,0:T(8,128)(2,1)} %copy-done.20) | copy-start | bytes 3145732
  272.2 35.8 %copy-start.31 = (f32[2,1024,256]{2,1,0:T(8,128)S(1)}, f32[2,1024,256]{2,1,0:T(8,128)}, u32[]{:S(2)}) copy-start(f32[2,1024,256]{2,1,0:T(8,128)} %fusion.37) | copy-start | bytes 6291460
  272.2 35.8 %copy-start.44 = (f32[2,1024]{1,0:T(2,128)S(1)}, f32[2,1024]{1,0:T(2,128)}, u32[]{:S(2)}) copy-start(f32[2,1024]{1,0:T(2,128)} %copy-done.43) | copy-start | bytes 24580
  311.7 17.9 %all-to-all-start.3 = ((bf16[2,1024,256]{2,0,1:T(2,128)(2,1)}), bf16[2,1024,256]{2,0,1:T(2,128)(2,1)S(1)}, u32[]{:S(2)}, u32[]{:S(2)}) async-start(bf16[2,1024,256]{2,0,1:T(2,128)(2,1)} %copy.108), calls=%async_computation.3 | async-start | bytes 2097152 | tf_op jit(solution)/shard_map/all_to_all | solution.py:446
  (59 other events, 165.0 us)

commit v3 on v2

--- a/solution.py
+++ b/solution.py
@@ -446,6 +446,492 @@
     return lax.all_to_all(low, "seq", split_axis=1, concat_axis=0, tiled=True).astype(jnp.float32)
 
 
+SIN_TERMS = (
+    0.9999999956945583,
+    -0.1666665793542191,
+    0.008333049779226345,
+    -0.00019808982984063025,
+    2.605019582312477e-06,
+)
+COS_TERMS = (
+    0.9999999997785896,
+    -0.4999999935376167,
+    0.04166663608814044,
+    -0.0013888359276781354,
+    2.47600539678114e-05,
+    -2.6049608156992194e-07,
+)
+PI_PARTS = (3.140625, 0.0009670257568359375, 6.27832957178498e-07)
+ROUND_SHIFT = 12582912.0
+TILE = 256
+
+
+def mm(left, right):
+    return jnp.dot(left, right, preferred_element_type=jnp.float32)
+
+
+def mm_right(left, right):
+    return lax.dot_general(
+        left, right, (((1,), (1,)), ((), ())), preferred_element_type=jnp.float32
+    )
+
+
+def mm_left(left, right):
+    return lax.dot_general(
+        left, right, (((0,), (0,)), ((), ())), preferred_element_type=jnp.float32
+    )
+
+
+def column_sum(cells):
+    return jnp.sum(cells, axis=0, keepdims=True)
+
+
+def sin_cos(angle):
+    turns = (angle * (1.0 / math.pi) + ROUND_SHIFT) - ROUND_SHIFT
+    rest = angle - turns * PI_PARTS[0]
+    rest = rest - turns * PI_PARTS[1]
+    rest = rest - turns * PI_PARTS[2]
+    square = rest * rest
+    sine = SIN_TERMS[-1]
+    for term in SIN_TERMS[-2::-1]:
+        sine = sine * square + term
+    cosine = COS_TERMS[-1]
+    for term in COS_TERMS[-2::-1]:
+        cosine = cosine * square + term
+    return (sine * rest, cosine)
+
+
+def mish_value(signal):
+    expo = jnp.exp(jnp.minimum(signal, 20.0))
+    upper = expo * (expo + 2.0)
+    return signal * (upper / (upper + 2.0))
+
+
+def mish_slope(signal):
+    expo = jnp.exp(jnp.minimum(signal, 20.0))
+    upper = expo * (expo + 2.0)
+    inverse = 1.0 / (upper + 2.0)
+    return upper * inverse + signal * (4.0 * expo * (1.0 + expo)) * (inverse * inverse)
+
+
+def row_norm(signal):
+    center = signal - jnp.mean(signal, axis=-1, keepdims=True)
+    spread = jnp.mean(center * center, axis=-1, keepdims=True)
+    inverse = lax.rsqrt(spread + EPSILON)
+    return (center * inverse, inverse)
+
+
+def row_norm_back(grad_out, normed, inverse, gain_row):
+    inner_grad = grad_out * gain_row
+    first = jnp.mean(inner_grad, axis=-1, keepdims=True)
+    second = jnp.mean(inner_grad * normed, axis=-1, keepdims=True)
+    return (inner_grad - first - normed * second) * inverse
+
+
+def step_kernel(
+    lengths_ref,
+    x_ref,
+    g_ref,
+    time_ref,
+    convs_ref,
+    res_ref,
+    rows_ref,
+    qkv_ref,
+    out_ref,
+    up_ref,
+    down_ref,
+    tf_rows_ref,
+    wide_ref,
+    final_ref,
+    gin_ref,
+    gtime_ref,
+    gconvs_ref,
+    gres_ref,
+    grows_ref,
+    gqkv_ref,
+    gout_ref,
+    gup_ref,
+    gdown_ref,
+    gtf_ref,
+    gwide_ref,
+    pad,
+    col_one,
+    col_two,
+    col_grad,
+    z_one,
+    z_two,
+    block,
+    grad_mid,
+    grad_norm,
+    attn_in,
+    heads_q,
+    heads_k,
+    heads_v,
+    heads_g,
+    attn_vals,
+    probs,
+    snake,
+    grad_up,
+    ff_in,
+    grad_attn,
+    grad_key,
+    grad_value,
+    grad_query,
+    grad_qkv,
+    grad_skip,
+):
+    frames = z_one.shape[0]
+    tiles = frames // TILE
+    utt = pl.program_id(0)
+    length_now = lengths_ref[utt]
+    number = length_now.astype(jnp.float32) * (C // GROUPS)
+
+    @pl.when(utt == 0)
+    def clear():
+        for ref in (
+            gconvs_ref,
+            gres_ref,
+            grows_ref,
+            gqkv_ref,
+            gout_ref,
+            gup_ref,
+            gdown_ref,
+            gtf_ref,
+            gwide_ref,
+        ):
+            ref[...] = jnp.zeros_like(ref)
+
+    edge = jnp.zeros((8, C), jnp.float32)
+    pad[0:8, :] = edge
+    pad[frames + 8 : frames + 16, :] = edge
+    gtime_ref[...] = jnp.zeros_like(gtime_ref)
+    group_row = lax.broadcasted_iota(jnp.int32, (C, C), 0) // (C // GROUPS)
+    group_column = lax.broadcasted_iota(jnp.int32, (C, C), 1) // (C // GROUPS)
+    group_ones = (group_row == group_column).astype(jnp.float32)
+    lane = lax.broadcasted_iota(jnp.int32, (1, INNER), 1) // HD
+    head_masks = [(lane == head).astype(jnp.float32) for head in range(HEADS)]
+    key_bias = jnp.where(
+        lax.broadcasted_iota(jnp.int32, (1, frames), 1) < length_now, 0.0, MASK_FILL
+    )
+
+    def rows_at(index, lead=0):
+        return pl.ds(pl.multiple_of(index * TILE + lead, 8), TILE)
+
+    def tile_mask(index):
+        ids = lax.broadcasted_iota(jnp.int32, (TILE, 1), 0) + index * TILE
+        return (ids < length_now).astype(jnp.float32)
+
+    def group_sum(row):
+        wide = jnp.broadcast_to(row, (8, C))
+        return jnp.dot(
+            wide,
+            group_ones,
+            precision=lax.Precision.HIGHEST,
+            preferred_element_type=jnp.float32,
+        )[0:1]
+
+    def build_columns(target):
+        for index in range(tiles):
+            start = index * TILE
+            for tap in range(3):
+                piece = pad[start + 7 + tap : start + 7 + tap + TILE, :]
+                target[start : start + TILE, tap * C : (tap + 1) * C] = piece.astype(jnp.bfloat16)
+
+    def loop(body):
+        def wrapped(index, carry):
+            body(index)
+            return carry
+
+        lax.fori_loop(0, tiles, wrapped, 0)
+
+    def conv_stage(columns, base, bias_at, target):
+        def one(index, carry):
+            rows = rows_at(index)
+            cells = mm(columns[rows, :], convs_ref[base : base + 3 * C, :])
+            cells = cells + rows_ref[bias_at : bias_at + 1, :]
+            target[rows, :] = cells
+            masked = cells * tile_mask(index)
+            return (carry[0] + column_sum(masked), carry[1] + column_sum(masked * masked))
+
+        zero = jnp.zeros((1, C), jnp.float32)
+        total, squares = lax.fori_loop(0, tiles, one, (zero, zero))
+        mean_row = group_sum(total) / number
+        inv_row = lax.rsqrt(group_sum(squares) / number - mean_row * mean_row + EPSILON)
+        return (mean_row, inv_row)
+
+    def copy_in(index):
+        pad[rows_at(index, 8), :] = x_ref[0, rows_at(index), :].astype(jnp.float32)
+
+    loop(copy_in)
+    build_columns(col_one)
+    mean_one, inv_one = conv_stage(col_one, 0, 0, z_one)
+
+    def hidden(index):
+        normed = (z_one[rows_at(index), :] - mean_one) * inv_one
+        act = mish_value(normed * rows_ref[1:2, :] + rows_ref[2:3, :])
+        pad[rows_at(index, 8), :] = (act + time_ref[0]) * tile_mask(index)
+
+    loop(hidden)
+    build_columns(col_two)
+    mean_two, inv_two = conv_stage(col_two, 3 * C, 3, z_two)
+
+    def enter(index):
+        rows = rows_at(index)
+        normed = (z_two[rows, :] - mean_two) * inv_two
+        act = mish_value(normed * rows_ref[4:5, :] + rows_ref[5:6, :]) * tile_mask(index)
+        state = act + mm(x_ref[0, rows, :], res_ref[...]) + rows_ref[6:7, :]
+        block[rows, :] = state
+        normed, _ = row_norm(state)
+        low = (normed * tf_rows_ref[0:1, :] + tf_rows_ref[1:2, :]).astype(jnp.bfloat16)
+        attn_in[rows, :] = low
+        parts = mm(low, qkv_ref[...]).astype(jnp.bfloat16).astype(jnp.float32)
+        query = parts[:, :INNER] * SCORE_SCALE
+        for head in range(HEADS):
+            heads_q[head, rows, :] = (query * head_masks[head]).astype(jnp.bfloat16)
+            heads_k[head, rows, :] = (parts[:, INNER : 2 * INNER] * head_masks[head]).astype(
+                jnp.bfloat16
+            )
+            heads_v[head, rows, :] = (parts[:, 2 * INNER :] * head_masks[head]).astype(
+                jnp.bfloat16
+            )
+
+    loop(enter)
+
+    def attend(index):
+        rows = rows_at(index)
+        total = jnp.zeros((TILE, INNER), jnp.float32)
+        for head in range(HEADS):
+            scores = mm_right(heads_q[head, rows, :], heads_k[head]) + key_bias
+            expo = jnp.exp(scores - jnp.max(scores, axis=-1, keepdims=True))
+            chance = expo * (1.0 / jnp.sum(expo, axis=-1, keepdims=True))
+            probs[head, rows, :] = chance
+            total = total + mm(chance.astype(jnp.bfloat16), heads_v[head])
+        attn_vals[rows, :] = total.astype(jnp.bfloat16)
+
+    loop(attend)
+
+    def feed(index):
+        rows = rows_at(index)
+        mid = block[rows, :] + mm(attn_vals[rows, :], out_ref[...]) + tf_rows_ref[2:3, :]
+        normed, inverse = row_norm(mid)
+        low = (normed * tf_rows_ref[3:4, :] + tf_rows_ref[4:5, :]).astype(jnp.bfloat16)
+        ff_in[rows, :] = low
+        grad_low = g_ref[0, rows, :]
+        result = jnp.zeros((TILE, C), jnp.float32)
+        grad_in = jnp.zeros((TILE, C), jnp.float32)
+        for chunk in range(F // 256):
+            lanes = slice(chunk * 256, (chunk + 1) * 256)
+            up_out = mm(low, up_ref[:, lanes]) + wide_ref[0:1, lanes]
+            grad_snake = mm_right(grad_low, down_ref[lanes, :])
+            speed = jnp.exp(wide_ref[1:2, lanes])
+            depth = 1.0 / (jnp.exp(wide_ref[2:3, lanes]) + 1e-09)
+            angle = up_out * speed
+            sine, cosine = sin_cos(angle)
+            square = sine * sine
+            value = (up_out + square * depth).astype(jnp.bfloat16)
+            snake[rows, lanes] = value
+            result = result + mm(value, down_ref[lanes, :])
+            slope = grad_snake * ((2.0 * sine) * cosine) * depth
+            grad_here = (grad_snake + slope * speed).astype(jnp.bfloat16)
+            grad_up[rows, lanes] = grad_here
+            grad_in = grad_in + mm_right(grad_here, up_ref[:, lanes])
+            gwide_ref[0:1, lanes] += column_sum(grad_here.astype(jnp.float32))
+            gwide_ref[1:2, lanes] += column_sum(slope * angle)
+            gwide_ref[2:3, lanes] += column_sum(grad_snake * square)
+        final_ref[0, rows, :] = ((mid + result + tf_rows_ref[5:6, :]) * tile_mask(index)).astype(
+            jnp.bfloat16
+        )
+        grad_wide = grad_low.astype(jnp.float32)
+        gtf_ref[5:6, :] += column_sum(grad_wide)
+        gtf_ref[3:4, :] += column_sum(grad_in * normed)
+        gtf_ref[4:5, :] += column_sum(grad_in)
+        grad_state = grad_wide + row_norm_back(grad_in, normed, inverse, tf_rows_ref[3:4, :])
+        grad_mid[rows, :] = grad_state
+        grad_state = grad_state.astype(jnp.bfloat16)
+        grad_attn[rows, :] = grad_state
+        gtf_ref[2:3, :] += column_sum(grad_state.astype(jnp.float32))
+        grad_vals = mm_right(grad_state, out_ref[...]).astype(jnp.bfloat16).astype(jnp.float32)
+        for head in range(HEADS):
+            heads_g[head, rows, :] = (grad_vals * head_masks[head]).astype(jnp.bfloat16)
+
+    loop(feed)
+
+    def feed_weights(index, carry):
+        lanes = pl.ds(pl.multiple_of(index * 256, 256), 256)
+        gdown_ref[lanes, :] += mm_left(snake[:, lanes], g_ref[0])
+        gup_ref[:, lanes] += mm_left(ff_in[...], grad_up[:, lanes])
+        return carry
+
+    lax.fori_loop(0, F // 256, feed_weights, 0)
+    gout_ref[...] += mm_left(attn_vals[...], grad_attn[...])
+    grad_key[...] = jnp.zeros_like(grad_key)
+    grad_value[...] = jnp.zeros_like(grad_value)
+
+    def attend_back(index):
+        rows = rows_at(index)
+        total = jnp.zeros((TILE, INNER), jnp.float32)
+        for head in range(HEADS):
+            grad_out = heads_g[head, rows, :]
+            chance = probs[head, rows, :]
+            grad_probs = mm_right(grad_out, heads_v[head])
+            dot_row = jnp.sum(chance * grad_probs, axis=-1, keepdims=True)
+            grad_scores = (chance * (grad_probs - dot_row)).astype(jnp.bfloat16)
+            total = total + mm(grad_scores, heads_k[head])
+            grad_key[...] += mm_left(grad_scores, heads_q[head, rows, :])
+            grad_value[...] += mm_left(chance.astype(jnp.bfloat16), grad_out)
+        grad_query[rows, :] = total * SCORE_SCALE
+
+    loop(attend_back)
+
+    def leave(index, carry):
+        rows = rows_at(index)
+        grad_qkv[rows, 0:INNER] = grad_query[rows, :].astype(jnp.bfloat16)
+        grad_qkv[rows, INNER : 2 * INNER] = grad_key[rows, :].astype(jnp.bfloat16)
+        grad_qkv[rows, 2 * INNER : 3 * INNER] = grad_value[rows, :].astype(jnp.bfloat16)
+        grad_in = mm_right(grad_qkv[rows, :], qkv_ref[...])
+        normed, inverse = row_norm(block[rows, :])
+        gtf_ref[0:1, :] += column_sum(grad_in * normed)
+        gtf_ref[1:2, :] += column_sum(grad_in)
+        grad_state = grad_mid[rows, :] + row_norm_back(
+            grad_in, normed, inverse, tf_rows_ref[0:1, :]
+        )
+        low = grad_state.astype(jnp.bfloat16)
+        grad_skip[rows, :] = low
+        grows_ref[6:7, :] += column_sum(low.astype(jnp.float32))
+        normed = (z_two[rows, :] - mean_two) * inv_two
+        grad_here = (
+            mish_slope(normed * rows_ref[4:5, :] + rows_ref[5:6, :])
+            * tile_mask(index)
+            * grad_state
+        )
+        grad_norm[rows, :] = grad_here
+        return (carry[0] + column_sum(grad_here), carry[1] + column_sum(grad_here * normed))
+
+    zero = jnp.zeros((1, C), jnp.float32)
+
+    def norm_back(target, mean_row, inv_row, gain_at, bias_at, shift_sum, gain_sum):
+        gain_row = rows_ref[gain_at : gain_at + 1, :]
+        grows_ref[gain_at : gain_at + 1, :] += gain_sum
+        grows_ref[gain_at + 1 : gain_at + 2, :] += shift_sum
+        first = group_sum(shift_sum * gain_row) / number
+        second = group_sum(gain_sum * gain_row) / number
+
+        def one(index):
+            rows = rows_at(index)
+            normed = (target[rows, :] - mean_row) * inv_row
+            cells = inv_row * (
+                grad_norm[rows, :] * gain_row - tile_mask(index) * (first + normed * second)
+            )
+            cells = cells.astype(jnp.bfloat16).astype(jnp.float32)
+            grows_ref[bias_at : bias_at + 1, :] += column_sum(cells)
+            pad[rows_at(index, 8), :] = cells
+
+        loop(one)
+        build_columns(col_grad)
+
+    def conv_back(rows, base):
+        total = mm_right(col_grad[rows, 2 * C : 3 * C], convs_ref[base : base + C, :])
+        total = total + mm_right(col_grad[rows, C : 2 * C], convs_ref[base + C : base + 2 * C, :])
+        return total + mm_right(col_grad[rows, 0:C], convs_ref[base + 2 * C : base + 3 * C, :])
+
+    def conv_weights(columns, base):
+        for tap in range(3):
+            gconvs_ref[base + tap * C : base + (tap + 1) * C, :] += mm_left(
+                columns[:, tap * C : (tap + 1) * C], col_grad[:, C : 2 * C]
+            )
+
+    shift_sum, gain_sum = lax.fori_loop(0, tiles, leave, (zero, zero))
+    norm_back(z_two, mean_two, inv_two, 4, 3, shift_sum, gain_sum)
+    conv_weights(col_two, 3 * C)
+
+    def hidden_back(index, carry):
+        rows = rows_at(index)
+        grad_here = conv_back(rows, 3 * C) * tile_mask(index)
+        gtime_ref[0] += column_sum(grad_here)
+        normed = (z_one[rows, :] - mean_one) * inv_one
+        grad_here = mish_slope(normed * rows_ref[1:2, :] + rows_ref[2:3, :]) * grad_here
+        grad_norm[rows, :] = grad_here
+        return (carry[0] + column_sum(grad_here), carry[1] + column_sum(grad_here * normed))
+
+    shift_sum, gain_sum = lax.fori_loop(0, tiles, hidden_back, (zero, zero))
+    grows_ref[7:8, :] += gtime_ref[0]
+    norm_back(z_one, mean_one, inv_one, 1, 0, shift_sum, gain_sum)
+    conv_weights(col_one, 0)
+
+    def finish(index):
+        rows = rows_at(index)
+        total = conv_back(rows, 0) + mm_right(grad_skip[rows, :], res_ref[...])
+        gin_ref[0, rows, :] = (total * tile_mask(index)).astype(jnp.bfloat16)
+
+    loop(finish)
+    gres_ref[...] += mm_left(x_ref[0], grad_skip[...])
+    gqkv_ref[...] += mm_left(attn_in[...], grad_qkv[...])
+
+    @pl.when(utt == pl.num_programs(0) - 1)
+    def scale_rows():
+        low_side = jnp.exp(wide_ref[2:3, :])
+        depth = 1.0 / (low_side + 1e-09)
+        gwide_ref[2:3, :] = -gwide_ref[2:3, :] * low_side * depth * depth
+
+
+def whole_step(lengths, cells, grads, time_proj, weights):
+    (convs, res_weight, rows, qkv_weight, out_weight, up_weight, down_weight, tf_rows, wide) = weights
+    utts, frames, _ = cells.shape
+    by_utt = pl.BlockSpec((1, frames, C), lambda u, s: (u, 0, 0))
+    row_by_utt = pl.BlockSpec((1, 1, C), lambda u, s: (u, 0, 0))
+
+    def fixed(array):
+        return pl.BlockSpec(array.shape, lambda u, s: (0, 0))
+
+    f32, low = jnp.float32, jnp.bfloat16
+    scratch = [
+        ((frames + 16, C), f32),
+        ((frames, 3 * C), low),
+        ((frames, 3 * C), low),
+        ((frames, 3 * C), low),
+        ((frames, C), f32),
+        ((frames, C), f32),
+        ((frames, C), f32),
+        ((frames, C), f32),
+        ((frames, C), f32),
+        ((frames, C), low),
+        ((HEADS, frames, INNER), low),
+        ((HEADS, frames, INNER), low),
+        ((HEADS, frames, INNER), low),
+        ((HEADS, frames, INNER), low),
+        ((frames, INNER), low),
+        ((HEADS, frames, frames), f32),
+        ((frames, F), low),
+        ((frames, F), low),
+        ((frames, C), low),
+        ((frames, C), low),
+        ((frames, INNER), f32),
+        ((frames, INNER), f32),
+        ((frames, INNER), f32),
+        ((frames, 3 * INNER), low),
+        ((frames, C), low),
+    ]
+    return pl.pallas_call(
+        step_kernel,
+        grid_spec=pltpu.PrefetchScalarGridSpec(
+            num_scalar_prefetch=1,
+            grid=(utts,),
+            in_specs=[by_utt, by_utt, row_by_utt] + [fixed(array) for array in weights],
+            out_specs=[by_utt, by_utt, row_by_utt] + [fixed(array) for array in weights],
+            scratch_shapes=[pltpu.VMEM(shape, kind) for shape, kind in scratch],
+        ),
+        out_shape=[
+            jax.ShapeDtypeStruct(cells.shape, low),
+            jax.ShapeDtypeStruct(cells.shape, low),
+            jax.ShapeDtypeStruct((utts, 1, C), f32),
+        ]
+        + [jax.ShapeDtypeStruct(array.shape, f32) for array in weights],
+        compiler_params=pltpu.CompilerParams(
+            dimension_semantics=("arbitrary",), vmem_limit_bytes=60 * 1024 * 1024
+        ),
+    )(lengths, cells, grads, time_proj, *weights)
+
+
 def per_device(
     inputs,
     encoded,
@@ -495,170 +981,36 @@
         tf_small,
         wide_small,
     ) = assemble_weights(places, shard_lengths, *gathered)
-    conv_one = convs[: 3 * C].reshape(3, C, C)
-    conv_two = convs[3 * C :].reshape(3, C, C)
     masked_in = to_utts((start_state * local_mask).astype(jnp.bfloat16))
     grad_ff = to_utts((cotangent * local_mask).astype(jnp.bfloat16))
     lengths = lax.dynamic_slice_in_dim(lengths, seq_index * utt_count, utt_count)
     time_embed = lax.dynamic_slice_in_dim(time_embed, seq_index * utt_count, utt_count)
-    frame_mask = (jnp.arange(key_total)[None, :] < lengths[:, None]).astype(jnp.float32)
-    wide_mask = frame_mask[:, :, None]
-    key_mask = jnp.arange(key_total, dtype=jnp.int32)[None, :] < lengths[:, None]
-    valid_count = lengths.astype(jnp.float32)
-    padded_one = rim_pad(masked_in)
-    z_one = conv_apply(padded_one, conv_one) + res_small[0]
-    norm_one, normed_one, inv_one = norm_forward(
-        z_one, frame_mask, valid_count, res_small[1], res_small[2]
-    )
-    act_one = mish_fn(norm_one) * wide_mask
     time_act = mish_fn(time_embed).astype(jnp.bfloat16)
     time_proj = jnp.dot(time_act, time_weight, preferred_element_type=jnp.float32) + res_small[7]
-    masked_two = ((act_one + time_proj[:, None, :]) * wide_mask).astype(jnp.bfloat16)
-    padded_two = rim_pad(masked_two)
-    z_two = conv_apply(padded_two, conv_two) + res_small[3]
-    norm_two, normed_two, inv_two = norm_forward(
-        z_two, frame_mask, valid_count, res_small[4], res_small[5]
-    )
-    act_two = mish_fn(norm_two) * wide_mask
-    skip_out = jnp.dot(masked_in, res_weight, preferred_element_type=jnp.float32) + res_small[6]
-    block_out = act_two + skip_out
-    attn_in = layer_norm(block_out, tf_small[0], tf_small[1]).astype(jnp.bfloat16)
-    qkv_all = jnp.dot(attn_in, qkv_weight, preferred_element_type=jnp.float32).astype(jnp.bfloat16)
-    queries = qkv_all[:, :, :inner].reshape(utt_count, key_total, HEADS, HD)
-    kv_whole = qkv_all[:, :, inner:]
-    keys = kv_whole[:, :, :inner].reshape(utt_count, key_total, HEADS, HD)
-    values = kv_whole[:, :, inner:].reshape(utt_count, key_total, HEADS, HD)
-    scores = (
-        jnp.einsum("uqhd,ukhd->uhqk", queries, keys, preferred_element_type=jnp.float32)
-        * SCORE_SCALE
-    )
-    scores = jnp.where(key_mask[:, None, None, :], scores, MASK_FILL)
-    top_score = jnp.max(scores, axis=-1, keepdims=True)
-    expo = jnp.exp(scores - top_score)
-    row_total = jnp.sum(expo, axis=-1, keepdims=True)
-    log_total = top_score + jnp.log(row_total)
-    probs_low = (expo / row_total).astype(jnp.bfloat16)
-    attn_vals = jnp.einsum("uhqk,ukhd->uqhd", probs_low, values, preferred_element_type=jnp.float32)
-    attn_vals = attn_vals.reshape(utt_count, key_total, inner).astype(jnp.bfloat16)
-    attn_out = jnp.dot(attn_vals, out_weight, preferred_element_type=jnp.float32) + tf_small[2]
-    mid_state = block_out + attn_out
-    ff_in = layer_norm(mid_state, tf_small[3], tf_small[4]).astype(jnp.bfloat16)
-    up_out = jnp.dot(ff_in, up_weight, preferred_element_type=jnp.float32) + wide_small[0]
-    snake_out = snake_fn(up_out, wide_small[1], wide_small[2]).astype(jnp.bfloat16)
-    ff_out = jnp.dot(snake_out, down_weight, preferred_element_type=jnp.float32) + tf_small[5]
-    final = (mid_state + ff_out) * wide_mask
-    grad_final = grad_ff.astype(jnp.float32)
-    grad_down_w = jnp.einsum("utf,utc->fc", snake_out, grad_ff, preferred_element_type=jnp.float32)
-    grad_down_b = jnp.sum(grad_ff, axis=(0, 1), dtype=jnp.float32)
-    grad_snake = jnp.einsum("utc,fc->utf", grad_ff, down_weight, preferred_element_type=jnp.float32)
-    snake_value, snake_pull = jax.vjp(snake_fn, up_out, wide_small[1], wide_small[2])
-    grad_up_f, grad_alpha, grad_beta = snake_pull(grad_snake)
-    grad_up = grad_up_f.astype(jnp.bfloat16)
-    grad_up_w = jnp.einsum("utc,utf->cf", ff_in, grad_up, preferred_element_type=jnp.float32)
-    grad_up_b = jnp.sum(grad_up, axis=(0, 1), dtype=jnp.float32)
-    grad_ff_in = jnp.einsum("utf,cf->utc", grad_up, up_weight, preferred_element_type=jnp.float32)
-    norm_value, norm_pull = jax.vjp(layer_norm, mid_state, tf_small[3], tf_small[4])
-    grad_mid_ln, grad_ln3_g, grad_ln3_b = norm_pull(grad_ff_in)
-    grad_mid = grad_final + grad_mid_ln
-    grad_attn = grad_mid.astype(jnp.bfloat16)
-    grad_out_w = jnp.einsum("uti,utc->ic", attn_vals, grad_attn, preferred_element_type=jnp.float32)
-    grad_out_b = jnp.sum(grad_attn, axis=(0, 1), dtype=jnp.float32)
-    grad_vals = jnp.einsum("utc,ic->uti", grad_attn, out_weight, preferred_element_type=jnp.float32)
-    grad_vals = grad_vals.astype(jnp.bfloat16).reshape(utt_count, key_total, HEADS, HD)
-    scores = (
-        jnp.einsum("uqhd,ukhd->uhqk", queries, keys, preferred_element_type=jnp.float32)
-        * SCORE_SCALE
-    )
-    scores = jnp.where(key_mask[:, None, None, :], scores, MASK_FILL)
-    probs = jnp.exp(scores - log_total)
-    probs_low = probs.astype(jnp.bfloat16)
-    grad_probs = jnp.einsum(
-        "uqhd,ukhd->uhqk", grad_vals, values, preferred_element_type=jnp.float32
-    )
-    row_dot = jnp.sum(probs * grad_probs, axis=-1, keepdims=True)
-    grad_scores = (probs * (grad_probs - row_dot)).astype(jnp.bfloat16)
-    grad_query = (
-        jnp.einsum("uhqk,ukhd->uqhd", grad_scores, keys, preferred_element_type=jnp.float32)
-        * SCORE_SCALE
-    )
-    grad_key = (
-        jnp.einsum("uhqk,uqhd->ukhd", grad_scores, queries, preferred_element_type=jnp.float32)
-        * SCORE_SCALE
-    )
-    grad_value = jnp.einsum(
-        "uhqk,uqhd->ukhd", probs_low, grad_vals, preferred_element_type=jnp.float32
-    )
-    grad_kv = jnp.concatenate(
-        [
-            grad_key.reshape(utt_count, key_total, inner),
-            grad_value.reshape(utt_count, key_total, inner),
-        ],
-        axis=2,
-    )
-    grad_kv_local = grad_kv
-    grad_qkv = jnp.concatenate(
-        [grad_query.reshape(utt_count, key_total, inner), grad_kv_local], axis=2
-    ).astype(jnp.bfloat16)
-    grad_qkv_w = jnp.einsum("utc,utd->cd", attn_in, grad_qkv, preferred_element_type=jnp.float32)
-    grad_attn_in = jnp.einsum(
-        "utd,cd->utc", grad_qkv, qkv_weight, preferred_element_type=jnp.float32
-    )
-    block_value, block_pull = jax.vjp(layer_norm, block_out, tf_small[0], tf_small[1])
-    grad_block_ln, grad_ln1_g, grad_ln1_b = block_pull(grad_attn_in)
-    grad_block = grad_mid + grad_block_ln
-    grad_skip = grad_block.astype(jnp.bfloat16)
-    grad_res_w = jnp.einsum("utc,utd->cd", masked_in, grad_skip, preferred_element_type=jnp.float32)
-    grad_res_b = jnp.sum(grad_skip, axis=(0, 1), dtype=jnp.float32)
-    grad_masked_in = jnp.einsum(
-        "utd,cd->utc", grad_skip, res_weight, preferred_element_type=jnp.float32
-    )
-    mish_two, mish_pull_two = jax.vjp(mish_fn, norm_two)
-    (grad_norm_two,) = mish_pull_two(grad_block * wide_mask)
-    grad_z_two, grad_gn2_g, grad_gn2_b = norm_backward(
-        grad_norm_two, normed_two, inv_two, frame_mask, valid_count, res_small[4]
-    )
-    grad_z_two = grad_z_two.astype(jnp.bfloat16)
-    grad_conv_two = conv_weight_grad(padded_two, grad_z_two)
-    grad_conv_two_b = jnp.sum(grad_z_two, axis=(0, 1), dtype=jnp.float32)
-    grad_hidden = conv_input_grad(grad_z_two, conv_two) * wide_mask
-    grad_time_proj = jnp.sum(grad_hidden, axis=1)
+    weights = (
+        convs,
+        res_weight,
+        res_small,
+        qkv_weight,
+        out_weight,
+        up_weight,
+        down_weight,
+        tf_small,
+        wide_small,
+    )
+    (
+        final,
+        grad_inputs,
+        grad_time_proj,
+        grad_convs,
+        grad_res_w,
+        grad_rows,
+        *tf_grads,
+    ) = whole_step(lengths, masked_in, grad_ff, time_proj[:, None, :], weights)
     grad_time_w = jnp.dot(
-        time_act.astype(jnp.float32).T, grad_time_proj, precision=lax.Precision.HIGHEST
-    )
-    grad_time_b = jnp.sum(grad_time_proj, axis=0)
-    mish_one, mish_pull_one = jax.vjp(mish_fn, norm_one)
-    (grad_norm_one,) = mish_pull_one(grad_hidden * wide_mask)
-    grad_z_one, grad_gn1_g, grad_gn1_b = norm_backward(
-        grad_norm_one, normed_one, inv_one, frame_mask, valid_count, res_small[1]
-    )
-    grad_z_one = grad_z_one.astype(jnp.bfloat16)
-    grad_conv_one = conv_weight_grad(padded_one, grad_z_one)
-    grad_conv_one_b = jnp.sum(grad_z_one, axis=(0, 1), dtype=jnp.float32)
-    grad_masked_in = grad_masked_in + conv_input_grad(grad_z_one, conv_one)
-    grad_inputs = grad_masked_in * wide_mask
-    grads = (
-        jnp.concatenate([grad_conv_one.reshape(-1, C), grad_conv_two.reshape(-1, C)]),
-        grad_res_w,
-        grad_time_w,
-        jnp.stack(
-            [
-                grad_conv_one_b,
-                grad_gn1_g,
-                grad_gn1_b,
-                grad_conv_two_b,
-                grad_gn2_g,
-                grad_gn2_b,
-                grad_res_b,
-                grad_time_b,
-            ]
-        ),
-        grad_qkv_w,
-        grad_out_w,
-        grad_up_w,
-        grad_down_w,
-        jnp.stack([grad_ln1_g, grad_ln1_b, grad_out_b, grad_ln3_g, grad_ln3_b, grad_down_b]),
-        jnp.stack([grad_up_b, grad_alpha, grad_beta]),
-    )
+        time_act.astype(jnp.float32).T, grad_time_proj[:, 0], precision=lax.Precision.HIGHEST
+    )
+    grads = (grad_convs, grad_res_w, grad_time_w, grad_rows, *tf_grads)
     summed = reduce_windows(orders, *cut_grads(places, shard_lengths, window_sizes, grads))
     res_share = from_window(summed[0], shard_lengths[0], owner)
     tf_share = from_window(summed[1], shard_lengths[1], owner)

time: 337 us -> 248 us (0.74); the launches traced: 332 us -> 247 us
  matrix products: 120 us -> 2.42 us
  Pallas kernels: 70.7 us -> 158 us
  other arithmetic: 55.2 us -> 11.5 us
  blocking collectives: 0 us -> 18.6 us
  local copies, waits for them, and re-layouts: 48.3 us -> 33.6 us
  waiting for transfers between devices: 18.8 us -> 10.3 us
  starting transfers between devices: 17 us -> 11.4 us
    dot_general x40 -> x1, matrix products: 119 us -> 1.41 us  [per_device(): jnp.dot(time_act.astype(jnp.float32).T, grad_time_proj[:, 0], precision=l...]
    pallas_call x0 -> x1, Pallas kernels: none -> 89.6 us  [whole_step(): pl.pallas_call(step_kernel, grid_spec=pltpu.PrefetchScalarGridSpec(num_sc...]
    reduce_sum x19 -> x0, other arithmetic: 27 us -> none  [the longest x1 5.19 us: norm_backward(): grad_gain = jnp.sum(grad_out * normed, axis=(0, 1))]
    all_to_all x0 -> x1, blocking collectives: none -> 18.6 us  [to_utts(): return lax.all_to_all(cells, 'seq', split_axis=0, concat_axis=1, tiled=True)]
    convert_element_type x2 -> x0, other arithmetic: 15.6 us -> none  [the longest x1 12.4 us: per_device(): grad_scores = (probs * (grad_probs - row_dot)).astype(jnp.bfloat16)]
    all_to_all x2 -> x1, waiting for transfers between devices: 8.5 us -> 0.01 us  [to_utts(): return lax.all_to_all(cells, 'seq', split_axis=0, concat_axis=1, tiled=True)]
    pallas_call x0 -> x2, local copies, waits for them, and re-layouts: none -> 5.33 us  [whole_step(): pl.pallas_call(step_kernel, grid_spec=pltpu.PrefetchScalarGridSpec(num_sc...]
    all_to_all x2 -> x1, starting transfers between devices: 8.84 us -> 3.52 us  [to_utts(): return lax.all_to_all(cells, 'seq', split_axis=0, concat_axis=1, tiled=True)]
  transfers between devices with their start and end apart: 4 -> 3, of which waited for: 2 -> 1; matrix products, arithmetic and copies ran while one was open for 7% -> 6% of each run, Pallas kernels for 21% -> 28%
where the time goes in v3:
time: 248 us; the launch traced here: 247 us
  Pallas kernels  158 us (64%)
  local copies, waits for them, and re-layouts  33.6 us (14%)
  blocking collectives  18.6 us (8%)
  other arithmetic  11.5 us (5%)
  starting transfers between devices  11.4 us (5%)
  waiting for transfers between devices  10.3 us (4%)
    pallas_call x1, Pallas kernels, whole_step(): pl.pallas_call(step_kernel, grid_spec=pltpu.PrefetchScalarGridSpec(num_sc...  89.6 us
    pallas_call x1, Pallas kernels, reduce_windows(): pl.pallas_call(functools.partial(reduce_kernel, orders), out_shape=(jax.S...  33.4 us
    pallas_call x1, Pallas kernels, gather_windows(): pl.pallas_call(functools.partial(gather_kernel, orders), out_shape=(jax.S...  33 us
    all_to_all x1, blocking collectives, to_utts(): return lax.all_to_all(cells, 'seq', split_axis=0, concat_axis=1, tiled=True)  18.6 us
    gather x1, local copies, waits for them, and re-layouts, take_rows(): return phone_table[phone_rows]  14.1 us
    all_to_all x2, waiting for transfers between devices, to_frames(): lax.all_to_all(low, 'seq', split_axis=1, concat_axis=0, tiled=True)  10.3 us
    all_to_all x2, starting transfers between devices, to_frames(): lax.all_to_all(low, 'seq', split_axis=1, concat_axis=0, tiled=True)  7.91 us
    unnamed x63, local copies, waits for them, and re-layouts  6.8 us
  transfers between devices with their start and end apart: 3, of which 1 were waited for; matrix products, arithmetic and copies ran while one was open for 6% of the time, Pallas kernels for 28%

profile of v3, /device:TPU:0, one launch (start us, length us, event | category | flops | bytes accessed | tf_op | source)
XLA Modules:
  0.0 247.0 jit_solution(8747083045752697726)
XLA Ops:
  0.7 1.1 reduce_window_sum.11
  2.2 0.7 compare_convert_fusion
  2.9 14.1 %gather_fusion = f32[2048,256]{1,0:T(8,128)S(1)} fusion(f32[8,128,256]{2,1,0:T(8,128)S(1)} %copy-done, s32[2048]{0:T(1024)S(1)} %bitcast.38), kind=kCustom, calls=%fused_computation | custom fusion | bytes 4210688 | tf_op jit(solution)/shard_map/vmap()/gather | solution.py:46
  17.0 3.7 %multiply_convert_fusion = (bf16[8,256,256]{2,1,0:T(8,128)(2,1)S(1)}, bf16[8,256,256]{2,1,0:T(8,128)(2,1)}) fusion(f32[8,256,256]{2,1,0:T(8,128)} %param.17, f32[8,256]{1,0:T(8,128)S(1)} %compare_convert_fusion, f32[8,256,256]{2,1,0:T(8,128)} %param.12, f32[8,256,256]{2,1,0:T(8,128)S(1)} %bitcast.39), kind=kLoop, calls=%fused_computation.3 | loop fusion | flops 2621440 | bytes 8396800 | tf_op jit(solution)/shard_map/convert_element_type | solution.py:985
  20.7 18.6 %all_to_all.54 = bf16[8,256,256]{2,1,0:T(8,128)(2,1)S(1)} all-to-all(bf16[8,256,256]{2,1,0:T(8,128)(2,1)S(1)} %get-tuple-element.76), channel_id=1, replica_groups=mesh['dp'=8,'seq'=4] {'seq'}, dimensions={0} | all-to-all | bytes 2097152 | tf_op jit(solution)/shard_map/all_to_all | solution.py:441
  39.3 3.5 %all-to-all-start = ((bf16[8,256,256]{2,1,0:T(8,128)(2,1)}), bf16[8,256,256]{2,1,0:T(8,128)(2,1)S(1)}, u32[]{:S(2)}, u32[]{:S(2)}) async-start(bf16[8,256,256]{2,1,0:T(8,128)(2,1)} %get-tuple-element.77), calls=%async_computation | async-start | bytes 2097152 | tf_op jit(solution)/shard_map/all_to_all | solution.py:441
  44.7 33.0 %shard_map.211 = (bf16[32,192,128]{2,1,0:T(8,128)(2,1)S(1)}, bf16[32,176,128]{2,1,0:T(8,128)(2,1)S(1)}) custom-call(bf16[192,128]{1,0:T(8,128)(2,1)S(1)} %bitcast.34, bf16[176,128]{1,0:T(8,128)(2,1)S(1)} %bitcast.35), custom_call_target="tpu_custom_call" | custom-call | tf_op jit(solution)/shard_map/pallas_call | solution.py:231
  77.8 1.1 shard_map.212
  78.9 0.9 copy-done.4
  79.7 0.8 copy-done.6
  80.5 0.7 copy-done.9
  83.1 1.0 convolution_add_fusion
  84.7 1.1 copy.39
  85.8 1.0 copy.38
  86.8 89.6 %shard_map.213 = (bf16[2,1024,256]{2,1,0:T(8,128)(2,1)}, bf16[2,1024,256]{2,1,0:T(8,128)(2,1)}, f32[2,1,256]{2,1,0:T(1,128)}, f32[1536,256]{1,0:T(8,128)}, f32[2...) custom-call(s32[2]{0:T(128)} %dynamic_slice.12.lengths_ref, ...), custom_call_target="tpu_custom_call" | custom-call | tf_op jit(solution)/shard_map/pallas_call | solution.py:914
  176.5 3.3 %copy.40 = bf16[2,1024,256]{2,0,1:T(2,128)(2,1)} copy(bf16[2,1024,256]{2,1,0:T(8,128)(2,1)} %get-tuple-element.52) | data formatting | bytes 2097152 | tf_op jit(solution)/shard_map/pallas_call | solution.py:914
  179.8 4.4 %all-to-all-start.2 = ((bf16[2,1024,256]{2,0,1:T(2,128)(2,1)}), bf16[2,1024,256]{2,0,1:T(2,128)(2,1)}, u32[]{:S(2)}, u32[]{:S(2)}) async-start(bf16[2,1024,256]{2,0,1:T(2,128)(2,1)} %copy.40), calls=%async_computation.2 | async-start | bytes 2097152 | tf_op jit(solution)/shard_map/all_to_all | solution.py:446
  184.2 1.4 fusion.4.refs_2_
  185.7 1.2 copy-done.2
  186.9 1.2 copy-done.3
  188.1 0.9 shard_map.214
  189.1 33.4 %shard_map.215 = (f32[192,128]{1,0:T(8,128)S(1)}, f32[176,128]{1,0:T(8,128)S(1)}) custom-call(bf16[32,192,128]{2,1,0:T(8,128)(2,1)S(1)} %get-tuple-element.64.in_a, bf16[32,176,128]{2,1,0:T(8,128)(2,1)S(1)} %get-tuple-element.65.in_b), custom_call_target="tpu_custom_call" | custom-call | tf_op jit(solution)/shard_map/pallas_call | solution.py:304
  222.5 0.8 fusion.7
  223.9 2.0 copy.42
  226.0 0.8 fusion.8
  226.8 3.5 %all-to-all-start.3 = ((bf16[2,1024,256]{2,0,1:T(2,128)(2,1)}), bf16[2,1024,256]{2,0,1:T(2,128)(2,1)S(1)}, u32[]{:S(2)}, u32[]{:S(2)}) async-start(bf16[2,1024,256]{2,0,1:T(2,128)(2,1)} %copy.42), calls=%async_computation.3 | async-start | bytes 2097152 | tf_op jit(solution)/shard_map/all_to_all | solution.py:446
  230.3 0.7 multiply_add_fusion
  231.0 1.9 convert_bitcast_fusion.1
  232.9 1.5 copy.41
  234.5 10.2 %all-to-all-done.3 = bf16[2,1024,256]{2,0,1:T(2,128)(2,1)S(1)} async-done(((bf16[2,1024,256]{2,0,1:T(2,128)(2,1)}), bf16[2,1024,256]{2,0,1:T(2,128)(2,1)S(1)}, u32[]{:S(2)}, u32[]{:S(2)}) %all-to-all-start.3) | async-done | bytes 1048608 | tf_op jit(solution)/shard_map/all_to_all | solution.py:446
  244.7 0.7 convert_bitcast_fusion
  245.4 1.5 copy.43
  (73 shorter events, 5.4 us)
Async XLA Ops:
  0.6 2.3 copy-start
  20.7 22.2 %copy-start.30 = (s32[8]{0:T(128)S(1)}, s32[8]{0:T(128)}, u32[]{:S(2)}) copy-start(s32[8]{0:T(128)} %param.15) | copy-start | bytes 100
  20.7 22.8 %copy-start.22 = (f32[20624]{0:T(1024)S(1)}, f32[20624]{0:T(1024)}, u32[]{:S(2)}) copy-start(f32[20624]{0:T(1024)} %param.21) | copy-start | bytes 247492
  20.7 22.8 %copy-start.20 = (f32[22592]{0:T(1024)S(1)}, f32[22592]{0:T(1024)}, u32[]{:S(2)}) copy-start(f32[22592]{0:T(1024)} %param.18) | copy-start | bytes 271108
  39.3 46.4 %all-to-all-start = ((bf16[8,256,256]{2,1,0:T(8,128)(2,1)}), bf16[8,256,256]{2,1,0:T(8,128)(2,1)S(1)}, u32[]{:S(2)}, u32[]{:S(2)}) async-start(bf16[8,256,256]{2,1,0:T(8,128)(2,1)} %get-tuple-element.77), calls=%async_computation | async-start | bytes 2097152 | tf_op jit(solution)/shard_map/all_to_all | solution.py:441
  78.8 0.9 copy-start.4
  79.7 0.8 copy-start.6
  80.5 0.7 copy-start.9
  81.2 0.6 copy-start.10
  83.1 1.0 copy-start.5
  83.1 1.6 copy-start.13
  83.1 3.7 %copy-start.15 = (f32[8,256]{1,0:T(8,128)}, f32[8,256]{1,0:T(8,128)S(1)}, u32[]{:S(2)}) copy-start(f32[8,256]{1,0:T(8,128)S(1)} %get-tuple-element.43.rows_ref) | copy-start | bytes 24580
  176.5 7.7 %copy-start.29 = (f32[2,1,256]{2,1,0:T(1,128)S(1)}, f32[2,1,256]{2,1,0:T(1,128)}, u32[]{:S(2)}) copy-start(f32[2,1,256]{2,1,0:T(1,128)} %get-tuple-element.56) | copy-start | bytes 6148
  179.8 5.9 %copy-start.1 = (f32[1536,256]{1,0:T(8,128)S(1)}, f32[1536,256]{1,0:T(8,128)}, u32[]{:S(2)}) copy-start(f32[1536,256]{1,0:T(8,128)} %get-tuple-element.54.refs_0_) | copy-start | bytes 4718596
  179.8 5.9 %copy-start.7 = (f32[256,384]{1,0:T(8,128)S(1)}, f32[256,384]{1,0:T(8,128)}, u32[]{:S(2)}) copy-start(f32[256,384]{1,0:T(8,128)} %get-tuple-element.58.refs_4_) | copy-start | bytes 1179652
  179.8 5.9 %copy-start.8 = (f32[256,256]{1,0:T(8,128)S(1)}, f32[256,256]{1,0:T(8,128)}, u32[]{:S(2)}) copy-start(f32[256,256]{1,0:T(8,128)} %get-tuple-element.55.refs_1_) | copy-start | bytes 786436
  179.8 5.9 %copy-start.11 = (f32[128,256]{1,0:T(8,128)S(1)}, f32[128,256]{1,0:T(8,128)}, u32[]{:S(2)}) copy-start(f32[128,256]{1,0:T(8,128)} %get-tuple-element.59.refs_5_) | copy-start | bytes 393220
  179.8 5.9 %copy-start.14 = (f32[3,1024]{1,0:T(4,128)S(1)}, f32[3,1024]{1,0:T(4,128)}, u32[]{:S(2)}) copy-start(f32[3,1024]{1,0:T(4,128)} %get-tuple-element.63.refs_9_) | copy-start | bytes 36868
  179.8 5.9 %copy-start.17 = (f32[8,256]{1,0:T(8,128)S(1)}, f32[8,256]{1,0:T(8,128)}, u32[]{:S(2)}) copy-start(f32[8,256]{1,0:T(8,128)} %get-tuple-element.57.refs_3_) | copy-start | bytes 24580
  179.8 5.9 %copy-start.18 = (f32[6,256]{1,0:T(8,128)S(1)}, f32[6,256]{1,0:T(8,128)}, u32[]{:S(2)}) copy-start(f32[6,256]{1,0:T(8,128)} %get-tuple-element.62.refs_8_) | copy-start | bytes 18436
  179.8 47.0 %all-to-all-start.2 = ((bf16[2,1024,256]{2,0,1:T(2,128)(2,1)}), bf16[2,1024,256]{2,0,1:T(2,128)(2,1)}, u32[]{:S(2)}, u32[]{:S(2)}) async-start(bf16[2,1024,256]{2,0,1:T(2,128)(2,1)} %copy.40), calls=%async_computation.2 | async-start | bytes 2097152 | tf_op jit(solution)/shard_map/all_to_all | solution.py:446
  185.7 1.2 copy-start.2
  186.9 1.2 copy-start.3
  189.0 33.5 %copy-start.23 = (f32[20624]{0:T(1024)S(1)}, f32[20624]{0:T(1024)}, u32[]{:S(2)}) copy-start(f32[20624]{0:T(1024)} %param.21) | copy-start | bytes 247492
  189.0 33.5 %copy-start.27 = (f32[20624]{0:T(1024)S(1)}, f32[20624]{0:T(1024)}, u32[]{:S(2)}) copy-start(f32[20624]{0:T(1024)} %param.22) | copy-start | bytes 247492
  189.0 34.2 %copy-start.28 = (f32[20624]{0:T(1024)S(1)}, f32[20624]{0:T(1024)}, u32[]{:S(2)}) copy-start(f32[20624]{0:T(1024)} %param.23) | copy-start | bytes 247492
  189.0 34.9 %copy-start.19 = (bf16[2,1024,256]{2,1,0:T(8,128)(2,1)S(1)}, bf16[2,1024,256]{2,1,0:T(8,128)(2,1)}, u32[]{:S(2)}) copy-start(bf16[2,1024,256]{2,1,0:T(8,128)(2,1)} %get-tuple-element.53) | copy-start | bytes 3145732
  222.5 3.5 %copy-start.26 = (f32[22592]{0:T(1024)S(1)}, f32[22592]{0:T(1024)}, u32[]{:S(2)}) copy-start(f32[22592]{0:T(1024)} %param.19) | copy-start | bytes 271108
  223.3 3.5 %copy-start.24 = (f32[20624]{0:T(1024)}, f32[20624]{0:T(1024)S(1)}, u32[]{:S(2)}) copy-start(f32[20624]{0:T(1024)S(1)} %get-tuple-element.69) | copy-start | bytes 247492
  223.9 6.4 %copy-start.25 = (f32[22592]{0:T(1024)S(1)}, f32[22592]{0:T(1024)}, u32[]{:S(2)}) copy-start(f32[22592]{0:T(1024)} %param.20) | copy-start | bytes 271108
  226.8 6.2 %copy-start.21 = (f32[22592]{0:T(1024)}, f32[22592]{0:T(1024)S(1)}, u32[]{:S(2)}) copy-start(f32[22592]{0:T(1024)S(1)} %get-tuple-element.73) | copy-start | bytes 271108
  226.8 17.9 %all-to-all-start.3 = ((bf16[2,1024,256]{2,0,1:T(2,128)(2,1)}), bf16[2,1024,256]{2,0,1:T(2,128)(2,1)S(1)}, u32[]{:S(2)}, u32[]{:S(2)}) async-start(bf16[2,1024,256]{2,0,1:T(2,128)(2,1)} %copy.42), calls=%async_computation.3 | async-start | bytes 2097152 | tf_op jit(solution)/shard_map/all_to_all | solution.py:446
  (2 other events, 1.2 us)

commit v4 on v3

--- a/solution.py
+++ b/solution.py
@@ -437,13 +437,8 @@
     return lax.dynamic_slice(window.reshape(-1), (lead,), (length_now,))
 
 
-def to_utts(cells):
-    return lax.all_to_all(cells, "seq", split_axis=0, concat_axis=1, tiled=True)
-
-
-def to_frames(cells):
-    low = cells.astype(jnp.bfloat16)
-    return lax.all_to_all(low, "seq", split_axis=1, concat_axis=0, tiled=True).astype(jnp.float32)
+def exchange(cells):
+    return lax.all_to_all(cells, "seq", split_axis=0, concat_axis=0)
 
 
 SIN_TERMS = (
@@ -463,7 +458,6 @@
 )
 PI_PARTS = (3.140625, 0.0009670257568359375, 6.27832957178498e-07)
 ROUND_SHIFT = 12582912.0
-TILE = 256
 
 
 def mm(left, right):
@@ -530,8 +524,7 @@
 
 def step_kernel(
     lengths_ref,
-    x_ref,
-    g_ref,
+    cells_ref,
     time_ref,
     convs_ref,
     res_ref,
@@ -542,8 +535,7 @@
     down_ref,
     tf_rows_ref,
     wide_ref,
-    final_ref,
-    gin_ref,
+    results_ref,
     gtime_ref,
     gconvs_ref,
     gres_ref,
@@ -581,7 +573,7 @@
     grad_skip,
 ):
     frames = z_one.shape[0]
-    tiles = frames // TILE
+    tiles, _, tile, _ = cells_ref.shape
     utt = pl.program_id(0)
     length_now = lengths_ref[utt]
     number = length_now.astype(jnp.float32) * (C // GROUPS)
@@ -615,10 +607,10 @@
     )
 
     def rows_at(index, lead=0):
-        return pl.ds(pl.multiple_of(index * TILE + lead, 8), TILE)
+        return pl.ds(pl.multiple_of(index * tile + lead, 8), tile)
 
     def tile_mask(index):
-        ids = lax.broadcasted_iota(jnp.int32, (TILE, 1), 0) + index * TILE
+        ids = lax.broadcasted_iota(jnp.int32, (tile, 1), 0) + index * tile
         return (ids < length_now).astype(jnp.float32)
 
     def group_sum(row):
@@ -632,10 +624,10 @@
 
     def build_columns(target):
         for index in range(tiles):
-            start = index * TILE
+            start = index * tile
             for tap in range(3):
-                piece = pad[start + 7 + tap : start + 7 + tap + TILE, :]
-                target[start : start + TILE, tap * C : (tap + 1) * C] = piece.astype(jnp.bfloat16)
+                piece = pad[start + 7 + tap : start + 7 + tap + tile, :]
+                target[start : start + tile, tap * C : (tap + 1) * C] = piece.astype(jnp.bfloat16)
 
     def loop(body):
         def wrapped(index, carry):
@@ -660,7 +652,7 @@
         return (mean_row, inv_row)
 
     def copy_in(index):
-        pad[rows_at(index, 8), :] = x_ref[0, rows_at(index), :].astype(jnp.float32)
+        pad[rows_at(index, 8), :] = cells_ref[index, 0, :, 0:C].astype(jnp.float32)
 
     loop(copy_in)
     build_columns(col_one)
@@ -679,7 +671,7 @@
         rows = rows_at(index)
         normed = (z_two[rows, :] - mean_two) * inv_two
         act = mish_value(normed * rows_ref[4:5, :] + rows_ref[5:6, :]) * tile_mask(index)
-        state = act + mm(x_ref[0, rows, :], res_ref[...]) + rows_ref[6:7, :]
+        state = act + mm(cells_ref[index, 0, :, 0:C], res_ref[...]) + rows_ref[6:7, :]
         block[rows, :] = state
         normed, _ = row_norm(state)
         low = (normed * tf_rows_ref[0:1, :] + tf_rows_ref[1:2, :]).astype(jnp.bfloat16)
@@ -699,7 +691,7 @@
 
     def attend(index):
         rows = rows_at(index)
-        total = jnp.zeros((TILE, INNER), jnp.float32)
+        total = jnp.zeros((tile, INNER), jnp.float32)
         for head in range(HEADS):
             scores = mm_right(heads_q[head, rows, :], heads_k[head]) + key_bias
             expo = jnp.exp(scores - jnp.max(scores, axis=-1, keepdims=True))
@@ -716,9 +708,9 @@
         normed, inverse = row_norm(mid)
         low = (normed * tf_rows_ref[3:4, :] + tf_rows_ref[4:5, :]).astype(jnp.bfloat16)
         ff_in[rows, :] = low
-        grad_low = g_ref[0, rows, :]
-        result = jnp.zeros((TILE, C), jnp.float32)
-        grad_in = jnp.zeros((TILE, C), jnp.float32)
+        grad_low = cells_ref[index, 0, :, C : 2 * C]
+        result = jnp.zeros((tile, C), jnp.float32)
+        grad_in = jnp.zeros((tile, C), jnp.float32)
         for chunk in range(F // 256):
             lanes = slice(chunk * 256, (chunk + 1) * 256)
             up_out = mm(low, up_ref[:, lanes]) + wide_ref[0:1, lanes]
@@ -738,7 +730,7 @@
             gwide_ref[0:1, lanes] += column_sum(grad_here.astype(jnp.float32))
             gwide_ref[1:2, lanes] += column_sum(slope * angle)
             gwide_ref[2:3, lanes] += column_sum(grad_snake * square)
-        final_ref[0, rows, :] = ((mid + result + tf_rows_ref[5:6, :]) * tile_mask(index)).astype(
+        results_ref[index, 0, :, 0:C] = ((mid + result + tf_rows_ref[5:6, :]) * tile_mask(index)).astype(
             jnp.bfloat16
         )
         grad_wide = grad_low.astype(jnp.float32)
@@ -758,7 +750,8 @@
 
     def feed_weights(index, carry):
         lanes = pl.ds(pl.multiple_of(index * 256, 256), 256)
-        gdown_ref[lanes, :] += mm_left(snake[:, lanes], g_ref[0])
+        grads = cells_ref[:, 0, :, C : 2 * C].reshape(frames, C)
+        gdown_ref[lanes, :] += mm_left(snake[:, lanes], grads)
         gup_ref[:, lanes] += mm_left(ff_in[...], grad_up[:, lanes])
         return carry
 
@@ -769,7 +762,7 @@
 
     def attend_back(index):
         rows = rows_at(index)
-        total = jnp.zeros((TILE, INNER), jnp.float32)
+        total = jnp.zeros((tile, INNER), jnp.float32)
         for head in range(HEADS):
             grad_out = heads_g[head, rows, :]
             chance = probs[head, rows, :]
@@ -861,10 +854,10 @@
     def finish(index):
         rows = rows_at(index)
         total = conv_back(rows, 0) + mm_right(grad_skip[rows, :], res_ref[...])
-        gin_ref[0, rows, :] = (total * tile_mask(index)).astype(jnp.bfloat16)
+        results_ref[index, 0, :, C : 2 * C] = (total * tile_mask(index)).astype(jnp.bfloat16)
 
     loop(finish)
-    gres_ref[...] += mm_left(x_ref[0], grad_skip[...])
+    gres_ref[...] += mm_left(cells_ref[:, 0, :, 0:C].reshape(frames, C), grad_skip[...])
     gqkv_ref[...] += mm_left(attn_in[...], grad_qkv[...])
 
     @pl.when(utt == pl.num_programs(0) - 1)
@@ -874,10 +867,11 @@
         gwide_ref[2:3, :] = -gwide_ref[2:3, :] * low_side * depth * depth
 
 
-def whole_step(lengths, cells, grads, time_proj, weights):
+def whole_step(lengths, cells, time_proj, weights):
     (convs, res_weight, rows, qkv_weight, out_weight, up_weight, down_weight, tf_rows, wide) = weights
-    utts, frames, _ = cells.shape
-    by_utt = pl.BlockSpec((1, frames, C), lambda u, s: (u, 0, 0))
+    tiles, utts, tile, _ = cells.shape
+    frames = tiles * tile
+    by_utt = pl.BlockSpec((tiles, 1, tile, 2 * C), lambda u, s: (0, u, 0, 0))
     row_by_utt = pl.BlockSpec((1, 1, C), lambda u, s: (u, 0, 0))
 
     def fixed(array):
@@ -916,12 +910,11 @@
         grid_spec=pltpu.PrefetchScalarGridSpec(
             num_scalar_prefetch=1,
             grid=(utts,),
-            in_specs=[by_utt, by_utt, row_by_utt] + [fixed(array) for array in weights],
-            out_specs=[by_utt, by_utt, row_by_utt] + [fixed(array) for array in weights],
+            in_specs=[by_utt, row_by_utt] + [fixed(array) for array in weights],
+            out_specs=[by_utt, row_by_utt] + [fixed(array) for array in weights],
             scratch_shapes=[pltpu.VMEM(shape, kind) for shape, kind in scratch],
         ),
         out_shape=[
-            jax.ShapeDtypeStruct(cells.shape, low),
             jax.ShapeDtypeStruct(cells.shape, low),
             jax.ShapeDtypeStruct((utts, 1, C), f32),
         ]
@@ -929,7 +922,62 @@
         compiler_params=pltpu.CompilerParams(
             dimension_semantics=("arbitrary",), vmem_limit_bytes=60 * 1024 * 1024
         ),
-    )(lengths, cells, grads, time_proj, *weights)
+    )(lengths, cells, time_proj, *weights)
+
+
+def prepare_kernel(
+    lengths_ref, place_ref, inputs_ref, encoded_ref, durations_ref, cotangent_ref, out_ref
+):
+    frames, phones = inputs_ref.shape[1], durations_ref.shape[2]
+    first = place_ref[0] * frames
+    durations = durations_ref[0].astype(jnp.float32)
+    before = lax.broadcasted_iota(jnp.int32, (phones, phones), 0)
+    after = lax.broadcasted_iota(jnp.int32, (phones, phones), 1)
+    upper = (before <= after).astype(jnp.bfloat16)
+    wide = jnp.broadcast_to(durations, (16, phones)).astype(jnp.bfloat16)
+    ends = mm(wide, upper)[0:1]
+    starts = ends - durations
+    last = lax.broadcasted_iota(jnp.int32, (1, phones), 1) == phones - 1
+    ends = jnp.where(last, 1e9, ends)
+    ids = lax.broadcasted_iota(jnp.int32, (frames, 1), 0) + first
+    times = ids.astype(jnp.float32)
+    picked = jnp.where((times >= starts) & (times < ends), 1.0, 0.0).astype(jnp.bfloat16)
+    table = encoded_ref[0]
+    high = table.astype(jnp.bfloat16)
+    rest = table - high.astype(jnp.float32)
+    middle = rest.astype(jnp.bfloat16)
+    low = (rest - middle.astype(jnp.float32)).astype(jnp.bfloat16)
+    rows = (mm(picked, high) + mm(picked, middle)) + mm(picked, low)
+    mask = (ids < lengths_ref[pl.program_id(0)]).astype(jnp.float32)
+    out_ref[0, 0, :, 0:C] = ((inputs_ref[0] + rows) * mask).astype(jnp.bfloat16)
+    out_ref[0, 0, :, C : 2 * C] = (cotangent_ref[0] * mask).astype(jnp.bfloat16)
+
+
+def prepare(inputs, encoded, durations, lengths, cotangent):
+    utts, frames, _ = inputs.shape
+    phones = durations.shape[1]
+    seq_size = lax.axis_size("seq")
+    group = utts // seq_size
+    place = jnp.full((1,), lax.axis_index("seq"), jnp.int32)
+    by_utt = lambda u, n, p: (u, 0, 0)
+    return pl.pallas_call(
+        prepare_kernel,
+        grid_spec=pltpu.PrefetchScalarGridSpec(
+            num_scalar_prefetch=2,
+            grid=(utts,),
+            in_specs=[
+                pl.BlockSpec((1, frames, C), by_utt),
+                pl.BlockSpec((1, phones, C), by_utt),
+                pl.BlockSpec((1, 1, phones), by_utt),
+                pl.BlockSpec((1, frames, C), by_utt),
+            ],
+            out_specs=pl.BlockSpec(
+                (1, 1, frames, 2 * C), lambda u, n, p: (u // group, u % group, 0, 0)
+            ),
+        ),
+        out_shape=jax.ShapeDtypeStruct((seq_size, group, frames, 2 * C), jnp.bfloat16),
+        compiler_params=pltpu.CompilerParams(dimension_semantics=("arbitrary",)),
+    )(lengths, place, inputs, encoded, durations[:, None, :], cotangent)
 
 
 def per_device(
@@ -950,14 +998,8 @@
     seq_size = lax.axis_size("seq")
     key_total = local_len * seq_size
     utt_count = utts_here // seq_size
-    inner = HEADS * HD
     seq_index = lax.axis_index("seq")
-    frame_ids = seq_index * local_len + jnp.arange(local_len, dtype=jnp.int32)
-    local_mask = (frame_ids[None, :] < lengths[:, None]).astype(jnp.float32)[:, :, None]
-    boundary = jnp.cumsum(durations, axis=1)
-    phone = jnp.sum((boundary[:, None, :] <= frame_ids[None, :, None]).astype(jnp.int32), axis=2)
-    phone = jnp.minimum(phone, durations.shape[1] - 1)
-    start_state = inputs + jax.vmap(take_rows)(encoded, phone)
+    cells = exchange(prepare(inputs, encoded, durations, lengths, cotangent))
     mesh_sizes = [(name, lax.axis_size(name)) for name in ("dp", "seq")]
     orders = part_orders(mesh_sizes)
     places = place_maps(orders, mesh_sizes)
@@ -981,8 +1023,6 @@
         tf_small,
         wide_small,
     ) = assemble_weights(places, shard_lengths, *gathered)
-    masked_in = to_utts((start_state * local_mask).astype(jnp.bfloat16))
-    grad_ff = to_utts((cotangent * local_mask).astype(jnp.bfloat16))
     lengths = lax.dynamic_slice_in_dim(lengths, seq_index * utt_count, utt_count)
     time_embed = lax.dynamic_slice_in_dim(time_embed, seq_index * utt_count, utt_count)
     time_act = mish_fn(time_embed).astype(jnp.bfloat16)
@@ -999,17 +1039,17 @@
         wide_small,
     )
     (
-        final,
-        grad_inputs,
+        results,
         grad_time_proj,
         grad_convs,
         grad_res_w,
         grad_rows,
         *tf_grads,
-    ) = whole_step(lengths, masked_in, grad_ff, time_proj[:, None, :], weights)
+    ) = whole_step(lengths, cells, time_proj[:, None, :], weights)
     grad_time_w = jnp.dot(
         time_act.astype(jnp.float32).T, grad_time_proj[:, 0], precision=lax.Precision.HIGHEST
     )
+    results = exchange(results).reshape(utts_here, local_len, 2 * C)
     grads = (grad_convs, grad_res_w, grad_time_w, grad_rows, *tf_grads)
     summed = reduce_windows(orders, *cut_grads(places, shard_lengths, window_sizes, grads))
     res_share = from_window(summed[0], shard_lengths[0], owner)
@@ -1023,8 +1063,8 @@
         tf_master, tf_moment, tf_average, tf_share, rate
     )
     return (
-        to_frames(final),
-        to_frames(grad_inputs),
+        results[:, :, :C].astype(jnp.float32),
+        results[:, :, C:].astype(jnp.float32),
         res_share,
         tf_share,
         res_new,

time: 248 us -> 219 us (0.88)
  Pallas kernels: 158 us -> 190 us
  local copies, waits for them, and re-layouts: 33.6 us -> 9.19 us
  blocking collectives: 18.6 us -> 0 us
  waiting for transfers between devices: 10.3 us -> 0.01 us
  other arithmetic: 11.5 us -> 6.9 us
    all_to_all x1 -> x0, blocking collectives: 18.6 us -> none  [to_utts(): return lax.all_to_all(cells, 'seq', split_axis=0, concat_axis=1, tiled=True)]
    pallas_call x1, Pallas kernels: 33.4 us -> 48.9 us  [reduce_windows(): pl.pallas_call(functools.partial(reduce_kernel, orders), out_shape=(jax.S...]
    gather x1 -> x0, local copies, waits for them, and re-layouts: 14.1 us -> none  [take_rows(): return phone_table[phone_rows]]
    all_to_all x3 -> x2, waiting for transfers between devices: 10.3 us -> 0.01 us  [exchange(): return lax.all_to_all(cells, 'seq', split_axis=0, concat_axis=0)]
    pallas_call x0 -> x1, Pallas kernels: none -> 8.37 us  [prepare(): pl.pallas_call(prepare_kernel, grid_spec=pltpu.PrefetchScalarGridSpec(num...]
    pallas_call x1, Pallas kernels: 33 us -> 41.3 us  [gather_windows(): pl.pallas_call(functools.partial(gather_kernel, orders), out_shape=(jax.S...]
    pallas_call x2 -> x0, local copies, waits for them, and re-layouts: 5.33 us -> none  [whole_step(): pl.pallas_call(step_kernel, grid_spec=pltpu.PrefetchScalarGridSpec(num_sc...]
    convert_element_type x4 -> x1, other arithmetic: 7.12 us -> 4 us  [per_device(): results[:, :, C:].astype(jnp.float32)]
  transfers between devices with their start and end apart: 3 -> 2, of which waited for: 1 -> 0; matrix products, arithmetic and copies ran while one was open for 6% -> 3% of each run, Pallas kernels for 28% -> 42%
where the time goes in v4:
time: 219 us
  Pallas kernels  190 us (87%)
  local copies, waits for them, and re-layouts  9.19 us (4%)
  starting transfers between devices  9.14 us (4%)
  other arithmetic  6.9 us (3%)
  matrix products  2.41 us (1%)
    pallas_call x1, Pallas kernels, whole_step(): pl.pallas_call(step_kernel, grid_spec=pltpu.PrefetchScalarGridSpec(num_sc...  89.5 us
    pallas_call x1, Pallas kernels, reduce_windows(): pl.pallas_call(functools.partial(reduce_kernel, orders), out_shape=(jax.S...  48.9 us
    pallas_call x1, Pallas kernels, gather_windows(): pl.pallas_call(functools.partial(gather_kernel, orders), out_shape=(jax.S...  41.3 us
    all_to_all x2, starting transfers between devices, exchange(): return lax.all_to_all(cells, 'seq', split_axis=0, concat_axis=0)  9.14 us
    pallas_call x1, Pallas kernels, prepare(): pl.pallas_call(prepare_kernel, grid_spec=pltpu.PrefetchScalarGridSpec(num...  8.37 us
    unnamed x60, local copies, waits for them, and re-layouts  6.9 us
  transfers between devices with their start and end apart: 2, of which 0 were waited for; matrix products, arithmetic and copies ran while one was open for 3% of the time, Pallas kernels for 42%

profile of v4, /device:TPU:0, one launch (start us, length us, event | category | flops | bytes accessed | tf_op | source)
XLA Modules:
  0.0 218.6 jit_solution(16867670677956717886)
XLA Ops:
  0.6 8.4 %shard_map.211 = bf16[4,2,256,512]{3,2,1,0:T(8,128)(2,1)} custom-call(s32[8]{0:T(128)} %lengths_ref.1, s32[1]{0:T(128)} %bitcast.place_ref, f32[8,256,256]{2,1,0:T(8,128)} %inputs_ref.1, f32[8,128,256]{2,1,0:T(8,128)} %encoded_ref.1, s32[8,1,128]{2,1,0:T(1,128)} %bitcast.16, f32[8,256,256]{2,1,0:T(8,128)} %cotangent_ref.1), custom_call_target="tpu_custom_call" | custom-call | tf_op jit(solution)/shard_map/pallas_call | solution.py:963
  9.0 4.4 %all-to-all-start = ((bf16[4,2,256,512]{3,2,1,0:T(8,128)(2,1)}), bf16[4,2,256,512]{3,2,1,0:T(8,128)(2,1)S(1)}, u32[]{:S(2)}, u32[]{:S(2)}) async-start(bf16[4,2,256,512]{3,2,1,0:T(8,128)(2,1)} %shard_map.211), calls=%async_computation | async-start | bytes 4194304 | tf_op jit(solution)/shard_map/all_to_all | solution.py:441
  13.4 0.6 dynamic_slice.12.lengths_ref
  14.1 0.5 dynamic_update_slice.7
  14.7 0.6 dynamic_update_slice.6
  15.2 41.3 %shard_map.212 = (bf16[32,192,128]{2,1,0:T(8,128)(2,1)S(1)}, bf16[32,176,128]{2,1,0:T(8,128)(2,1)S(1)}) custom-call(bf16[192,128]{1,0:T(8,128)(2,1)S(1)} %bitcast.12, bf16[176,128]{1,0:T(8,128)(2,1)S(1)} %bitcast.13), custom_call_target="tpu_custom_call" | custom-call | tf_op jit(solution)/shard_map/pallas_call | solution.py:231
  56.5 1.1 shard_map.213
  57.6 0.9 copy-done.3
  58.5 0.8 copy-done.5
  59.3 0.7 copy-done.8
  60.0 0.7 copy-done.9
  60.7 0.6 copy-done.11
  61.3 0.6 copy-done.15
  61.9 1.0 convolution_add_fusion
  62.9 0.6 broadcast_in_dim.19.time_ref
  63.5 1.3 copy-done.18
  64.8 89.5 %shard_map.214 = (bf16[4,2,256,512]{3,2,1,0:T(8,128)(2,1)}, f32[2,1,256]{2,1,0:T(1,128)}, f32[1536,256]{1,0:T(8,128)}, f32[256,256]{1,0:T(8,128)}, f32[8,256]{1,...) custom-call(s32[2]{0:T(128)} %dynamic_slice.12.lengths_ref, ...), custom_call_target="tpu_custom_call" | custom-call | tf_op jit(solution)/shard_map/pallas_call | solution.py:908
  154.3 0.0 copy-start.28
  154.3 0.0 copy-start.17
  154.4 4.7 %all-to-all-start.1 = ((bf16[4,2,256,512]{3,2,1,0:T(8,128)(2,1)}), bf16[4,2,256,512]{3,2,1,0:T(8,128)(2,1)}, u32[]{:S(2)}, u32[]{:S(2)}) async-start(bf16[4,2,256,512]{3,2,1,0:T(8,128)(2,1)} %get-tuple-element.51), calls=%async_computation.1 | async-start | bytes 4194304 | tf_op jit(solution)/shard_map/all_to_all | solution.py:441
  159.1 1.4 fusion.refs_2_
  160.6 1.2 copy-done.2
  161.8 0.9 shard_map.215
  162.7 0.0 copy-start.22
  162.7 0.0 copy-start.26
  162.8 0.0 copy-start.24
  162.8 48.9 %shard_map.216 = (f32[192,128]{1,0:T(8,128)S(1)}, f32[176,128]{1,0:T(8,128)S(1)}) custom-call(bf16[32,192,128]{2,1,0:T(8,128)(2,1)S(1)} %get-tuple-element.62.in_a, bf16[32,176,128]{2,1,0:T(8,128)(2,1)S(1)} %get-tuple-element.63.in_b), custom_call_target="tpu_custom_call" | custom-call | tf_op jit(solution)/shard_map/pallas_call | solution.py:304
  211.7 0.8 fusion.3
  212.5 0.7 multiply_add_fusion.2
  213.2 0.8 fusion.4
  213.9 0.7 multiply_add_fusion
  214.6 4.0 %slice_convert_fusion = (f32[8,256,256]{2,1,0:T(8,128)}, f32[8,256,256]{2,1,0:T(8,128)}) fusion(bf16[8,256,512]{2,1,0:T(8,128)(2,1)} %bitcast.5), kind=kLoop, calls=%fused_computation.1 | loop fusion | flops 1048576 | bytes 6291456 | tf_op jit(solution)/shard_map/convert_element_type | solution.py:1067
  (54 shorter events, 0.1 us)
Async XLA Ops:
  9.0 4.4 %copy-start.29 = (s32[8]{0:T(128)S(1)}, s32[8]{0:T(128)}, u32[]{:S(2)}) copy-start(s32[8]{0:T(128)} %lengths_ref.1) | copy-start | bytes 100
  9.0 5.0 %copy-start.21 = (f32[20624]{0:T(1024)S(1)}, f32[20624]{0:T(1024)}, u32[]{:S(2)}) copy-start(f32[20624]{0:T(1024)} %param.21) | copy-start | bytes 247492
  9.0 5.0 %copy-start.19 = (f32[22592]{0:T(1024)S(1)}, f32[22592]{0:T(1024)}, u32[]{:S(2)}) copy-start(f32[22592]{0:T(1024)} %param.18) | copy-start | bytes 271108
  9.0 54.5 %all-to-all-start = ((bf16[4,2,256,512]{3,2,1,0:T(8,128)(2,1)}), bf16[4,2,256,512]{3,2,1,0:T(8,128)(2,1)S(1)}, u32[]{:S(2)}, u32[]{:S(2)}) async-start(bf16[4,2,256,512]{3,2,1,0:T(8,128)(2,1)} %shard_map.211), calls=%async_computation | async-start | bytes 4194304 | tf_op jit(solution)/shard_map/all_to_all | solution.py:441
  57.6 0.9 copy-start.3
  58.5 0.8 copy-start.5
  59.3 0.7 copy-start.8
  60.0 0.7 copy-start.9
  60.6 0.6 copy-start.11
  61.3 0.6 copy-start.15
  61.9 1.0 copy-start.4
  61.9 1.0 copy-start.12
  61.9 1.6 copy-start.14
  63.5 1.3 copy-start.18
  154.3 4.8 %copy-start.28 = (f32[2,1,256]{2,1,0:T(1,128)S(1)}, f32[2,1,256]{2,1,0:T(1,128)}, u32[]{:S(2)}) copy-start(f32[2,1,256]{2,1,0:T(1,128)} %get-tuple-element.54) | copy-start | bytes 6148
  154.3 6.3 %copy-start = (f32[1536,256]{1,0:T(8,128)S(1)}, f32[1536,256]{1,0:T(8,128)}, u32[]{:S(2)}) copy-start(f32[1536,256]{1,0:T(8,128)} %get-tuple-element.52.refs_0_) | copy-start | bytes 4718596
  154.3 6.3 %copy-start.1 = (f32[256,1024]{1,0:T(8,128)S(1)}, f32[256,1024]{1,0:T(8,128)}, u32[]{:S(2)}) copy-start(f32[256,1024]{1,0:T(8,128)} %get-tuple-element.58.refs_6_) | copy-start | bytes 3145732
  154.3 6.3 %copy-start.6 = (f32[256,384]{1,0:T(8,128)S(1)}, f32[256,384]{1,0:T(8,128)}, u32[]{:S(2)}) copy-start(f32[256,384]{1,0:T(8,128)} %get-tuple-element.56.refs_4_) | copy-start | bytes 1179652
  154.3 6.3 %copy-start.7 = (f32[256,256]{1,0:T(8,128)S(1)}, f32[256,256]{1,0:T(8,128)}, u32[]{:S(2)}) copy-start(f32[256,256]{1,0:T(8,128)} %get-tuple-element.53.refs_1_) | copy-start | bytes 786436
  154.3 6.3 %copy-start.10 = (f32[128,256]{1,0:T(8,128)S(1)}, f32[128,256]{1,0:T(8,128)}, u32[]{:S(2)}) copy-start(f32[128,256]{1,0:T(8,128)} %get-tuple-element.57.refs_5_) | copy-start | bytes 393220
  154.3 6.3 %copy-start.13 = (f32[3,1024]{1,0:T(4,128)S(1)}, f32[3,1024]{1,0:T(4,128)}, u32[]{:S(2)}) copy-start(f32[3,1024]{1,0:T(4,128)} %get-tuple-element.61.refs_9_) | copy-start | bytes 36868
  154.3 6.3 %copy-start.16 = (f32[8,256]{1,0:T(8,128)S(1)}, f32[8,256]{1,0:T(8,128)}, u32[]{:S(2)}) copy-start(f32[8,256]{1,0:T(8,128)} %get-tuple-element.55.refs_3_) | copy-start | bytes 24580
  154.3 6.3 %copy-start.17 = (f32[6,256]{1,0:T(8,128)S(1)}, f32[6,256]{1,0:T(8,128)}, u32[]{:S(2)}) copy-start(f32[6,256]{1,0:T(8,128)} %get-tuple-element.60.refs_8_) | copy-start | bytes 18436
  154.4 60.2 %all-to-all-start.1 = ((bf16[4,2,256,512]{3,2,1,0:T(8,128)(2,1)}), bf16[4,2,256,512]{3,2,1,0:T(8,128)(2,1)}, u32[]{:S(2)}, u32[]{:S(2)}) async-start(bf16[4,2,256,512]{3,2,1,0:T(8,128)(2,1)} %get-tuple-element.51), calls=%async_computation.1 | async-start | bytes 4194304 | tf_op jit(solution)/shard_map/all_to_all | solution.py:441
  160.6 1.2 copy-start.2
  162.7 49.0 %copy-start.22 = (f32[20624]{0:T(1024)S(1)}, f32[20624]{0:T(1024)}, u32[]{:S(2)}) copy-start(f32[20624]{0:T(1024)} %param.21) | copy-start | bytes 247492
  162.7 49.0 %copy-start.26 = (f32[20624]{0:T(1024)S(1)}, f32[20624]{0:T(1024)}, u32[]{:S(2)}) copy-start(f32[20624]{0:T(1024)} %param.22) | copy-start | bytes 247492
  162.7 49.8 %copy-start.27 = (f32[20624]{0:T(1024)S(1)}, f32[20624]{0:T(1024)}, u32[]{:S(2)}) copy-start(f32[20624]{0:T(1024)} %param.23) | copy-start | bytes 247492
  162.7 50.4 %copy-start.25 = (f32[22592]{0:T(1024)S(1)}, f32[22592]{0:T(1024)}, u32[]{:S(2)}) copy-start(f32[22592]{0:T(1024)} %param.19) | copy-start | bytes 271108
  162.8 51.2 %copy-start.24 = (f32[22592]{0:T(1024)S(1)}, f32[22592]{0:T(1024)}, u32[]{:S(2)}) copy-start(f32[22592]{0:T(1024)} %param.20) | copy-start | bytes 271108
  212.5 6.1 %copy-start.23 = (f32[20624]{0:T(1024)}, f32[20624]{0:T(1024)S(1)}, u32[]{:S(2)}) copy-start(f32[20624]{0:T(1024)S(1)} %get-tuple-element.67) | copy-start | bytes 247492
  213.9 4.7 %copy-start.20 = (f32[22592]{0:T(1024)}, f32[22592]{0:T(1024)S(1)}, u32[]{:S(2)}) copy-start(f32[22592]{0:T(1024)S(1)} %get-tuple-element.71) | copy-start | bytes 271108

commit v5 on v4

--- a/solution.py
+++ b/solution.py
@@ -138,10 +138,10 @@
 
 
 def part_orders(mesh_sizes):
-    first = axis_bits(mesh_sizes)
-    second = list(first)
-    if len(second) >= 3:
-        second[-3], second[-2] = second[-2], second[-3]
+    wide = axis_bits(mesh_sizes[:1])
+    near = axis_bits(mesh_sizes[1:])
+    first = near[:-1] + wide + near[-1:]
+    second = near[:-1] + wide[-1:] + wide[:-1] + near[-1:]
     return (first, second)
 
 
@@ -170,19 +170,52 @@
     return {name: lax.axis_index(name) + (1 - 2 * bit_of(name, weight)) * weight}
 
 
+def seq_neighbour(step):
+    return lax.rem(lax.axis_index("seq") + step, lax.axis_size("seq"))
+
+
 def greet(orders):
     barrier = pltpu.get_barrier_semaphore()
-    for name, weight in orders[0]:
+    others = [partner_of(name, weight) for name, weight in orders[0] if name != "seq"]
+    others += [{"seq": seq_neighbour(step)} for step in range(1, lax.axis_size("seq"))]
+    for other in others:
         pl.semaphore_signal(
-            barrier,
-            inc=1,
-            device_id=partner_of(name, weight),
-            device_id_type=pl.DeviceIdType.MESH,
+            barrier, inc=1, device_id=other, device_id_type=pl.DeviceIdType.MESH
         )
-    pl.semaphore_wait(barrier, len(orders[0]))
-
-
-def gather_kernel(orders, in_a, in_b, out_a, out_b, local_sem, send_sem, recv_sem):
+    pl.semaphore_wait(barrier, len(others))
+
+
+def exchange_copies(cells, cells_out, swap_send, swap_recv):
+    copies = []
+    for step in range(1, lax.axis_size("seq")):
+        target = seq_neighbour(step)
+        copies.append(
+            pltpu.make_async_remote_copy(
+                src_ref=cells.at[target],
+                dst_ref=cells_out.at[lax.axis_index("seq")],
+                send_sem=swap_send.at[step - 1],
+                recv_sem=swap_recv.at[step - 1],
+                device_id={"seq": target},
+                device_id_type=pl.DeviceIdType.MESH,
+            )
+        )
+    return copies
+
+
+def gather_kernel(
+    orders,
+    in_a,
+    in_b,
+    cells,
+    out_a,
+    out_b,
+    cells_out,
+    local_sem,
+    send_sem,
+    recv_sem,
+    swap_send,
+    swap_recv,
+):
     ins, outs = (in_a, in_b), (out_a, out_b)
     stage_count = len(orders[0])
     offsets = []
@@ -195,9 +228,12 @@
         pltpu.make_async_copy(ins[part], outs[part].at[offsets[part]], local_sem.at[part])
         for part in range(2)
     ]
+    place = lax.axis_index("seq")
+    locals_now.append(pltpu.make_async_copy(cells.at[place], cells_out.at[place], local_sem.at[2]))
     for copy in locals_now:
         copy.start()
     greet(orders)
+    swaps = exchange_copies(cells, cells_out, swap_send, swap_recv)
     for copy in locals_now:
         copy.wait()
     copies = []
@@ -217,15 +253,20 @@
             )
             copy.start()
             copies.append(copy)
+        if step == 0:
+            for copy in swaps:
+                copy.start()
         for part in range(2):
             copies[2 * step + part].wait_recv()
             name, weight = orders[part][step]
             offsets[part] = offsets[part] - bit_of(name, weight) * held
     for copy in copies:
         copy.wait_send()
-
-
-def gather_windows(orders, win_a, win_b):
+    for copy in swaps:
+        copy.wait()
+
+
+def gather_windows(orders, win_a, win_b, cells):
     count = 1 << len(orders[0])
     stages = len(orders[0])
     return pl.pallas_call(
@@ -233,24 +274,46 @@
         out_shape=(
             jax.ShapeDtypeStruct((count,) + win_a.shape, win_a.dtype),
             jax.ShapeDtypeStruct((count,) + win_b.shape, win_b.dtype),
+            jax.ShapeDtypeStruct(cells.shape, cells.dtype),
         ),
-        in_specs=[pl.BlockSpec(memory_space=pltpu.VMEM)] * 2,
-        out_specs=[pl.BlockSpec(memory_space=pltpu.VMEM)] * 2,
+        in_specs=[pl.BlockSpec(memory_space=pltpu.VMEM)] * 3,
+        out_specs=[pl.BlockSpec(memory_space=pltpu.VMEM)] * 3,
         scratch_shapes=[
-            pltpu.SemaphoreType.DMA((2,)),
+            pltpu.SemaphoreType.DMA((3,)),
             pltpu.SemaphoreType.DMA((2, stages)),
             pltpu.SemaphoreType.DMA((2, stages)),
+            pltpu.SemaphoreType.DMA((cells.shape[0] - 1,)),
+            pltpu.SemaphoreType.DMA((cells.shape[0] - 1,)),
         ],
         compiler_params=pltpu.CompilerParams(
             collective_id=0, has_side_effects=True, vmem_limit_bytes=32 * 1024 * 1024
         ),
-    )(win_a, win_b)
-
-
-def reduce_kernel(orders, in_a, in_b, out_a, out_b, land_a, land_b, send_sem, recv_sem):
+    )(win_a, win_b, cells)
+
+
+def reduce_kernel(
+    orders,
+    in_a,
+    in_b,
+    cells,
+    out_a,
+    out_b,
+    cells_out,
+    land_a,
+    land_b,
+    local_sem,
+    send_sem,
+    recv_sem,
+    swap_send,
+    swap_recv,
+):
     ins, outs, lands = (in_a, in_b), (out_a, out_b), (land_a, land_b)
     stage_count = len(orders[0])
+    place = lax.axis_index("seq")
+    local = pltpu.make_async_copy(cells.at[place], cells_out.at[place], local_sem.at[0])
+    local.start()
     greet(orders)
+    swaps = exchange_copies(cells, cells_out, swap_send, swap_recv)
     copies = []
 
     def source(part, step, keep):
@@ -278,6 +341,9 @@
             )
             copy.start()
             copies.append(copy)
+        if step == 0:
+            for copy in swaps:
+                copy.start()
         for part in range(2):
             copies[2 * step + part].wait_recv()
             mine = source(part, step, True)
@@ -296,9 +362,12 @@
                 lax.fori_loop(0, held, add_one, 0)
     for copy in copies:
         copy.wait_send()
-
-
-def reduce_windows(orders, rows_a, rows_b):
+    for copy in swaps:
+        copy.wait()
+    local.wait()
+
+
+def reduce_windows(orders, rows_a, rows_b, cells):
     count = 1 << len(orders[0])
     stages = len(orders[0])
     return pl.pallas_call(
@@ -306,19 +375,23 @@
         out_shape=(
             jax.ShapeDtypeStruct(rows_a.shape[1:], jnp.float32),
             jax.ShapeDtypeStruct(rows_b.shape[1:], jnp.float32),
+            jax.ShapeDtypeStruct(cells.shape, cells.dtype),
         ),
-        in_specs=[pl.BlockSpec(memory_space=pltpu.VMEM)] * 2,
-        out_specs=[pl.BlockSpec(memory_space=pltpu.VMEM)] * 2,
+        in_specs=[pl.BlockSpec(memory_space=pltpu.VMEM)] * 3,
+        out_specs=[pl.BlockSpec(memory_space=pltpu.VMEM)] * 3,
         scratch_shapes=[
             pltpu.VMEM((count - 1,) + rows_a.shape[1:], rows_a.dtype),
             pltpu.VMEM((count - 1,) + rows_b.shape[1:], rows_b.dtype),
+            pltpu.SemaphoreType.DMA((1,)),
             pltpu.SemaphoreType.DMA((2, stages)),
             pltpu.SemaphoreType.DMA((2, stages)),
+            pltpu.SemaphoreType.DMA((cells.shape[0] - 1,)),
+            pltpu.SemaphoreType.DMA((cells.shape[0] - 1,)),
         ],
         compiler_params=pltpu.CompilerParams(
             collective_id=1, has_side_effects=True, vmem_limit_bytes=32 * 1024 * 1024
         ),
-    )(rows_a, rows_b)
+    )(rows_a, rows_b, cells)
 
 
 RES_SQUARES = 7 * C * C
@@ -437,26 +510,20 @@
     return lax.dynamic_slice(window.reshape(-1), (lead,), (length_now,))
 
 
-def exchange(cells):
-    return lax.all_to_all(cells, "seq", split_axis=0, concat_axis=0)
-
-
 SIN_TERMS = (
-    0.9999999956945583,
-    -0.1666665793542191,
-    0.008333049779226345,
-    -0.00019808982984063025,
-    2.605019582312477e-06,
+    3.141592640063848,
+    -5.167710072816043,
+    2.5500772667383647,
+    -0.5982893715546711,
+    0.07765328748430061,
 )
 COS_TERMS = (
-    0.9999999997785896,
-    -0.4999999935376167,
-    0.04166663608814044,
-    -0.0013888359276781354,
-    2.47600539678114e-05,
-    -2.6049608156992194e-07,
+    0.9999999530157438,
+    -4.934792793539851,
+    4.058410463392346,
+    -1.3318699300230954,
+    0.21967444597863747,
 )
-PI_PARTS = (3.140625, 0.0009670257568359375, 6.27832957178498e-07)
 ROUND_SHIFT = 12582912.0
 
 
@@ -480,11 +547,8 @@
     return jnp.sum(cells, axis=0, keepdims=True)
 
 
-def sin_cos(angle):
-    turns = (angle * (1.0 / math.pi) + ROUND_SHIFT) - ROUND_SHIFT
-    rest = angle - turns * PI_PARTS[0]
-    rest = rest - turns * PI_PARTS[1]
-    rest = rest - turns * PI_PARTS[2]
+def sin_cos(half_turns):
+    rest = half_turns - ((half_turns + ROUND_SHIFT) - ROUND_SHIFT)
     square = rest * rest
     sine = SIN_TERMS[-1]
     for term in SIN_TERMS[-2::-1]:
@@ -717,18 +781,18 @@
             grad_snake = mm_right(grad_low, down_ref[lanes, :])
             speed = jnp.exp(wide_ref[1:2, lanes])
             depth = 1.0 / (jnp.exp(wide_ref[2:3, lanes]) + 1e-09)
-            angle = up_out * speed
-            sine, cosine = sin_cos(angle)
+            half_turns = up_out * (speed * (1.0 / math.pi))
+            sine, cosine = sin_cos(half_turns)
             square = sine * sine
             value = (up_out + square * depth).astype(jnp.bfloat16)
             snake[rows, lanes] = value
             result = result + mm(value, down_ref[lanes, :])
-            slope = grad_snake * ((2.0 * sine) * cosine) * depth
+            slope = (grad_snake * (2.0 * depth)) * (sine * cosine)
             grad_here = (grad_snake + slope * speed).astype(jnp.bfloat16)
             grad_up[rows, lanes] = grad_here
             grad_in = grad_in + mm_right(grad_here, up_ref[:, lanes])
             gwide_ref[0:1, lanes] += column_sum(grad_here.astype(jnp.float32))
-            gwide_ref[1:2, lanes] += column_sum(slope * angle)
+            gwide_ref[1:2, lanes] += column_sum(slope * half_turns)
             gwide_ref[2:3, lanes] += column_sum(grad_snake * square)
         results_ref[index, 0, :, 0:C] = ((mid + result + tf_rows_ref[5:6, :]) * tile_mask(index)).astype(
             jnp.bfloat16
@@ -763,6 +827,7 @@
     def attend_back(index):
         rows = rows_at(index)
         total = jnp.zeros((tile, INNER), jnp.float32)
+        scores_low, chances_low = [], []
         for head in range(HEADS):
             grad_out = heads_g[head, rows, :]
             chance = probs[head, rows, :]
@@ -770,8 +835,15 @@
             dot_row = jnp.sum(chance * grad_probs, axis=-1, keepdims=True)
             grad_scores = (chance * (grad_probs - dot_row)).astype(jnp.bfloat16)
             total = total + mm(grad_scores, heads_k[head])
-            grad_key[...] += mm_left(grad_scores, heads_q[head, rows, :])
-            grad_value[...] += mm_left(chance.astype(jnp.bfloat16), grad_out)
+            scores_low.append(grad_scores)
+            chances_low.append(chance.astype(jnp.bfloat16))
+        both = (HEADS * tile, INNER)
+        grad_key[...] += mm_left(
+            jnp.concatenate(scores_low, axis=0), heads_q[:, rows, :].reshape(both)
+        )
+        grad_value[...] += mm_left(
+            jnp.concatenate(chances_low, axis=0), heads_g[:, rows, :].reshape(both)
+        )
         grad_query[rows, :] = total * SCORE_SCALE
 
     loop(attend_back)
@@ -864,6 +936,7 @@
     def scale_rows():
         low_side = jnp.exp(wide_ref[2:3, :])
         depth = 1.0 / (low_side + 1e-09)
+        gwide_ref[1:2, :] = gwide_ref[1:2, :] * math.pi
         gwide_ref[2:3, :] = -gwide_ref[2:3, :] * low_side * depth * depth
 
 
@@ -999,17 +1072,18 @@
     key_total = local_len * seq_size
     utt_count = utts_here // seq_size
     seq_index = lax.axis_index("seq")
-    cells = exchange(prepare(inputs, encoded, durations, lengths, cotangent))
+    cells = prepare(inputs, encoded, durations, lengths, cotangent)
     mesh_sizes = [(name, lax.axis_size(name)) for name in ("dp", "seq")]
     orders = part_orders(mesh_sizes)
     places = place_maps(orders, mesh_sizes)
     owner = flat_index(mesh_sizes)
     shard_lengths = (res_master.shape[0], tf_master.shape[0])
     window_sizes = [window_rows(size, len(places[0])) for size in shard_lengths]
-    gathered = gather_windows(
+    *gathered, cells = gather_windows(
         orders,
         to_window(res_master, window_sizes[0], owner),
         to_window(tf_master, window_sizes[1], owner),
+        cells,
     )
     (
         convs,
@@ -1049,9 +1123,11 @@
     grad_time_w = jnp.dot(
         time_act.astype(jnp.float32).T, grad_time_proj[:, 0], precision=lax.Precision.HIGHEST
     )
-    results = exchange(results).reshape(utts_here, local_len, 2 * C)
     grads = (grad_convs, grad_res_w, grad_time_w, grad_rows, *tf_grads)
-    summed = reduce_windows(orders, *cut_grads(places, shard_lengths, window_sizes, grads))
+    *summed, results = reduce_windows(
+        orders, *cut_grads(places, shard_lengths, window_sizes, grads), results
+    )
+    results = results.reshape(utts_here, local_len, 2 * C)
     res_share = from_window(summed[0], shard_lengths[0], owner)
     tf_share = from_window(summed[1], shard_lengths[1], owner)
     tokens_total = utts_here * key_total * lax.axis_size("dp")

time: 219 us -> 195 us (0.89)
  Pallas kernels: 190 us -> 165 us
  local copies, waits for them, and re-layouts: 9.19 us -> 19.6 us
  starting transfers between devices: 9.14 us -> 0 us
    pallas_call x1, Pallas kernels: 48.9 us -> 35.1 us  [reduce_windows(): pl.pallas_call(functools.partial(reduce_kernel, orders), out_shape=(jax.S...]
    unnamed x60, local copies, waits for them, and re-layouts: 6.9 us -> 16.7 us
    all_to_all x2 -> x0, starting transfers between devices: 9.14 us -> none  [exchange(): return lax.all_to_all(cells, 'seq', split_axis=0, concat_axis=0)]
    pallas_call x1, Pallas kernels: 41.3 us -> 35.4 us  [gather_windows(): pl.pallas_call(functools.partial(gather_kernel, orders), out_shape=(jax.S...]
    pallas_call x1, Pallas kernels: 89.5 us -> 84 us  [whole_step(): pl.pallas_call(step_kernel, grid_spec=pltpu.PrefetchScalarGridSpec(num_sc...]
  transfers between devices with their start and end apart: 2 -> 0, of which waited for: 0 -> 0; matrix products, arithmetic and copies ran while one was open for 3% -> 0% of each run, Pallas kernels for 42% -> 0%
where the time goes in v5:
time: 195 us; the launch traced here: 194 us
  Pallas kernels  165 us (85%)
  local copies, waits for them, and re-layouts  19.6 us (10%)
  other arithmetic  7.1 us (4%)
    pallas_call x1, Pallas kernels, whole_step(): pl.pallas_call(step_kernel, grid_spec=pltpu.PrefetchScalarGridSpec(num_sc...  84 us
    pallas_call x1, Pallas kernels, gather_windows(): pl.pallas_call(functools.partial(gather_kernel, orders), out_shape=(jax.S...  35.4 us
    pallas_call x1, Pallas kernels, reduce_windows(): pl.pallas_call(functools.partial(reduce_kernel, orders), out_shape=(jax.S...  35.1 us
    unnamed x60, local copies, waits for them, and re-layouts  16.7 us
    pallas_call x1, Pallas kernels, prepare(): pl.pallas_call(prepare_kernel, grid_spec=pltpu.PrefetchScalarGridSpec(num...  8.37 us

profile of v5, /device:TPU:0, one launch (start us, length us, event | category | flops | bytes accessed | tf_op | source)
XLA Modules:
  0.0 194.0 jit_solution(18075651748153078464)
XLA Ops:
  0.7 1.2 dynamic_slice.12.lengths_ref
  1.9 0.9 convert_element_type.23
  3.4 0.9 convert_element_type.22
  4.9 8.4 %shard_map.211.cells = bf16[4,2,256,512]{3,2,1,0:T(8,128)(2,1)} custom-call(s32[8]{0:T(128)} %lengths_ref.1, s32[1]{0:T(128)} %bitcast.2.place_ref, f32[8,256,256]{2,1,0:T(8,128)} %inputs_ref.1, f32[8,128,256]{2,1,0:T(8,128)} %encoded_ref.1, s32[8,1,128]{2,1,0:T(1,128)} %bitcast.17, f32[8,256,256]{2,1,0:T(8,128)} %cotangent_ref.1), custom_call_target="tpu_custom_call" | custom-call | tf_op jit(solution)/shard_map/pallas_call | solution.py:1036
  13.2 1.6 copy-done
  14.8 35.4 %shard_map.212 = (bf16[32,192,128]{2,1,0:T(8,128)(2,1)S(1)}, bf16[32,176,128]{2,1,0:T(8,128)(2,1)S(1)}, bf16[4,2,256,512]{3,2,1,0:T(8,128)(2,1)S(1)}) custom-call(bf16[192,128]{1,0:T(8,128)(2,1)S(1)} %bitcast.13, bf16[176,128]{1,0:T(8,128)(2,1)S(1)} %bitcast.14, bf16[4,2,256,512]{3,2,1,0:T(8,128)(2,1)S(1)} %copy-done), custom_call_target="tpu_custom_call" | custom-call | tf_op jit(solution)/shard_map/pallas_call | solution.py:272
  50.3 1.3 copy-done.1
  51.6 1.1 shard_map.213
  52.7 0.9 copy-done.6
  53.6 0.8 copy-done.8
  54.4 0.7 copy-done.11
  55.1 0.6 copy-done.12
  55.7 0.6 copy-done.14
  57.7 84.0 %shard_map.214 = (bf16[4,2,256,512]{3,2,1,0:T(8,128)(2,1)}, f32[2,1,256]{2,1,0:T(1,128)}, f32[1536,256]{1,0:T(8,128)}, f32[256,256]{1,0:T(8,128)}, f32[8,256]{1,...) custom-call(s32[2]{0:T(128)} %dynamic_slice.12.lengths_ref, ...), custom_call_target="tpu_custom_call" | custom-call | tf_op jit(solution)/shard_map/pallas_call | solution.py:981
  141.7 1.3 fusion.refs_2_
  143.1 1.4 copy-done.3
  144.5 1.2 copy-done.4
  145.7 1.2 copy-done.5
  146.9 1.0 copy-done.9
  147.9 0.9 copy-done.10
  148.9 0.9 copy-done.13
  149.8 0.7 copy-done.16
  150.5 0.7 copy-done.19
  151.2 0.7 copy-done.20
  151.9 0.9 shard_map.215
  152.7 0.7 copy-done.2
  153.5 35.1 %shard_map.216 = (f32[192,128]{1,0:T(8,128)S(1)}, f32[176,128]{1,0:T(8,128)S(1)}, bf16[4,2,256,512]{3,2,1,0:T(8,128)(2,1)S(1)}) custom-call(bf16[32,192,128]{2,1,0:T(8,128)(2,1)S(1)} %get-tuple-element.64.in_a, bf16[32,176,128]{2,1,0:T(8,128)(2,1)S(1)} %get-tuple-element.65.in_b, bf16[4,2,256,512]{3,2,1,0:T(8,128)(2,1)S(1)} %copy-done.2), custom_call_target="tpu_custom_call" | custom-call | tf_op jit(solution)/shard_map/pallas_call | solution.py:373
  188.7 0.8 fusion.4
  189.5 0.7 multiply_add_fusion
  190.1 0.8 fusion.3
  190.9 0.7 multiply_add_fusion.2
  191.6 2.4 %slice_convert_fusion = (f32[8,256,256]{2,1,0:T(8,128)}, f32[8,256,256]{2,1,0:T(8,128)}) fusion(bf16[8,256,512]{2,1,0:T(8,128)(2,1)S(1)} %bitcast.12), kind=kLoop, calls=%fused_computation.1 | loop fusion | flops 1048576 | bytes 6291456 | tf_op jit(solution)/shard_map/convert_element_type | solution.py:1143
  (50 shorter events, 2.5 us)
Async XLA Ops:
  13.2 1.6 copy-start
  14.8 41.5 %copy-start.29 = (f32[8,1024]{1,0:T(8,128)S(1)}, f32[8,1024]{1,0:T(8,128)}, u32[]{:S(2)}) copy-start(f32[8,1024]{1,0:T(8,128)} %param.16) | copy-start | bytes 98308
  50.3 1.3 copy-start.1
  52.7 0.9 copy-start.6
  53.6 0.8 copy-start.8
  54.4 0.7 copy-start.11
  55.1 0.7 copy-start.12
  55.7 0.6 copy-start.14
  56.3 0.8 copy-start.7
  56.3 0.8 copy-start.15
  56.3 0.8 copy-start.18
  56.3 1.4 copy-start.17
  143.1 1.4 copy-start.3
  144.5 1.2 copy-start.4
  145.7 1.2 copy-start.5
  146.9 1.0 copy-start.9
  147.9 0.9 copy-start.10
  148.9 0.9 copy-start.13
  149.8 0.7 copy-start.16
  150.5 0.7 copy-start.19
  151.2 0.7 copy-start.20
  151.9 1.6 copy-start.2
  153.5 35.2 %copy-start.21 = (f32[22592]{0:T(1024)S(1)}, f32[22592]{0:T(1024)}, u32[]{:S(2)}) copy-start(f32[22592]{0:T(1024)} %param.18) | copy-start | bytes 271108
  153.5 35.2 %copy-start.26 = (f32[22592]{0:T(1024)S(1)}, f32[22592]{0:T(1024)}, u32[]{:S(2)}) copy-start(f32[22592]{0:T(1024)} %param.19) | copy-start | bytes 271108
  153.5 36.0 %copy-start.25 = (f32[22592]{0:T(1024)S(1)}, f32[22592]{0:T(1024)}, u32[]{:S(2)}) copy-start(f32[22592]{0:T(1024)} %param.20) | copy-start | bytes 271108
  153.5 36.7 %copy-start.23 = (f32[20624]{0:T(1024)S(1)}, f32[20624]{0:T(1024)}, u32[]{:S(2)}) copy-start(f32[20624]{0:T(1024)} %param.21) | copy-start | bytes 247492
  153.5 36.7 %copy-start.27 = (f32[20624]{0:T(1024)S(1)}, f32[20624]{0:T(1024)}, u32[]{:S(2)}) copy-start(f32[20624]{0:T(1024)} %param.22) | copy-start | bytes 247492
  153.5 37.4 %copy-start.28 = (f32[20624]{0:T(1024)S(1)}, f32[20624]{0:T(1024)}, u32[]{:S(2)}) copy-start(f32[20624]{0:T(1024)} %param.23) | copy-start | bytes 247492
  189.5 4.5 %copy-start.22 = (f32[22592]{0:T(1024)}, f32[22592]{0:T(1024)S(1)}, u32[]{:S(2)}) copy-start(f32[22592]{0:T(1024)S(1)} %get-tuple-element.75) | copy-start | bytes 271108
  190.9 3.1 %copy-start.24 = (f32[20624]{0:T(1024)}, f32[20624]{0:T(1024)S(1)}, u32[]{:S(2)}) copy-start(f32[20624]{0:T(1024)S(1)} %get-tuple-element.71) | copy-start | bytes 247492

commit v6 on v5

--- a/solution.py
+++ b/solution.py
@@ -22,102 +22,6 @@
 AVERAGE_DECAY = 0.99
 LEARN_BASE = 0.015
 MASK_FILL = -1e30
-
-
-def soft_plus(signal):
-    return jnp.log1p(jnp.exp(-jnp.abs(signal))) + jnp.maximum(signal, 0.0)
-
-
-def mish_fn(signal):
-    return signal * jnp.tanh(soft_plus(signal))
-
-
-def snake_fn(signal, alpha_row, beta_row):
-    return signal + jnp.sin(signal * jnp.exp(alpha_row)) ** 2 / (jnp.exp(beta_row) + 1e-09)
-
-
-def layer_norm(signal, gain_row, shift_row):
-    center = signal - jnp.mean(signal, axis=-1, keepdims=True)
-    spread = jnp.mean(center * center, axis=-1, keepdims=True)
-    return center * lax.rsqrt(spread + EPSILON) * gain_row + shift_row
-
-
-def take_rows(phone_table, phone_rows):
-    return phone_table[phone_rows]
-
-
-def rim_pad(signal):
-    return jnp.pad(signal, ((0, 0), (1, 1), (0, 0)))
-
-
-def conv_apply(padded, weight):
-    length_here = padded.shape[1] - 2
-    result = jnp.dot(padded[:, 0:length_here], weight[0], preferred_element_type=jnp.float32)
-    result = result + jnp.dot(
-        padded[:, 1 : length_here + 1], weight[1], preferred_element_type=jnp.float32
-    )
-    return result + jnp.dot(padded[:, 2:], weight[2], preferred_element_type=jnp.float32)
-
-
-def conv_weight_grad(padded, grad_low):
-    length_here = grad_low.shape[1]
-    return jnp.stack(
-        [
-            jnp.einsum(
-                "utc,utd->cd",
-                padded[:, tap_index : tap_index + length_here],
-                grad_low,
-                preferred_element_type=jnp.float32,
-            )
-            for tap_index in range(3)
-        ]
-    )
-
-
-def conv_input_grad(grad_low, weight):
-    padded = rim_pad(grad_low)
-    length_here = grad_low.shape[1]
-    result = jnp.einsum("utd,cd->utc", padded[:, 2:], weight[0], preferred_element_type=jnp.float32)
-    result = result + jnp.einsum(
-        "utd,cd->utc", padded[:, 1 : length_here + 1], weight[1], preferred_element_type=jnp.float32
-    )
-    return result + jnp.einsum(
-        "utd,cd->utc", padded[:, 0:length_here], weight[2], preferred_element_type=jnp.float32
-    )
-
-
-def norm_forward(signal, frame_mask, valid_count, gain_row, shift_row):
-    width = C // GROUPS
-    shape_now = signal.shape
-    grouped = (signal * frame_mask[:, :, None]).reshape(shape_now[0], shape_now[1], GROUPS, width)
-    total = jnp.sum(grouped, axis=(1, 3))
-    squares = jnp.sum(grouped * grouped, axis=(1, 3))
-    number = valid_count[:, None] * width
-    mean_now = total / number
-    inv_std = lax.rsqrt(squares / number - mean_now * mean_now + EPSILON)
-    mean_wide = jnp.repeat(mean_now, width, axis=1)[:, None, :]
-    inv_wide = jnp.repeat(inv_std, width, axis=1)[:, None, :]
-    normed = (signal - mean_wide) * inv_wide
-    return (normed * gain_row + shift_row, normed, inv_wide)
-
-
-def norm_backward(grad_out, normed, inv_wide, frame_mask, valid_count, gain_row):
-    width = C // GROUPS
-    shape_now = grad_out.shape
-    grad_norm = grad_out * gain_row
-    first_sum = jnp.sum(grad_norm.reshape(shape_now[0], shape_now[1], GROUPS, width), axis=(1, 3))
-    second_sum = jnp.sum(
-        (grad_norm * normed).reshape(shape_now[0], shape_now[1], GROUPS, width), axis=(1, 3)
-    )
-    number = valid_count[:, None] * width
-    first_wide = jnp.repeat(first_sum / number, width, axis=1)[:, None, :]
-    second_wide = jnp.repeat(second_sum / number, width, axis=1)[:, None, :]
-    grad_signal = inv_wide * (
-        grad_norm - frame_mask[:, :, None] * (first_wide + normed * second_wide)
-    )
-    grad_gain = jnp.sum(grad_out * normed, axis=(0, 1))
-    grad_shift = jnp.sum(grad_out, axis=(0, 1))
-    return (grad_signal, grad_gain, grad_shift)
 
 
 def update(master, moment, average, grad, rate):
@@ -276,8 +180,9 @@
             jax.ShapeDtypeStruct((count,) + win_b.shape, win_b.dtype),
             jax.ShapeDtypeStruct(cells.shape, cells.dtype),
         ),
-        in_specs=[pl.BlockSpec(memory_space=pltpu.VMEM)] * 3,
-        out_specs=[pl.BlockSpec(memory_space=pltpu.VMEM)] * 3,
+        in_specs=[pl.BlockSpec(memory_space=pltpu.VMEM)] * 2
+        + [pl.BlockSpec(memory_space=pltpu.HBM)],
+        out_specs=[pl.BlockSpec(memory_space=pltpu.HBM)] * 3,
         scratch_shapes=[
             pltpu.SemaphoreType.DMA((3,)),
             pltpu.SemaphoreType.DMA((2, stages)),
@@ -286,7 +191,7 @@
             pltpu.SemaphoreType.DMA((cells.shape[0] - 1,)),
         ],
         compiler_params=pltpu.CompilerParams(
-            collective_id=0, has_side_effects=True, vmem_limit_bytes=32 * 1024 * 1024
+            collective_id=0, has_side_effects=True, vmem_limit_bytes=62 * 1024 * 1024
         ),
     )(win_a, win_b, cells)
 
@@ -377,8 +282,10 @@
             jax.ShapeDtypeStruct(rows_b.shape[1:], jnp.float32),
             jax.ShapeDtypeStruct(cells.shape, cells.dtype),
         ),
-        in_specs=[pl.BlockSpec(memory_space=pltpu.VMEM)] * 3,
-        out_specs=[pl.BlockSpec(memory_space=pltpu.VMEM)] * 3,
+        in_specs=[pl.BlockSpec(memory_space=pltpu.VMEM)] * 2
+        + [pl.BlockSpec(memory_space=pltpu.HBM)],
+        out_specs=[pl.BlockSpec(memory_space=pltpu.VMEM)] * 2
+        + [pl.BlockSpec(memory_space=pltpu.HBM)],
         scratch_shapes=[
             pltpu.VMEM((count - 1,) + rows_a.shape[1:], rows_a.dtype),
             pltpu.VMEM((count - 1,) + rows_b.shape[1:], rows_b.dtype),
@@ -389,7 +296,7 @@
             pltpu.SemaphoreType.DMA((cells.shape[0] - 1,)),
         ],
         compiler_params=pltpu.CompilerParams(
-            collective_id=1, has_side_effects=True, vmem_limit_bytes=32 * 1024 * 1024
+            collective_id=1, has_side_effects=True, vmem_limit_bytes=62 * 1024 * 1024
         ),
     )(rows_a, rows_b, cells)
 
@@ -419,7 +326,7 @@
     return views
 
 
-def assemble_kernel(places, lengths_now, in_a, in_b, *refs):
+def assemble(places, lengths_now, in_a, in_b, *refs):
     outs, flats = refs[:10], refs[10:12]
     count = len(places[0])
     for part, ref in enumerate((in_a, in_b)):
@@ -439,25 +346,7 @@
             out[:, lane * 128 : (lane + 1) * 128] = piece.astype(out.dtype)
 
 
-def assemble_weights(places, lengths_now, win_a, win_b):
-    shapes = []
-    for index, (part, row, rows, width) in enumerate(matrix_views()):
-        kind = jnp.float32 if index in (3, 8, 9) else jnp.bfloat16
-        shapes.append(jax.ShapeDtypeStruct((rows, width), kind))
-    return pl.pallas_call(
-        functools.partial(assemble_kernel, places, lengths_now),
-        out_shape=shapes,
-        in_specs=[pl.BlockSpec(memory_space=pltpu.VMEM)] * 2,
-        out_specs=[pl.BlockSpec(memory_space=pltpu.VMEM)] * 10,
-        scratch_shapes=[
-            pltpu.VMEM((RES_ROWS + 8, 128), jnp.float32),
-            pltpu.VMEM((TF_ROWS + 12, 128), jnp.float32),
-        ],
-        compiler_params=pltpu.CompilerParams(vmem_limit_bytes=32 * 1024 * 1024),
-    )(win_a, win_b)
-
-
-def cut_kernel(places, lengths_now, *refs):
+def cut(places, lengths_now, *refs):
     ins, outs, flats = refs[:10], refs[10:12], refs[12:14]
     count = len(places[0])
     for ref, (part, row, rows, width) in zip(ins, matrix_views()):
@@ -475,23 +364,6 @@
             )
 
 
-def cut_grads(places, lengths_now, window_sizes, grads):
-    count = len(places[0])
-    return pl.pallas_call(
-        functools.partial(cut_kernel, places, lengths_now),
-        out_shape=[
-            jax.ShapeDtypeStruct((count, rows, 128), jnp.bfloat16) for rows in window_sizes
-        ],
-        in_specs=[pl.BlockSpec(memory_space=pltpu.VMEM)] * 10,
-        out_specs=[pl.BlockSpec(memory_space=pltpu.VMEM)] * 2,
-        scratch_shapes=[
-            pltpu.VMEM((RES_ROWS + 24, 128), jnp.float32),
-            pltpu.VMEM((TF_ROWS + 28, 128), jnp.float32),
-        ],
-        compiler_params=pltpu.CompilerParams(vmem_limit_bytes=40 * 1024 * 1024),
-    )(*grads)
-
-
 def flat_index(mesh_sizes):
     index = 0
     for name, size in mesh_sizes:
@@ -587,11 +459,20 @@
 
 
 def step_kernel(
+    places,
+    shard_lengths,
     lengths_ref,
+    place_ref,
     cells_ref,
     time_ref,
+    win_a,
+    win_b,
+    results_ref,
+    cut_a,
+    cut_b,
     convs_ref,
     res_ref,
+    timew_ref,
     rows_ref,
     qkv_ref,
     out_ref,
@@ -599,10 +480,9 @@
     down_ref,
     tf_rows_ref,
     wide_ref,
-    results_ref,
-    gtime_ref,
     gconvs_ref,
     gres_ref,
+    gtimew_ref,
     grows_ref,
     gqkv_ref,
     gout_ref,
@@ -610,6 +490,10 @@
     gdown_ref,
     gtf_ref,
     gwide_ref,
+    flat_a,
+    flat_b,
+    time_rows,
+    gtime_rows,
     pad,
     col_one,
     col_two,
@@ -639,28 +523,47 @@
     frames = z_one.shape[0]
     tiles, _, tile, _ = cells_ref.shape
     utt = pl.program_id(0)
-    length_now = lengths_ref[utt]
+    row_at = place_ref[0] * pl.num_programs(0) + utt
+    length_now = lengths_ref[row_at]
     number = length_now.astype(jnp.float32) * (C // GROUPS)
+    weight_refs = (
+        convs_ref,
+        res_ref,
+        timew_ref,
+        rows_ref,
+        qkv_ref,
+        out_ref,
+        up_ref,
+        down_ref,
+        tf_rows_ref,
+        wide_ref,
+    )
+    grad_refs = (
+        gconvs_ref,
+        gres_ref,
+        gtimew_ref,
+        grows_ref,
+        gqkv_ref,
+        gout_ref,
+        gup_ref,
+        gdown_ref,
+        gtf_ref,
+        gwide_ref,
+    )
 
     @pl.when(utt == 0)
-    def clear():
-        for ref in (
-            gconvs_ref,
-            gres_ref,
-            grows_ref,
-            gqkv_ref,
-            gout_ref,
-            gup_ref,
-            gdown_ref,
-            gtf_ref,
-            gwide_ref,
-        ):
+    def begin():
+        assemble(places, shard_lengths, win_a, win_b, *weight_refs, flat_a, flat_b)
+        for ref in grad_refs:
             ref[...] = jnp.zeros_like(ref)
-
+        gtime_rows[...] = jnp.zeros_like(gtime_rows)
+        low = mish_value(time_ref[...]).astype(jnp.bfloat16)
+        time_rows[...] = mm(low, timew_ref[...]) + rows_ref[7:8, :]
+
+    time_row = time_rows[pl.ds(row_at, 1), :]
     edge = jnp.zeros((8, C), jnp.float32)
     pad[0:8, :] = edge
     pad[frames + 8 : frames + 16, :] = edge
-    gtime_ref[...] = jnp.zeros_like(gtime_ref)
     group_row = lax.broadcasted_iota(jnp.int32, (C, C), 0) // (C // GROUPS)
     group_column = lax.broadcasted_iota(jnp.int32, (C, C), 1) // (C // GROUPS)
     group_ones = (group_row == group_column).astype(jnp.float32)
@@ -725,7 +628,7 @@
     def hidden(index):
         normed = (z_one[rows_at(index), :] - mean_one) * inv_one
         act = mish_value(normed * rows_ref[1:2, :] + rows_ref[2:3, :])
-        pad[rows_at(index, 8), :] = (act + time_ref[0]) * tile_mask(index)
+        pad[rows_at(index, 8), :] = (act + time_row) * tile_mask(index)
 
     loop(hidden)
     build_columns(col_two)
@@ -912,14 +815,19 @@
     def hidden_back(index, carry):
         rows = rows_at(index)
         grad_here = conv_back(rows, 3 * C) * tile_mask(index)
-        gtime_ref[0] += column_sum(grad_here)
+        time_sum = column_sum(grad_here)
         normed = (z_one[rows, :] - mean_one) * inv_one
         grad_here = mish_slope(normed * rows_ref[1:2, :] + rows_ref[2:3, :]) * grad_here
         grad_norm[rows, :] = grad_here
-        return (carry[0] + column_sum(grad_here), carry[1] + column_sum(grad_here * normed))
-
-    shift_sum, gain_sum = lax.fori_loop(0, tiles, hidden_back, (zero, zero))
-    grows_ref[7:8, :] += gtime_ref[0]
+        return (
+            carry[0] + column_sum(grad_here),
+            carry[1] + column_sum(grad_here * normed),
+            carry[2] + time_sum,
+        )
+
+    shift_sum, gain_sum, time_sum = lax.fori_loop(0, tiles, hidden_back, (zero, zero, zero))
+    grows_ref[7:8, :] += time_sum
+    gtime_rows[pl.ds(row_at, 1), :] = time_sum
     norm_back(z_one, mean_one, inv_one, 1, 0, shift_sum, gain_sum)
     conv_weights(col_one, 0)
 
@@ -933,25 +841,43 @@
     gqkv_ref[...] += mm_left(attn_in[...], grad_qkv[...])
 
     @pl.when(utt == pl.num_programs(0) - 1)
-    def scale_rows():
+    def end():
         low_side = jnp.exp(wide_ref[2:3, :])
         depth = 1.0 / (low_side + 1e-09)
         gwide_ref[1:2, :] = gwide_ref[1:2, :] * math.pi
         gwide_ref[2:3, :] = -gwide_ref[2:3, :] * low_side * depth * depth
-
-
-def whole_step(lengths, cells, time_proj, weights):
-    (convs, res_weight, rows, qkv_weight, out_weight, up_weight, down_weight, tf_rows, wide) = weights
+        time_low = mish_value(time_ref[...]).astype(jnp.bfloat16).astype(jnp.float32)
+        gtimew_ref[...] = lax.dot_general(
+            time_low,
+            gtime_rows[...],
+            (((0,), (0,)), ((), ())),
+            precision=lax.Precision.HIGHEST,
+            preferred_element_type=jnp.float32,
+        )
+        cut(places, shard_lengths, *grad_refs, cut_a, cut_b, flat_a, flat_b)
+
+
+def whole_step(places, shard_lengths, lengths, place, cells, time_embed, windows):
     tiles, utts, tile, _ = cells.shape
     frames = tiles * tile
-    by_utt = pl.BlockSpec((tiles, 1, tile, 2 * C), lambda u, s: (0, u, 0, 0))
-    row_by_utt = pl.BlockSpec((1, 1, C), lambda u, s: (u, 0, 0))
+    by_utt = pl.BlockSpec((tiles, 1, tile, 2 * C), lambda u, n, p: (0, u, 0, 0))
 
     def fixed(array):
-        return pl.BlockSpec(array.shape, lambda u, s: (0, 0))
+        return pl.BlockSpec(
+            array.shape, lambda u, n, p: (0,) * array.ndim, pipeline_mode=pl.Buffered(1)
+        )
 
     f32, low = jnp.float32, jnp.bfloat16
-    scratch = [
+    weight_kinds = [
+        ((rows, width), f32 if index in (3, 8, 9) else low)
+        for index, (part, row, rows, width) in enumerate(matrix_views())
+    ]
+    scratch = weight_kinds + [(shape, f32) for shape, kind in weight_kinds]
+    scratch += [
+        ((RES_ROWS + 24, 128), f32),
+        ((TF_ROWS + 28, 128), f32),
+        (time_embed.shape[:1] + (C,), f32),
+        (time_embed.shape[:1] + (C,), f32),
         ((frames + 16, C), f32),
         ((frames, 3 * C), low),
         ((frames, 3 * C), low),
@@ -979,74 +905,69 @@
         ((frames, C), low),
     ]
     return pl.pallas_call(
-        step_kernel,
+        functools.partial(step_kernel, places, shard_lengths),
         grid_spec=pltpu.PrefetchScalarGridSpec(
-            num_scalar_prefetch=1,
+            num_scalar_prefetch=2,
             grid=(utts,),
-            in_specs=[by_utt, row_by_utt] + [fixed(array) for array in weights],
-            out_specs=[by_utt, row_by_utt] + [fixed(array) for array in weights],
+            in_specs=[by_utt] + [fixed(array) for array in (time_embed, *windows)],
+            out_specs=[by_utt] + [fixed(array) for array in windows],
             scratch_shapes=[pltpu.VMEM(shape, kind) for shape, kind in scratch],
         ),
-        out_shape=[
-            jax.ShapeDtypeStruct(cells.shape, low),
-            jax.ShapeDtypeStruct((utts, 1, C), f32),
-        ]
-        + [jax.ShapeDtypeStruct(array.shape, f32) for array in weights],
+        out_shape=[jax.ShapeDtypeStruct(array.shape, low) for array in (cells, *windows)],
         compiler_params=pltpu.CompilerParams(
-            dimension_semantics=("arbitrary",), vmem_limit_bytes=60 * 1024 * 1024
+            dimension_semantics=("arbitrary",), vmem_limit_bytes=61 * 1024 * 1024
         ),
-    )(lengths, cells, time_proj, *weights)
+    )(lengths, place, cells, time_embed, *windows)
 
 
 def prepare_kernel(
     lengths_ref, place_ref, inputs_ref, encoded_ref, durations_ref, cotangent_ref, out_ref
 ):
-    frames, phones = inputs_ref.shape[1], durations_ref.shape[2]
+    group, frames, _ = inputs_ref.shape
+    phones = durations_ref.shape[2]
     first = place_ref[0] * frames
-    durations = durations_ref[0].astype(jnp.float32)
     before = lax.broadcasted_iota(jnp.int32, (phones, phones), 0)
     after = lax.broadcasted_iota(jnp.int32, (phones, phones), 1)
     upper = (before <= after).astype(jnp.bfloat16)
-    wide = jnp.broadcast_to(durations, (16, phones)).astype(jnp.bfloat16)
-    ends = mm(wide, upper)[0:1]
-    starts = ends - durations
     last = lax.broadcasted_iota(jnp.int32, (1, phones), 1) == phones - 1
-    ends = jnp.where(last, 1e9, ends)
     ids = lax.broadcasted_iota(jnp.int32, (frames, 1), 0) + first
     times = ids.astype(jnp.float32)
-    picked = jnp.where((times >= starts) & (times < ends), 1.0, 0.0).astype(jnp.bfloat16)
-    table = encoded_ref[0]
-    high = table.astype(jnp.bfloat16)
-    rest = table - high.astype(jnp.float32)
-    middle = rest.astype(jnp.bfloat16)
-    low = (rest - middle.astype(jnp.float32)).astype(jnp.bfloat16)
-    rows = (mm(picked, high) + mm(picked, middle)) + mm(picked, low)
-    mask = (ids < lengths_ref[pl.program_id(0)]).astype(jnp.float32)
-    out_ref[0, 0, :, 0:C] = ((inputs_ref[0] + rows) * mask).astype(jnp.bfloat16)
-    out_ref[0, 0, :, C : 2 * C] = (cotangent_ref[0] * mask).astype(jnp.bfloat16)
-
-
-def prepare(inputs, encoded, durations, lengths, cotangent):
+    for utt in range(group):
+        durations = durations_ref[utt].astype(jnp.float32)
+        wide = jnp.broadcast_to(durations, (16, phones)).astype(jnp.bfloat16)
+        ends = mm(wide, upper)[0:1]
+        starts = ends - durations
+        ends = jnp.where(last, 1e9, ends)
+        picked = jnp.where((times >= starts) & (times < ends), 1.0, 0.0).astype(jnp.bfloat16)
+        table = encoded_ref[utt]
+        high = table.astype(jnp.bfloat16)
+        rest = table - high.astype(jnp.float32)
+        middle = rest.astype(jnp.bfloat16)
+        low = (rest - middle.astype(jnp.float32)).astype(jnp.bfloat16)
+        rows = (mm(picked, high) + mm(picked, middle)) + mm(picked, low)
+        mask = (ids < lengths_ref[pl.program_id(0) * group + utt]).astype(jnp.float32)
+        out_ref[0, utt, :, 0:C] = ((inputs_ref[utt] + rows) * mask).astype(jnp.bfloat16)
+        out_ref[0, utt, :, C : 2 * C] = (cotangent_ref[utt] * mask).astype(jnp.bfloat16)
+
+
+def prepare(inputs, encoded, durations, lengths, place, cotangent):
     utts, frames, _ = inputs.shape
     phones = durations.shape[1]
     seq_size = lax.axis_size("seq")
     group = utts // seq_size
-    place = jnp.full((1,), lax.axis_index("seq"), jnp.int32)
-    by_utt = lambda u, n, p: (u, 0, 0)
+    by_group = lambda s, n, p: (s, 0, 0)
     return pl.pallas_call(
         prepare_kernel,
         grid_spec=pltpu.PrefetchScalarGridSpec(
             num_scalar_prefetch=2,
-            grid=(utts,),
+            grid=(seq_size,),
             in_specs=[
-                pl.BlockSpec((1, frames, C), by_utt),
-                pl.BlockSpec((1, phones, C), by_utt),
-                pl.BlockSpec((1, 1, phones), by_utt),
-                pl.BlockSpec((1, frames, C), by_utt),
+                pl.BlockSpec((group, frames, C), by_group),
+                pl.BlockSpec((group, phones, C), by_group),
+                pl.BlockSpec((group, 1, phones), by_group),
+                pl.BlockSpec((group, frames, C), by_group),
             ],
-            out_specs=pl.BlockSpec(
-                (1, 1, frames, 2 * C), lambda u, n, p: (u // group, u % group, 0, 0)
-            ),
+            out_specs=pl.BlockSpec((1, group, frames, 2 * C), lambda s, n, p: (s, 0, 0, 0)),
         ),
         out_shape=jax.ShapeDtypeStruct((seq_size, group, frames, 2 * C), jnp.bfloat16),
         compiler_params=pltpu.CompilerParams(dimension_semantics=("arbitrary",)),
@@ -1068,11 +989,9 @@
     tf_average,
 ):
     utts_here, local_len, _ = inputs.shape
-    seq_size = lax.axis_size("seq")
-    key_total = local_len * seq_size
-    utt_count = utts_here // seq_size
-    seq_index = lax.axis_index("seq")
-    cells = prepare(inputs, encoded, durations, lengths, cotangent)
+    key_total = local_len * lax.axis_size("seq")
+    place = jnp.full((1,), lax.axis_index("seq"), jnp.int32)
+    cells = prepare(inputs, encoded, durations, lengths, place, cotangent)
     mesh_sizes = [(name, lax.axis_size(name)) for name in ("dp", "seq")]
     orders = part_orders(mesh_sizes)
     places = place_maps(orders, mesh_sizes)
@@ -1085,48 +1004,10 @@
         to_window(tf_master, window_sizes[1], owner),
         cells,
     )
-    (
-        convs,
-        res_weight,
-        time_weight,
-        res_small,
-        qkv_weight,
-        out_weight,
-        up_weight,
-        down_weight,
-        tf_small,
-        wide_small,
-    ) = assemble_weights(places, shard_lengths, *gathered)
-    lengths = lax.dynamic_slice_in_dim(lengths, seq_index * utt_count, utt_count)
-    time_embed = lax.dynamic_slice_in_dim(time_embed, seq_index * utt_count, utt_count)
-    time_act = mish_fn(time_embed).astype(jnp.bfloat16)
-    time_proj = jnp.dot(time_act, time_weight, preferred_element_type=jnp.float32) + res_small[7]
-    weights = (
-        convs,
-        res_weight,
-        res_small,
-        qkv_weight,
-        out_weight,
-        up_weight,
-        down_weight,
-        tf_small,
-        wide_small,
-    )
-    (
-        results,
-        grad_time_proj,
-        grad_convs,
-        grad_res_w,
-        grad_rows,
-        *tf_grads,
-    ) = whole_step(lengths, cells, time_proj[:, None, :], weights)
-    grad_time_w = jnp.dot(
-        time_act.astype(jnp.float32).T, grad_time_proj[:, 0], precision=lax.Precision.HIGHEST
-    )
-    grads = (grad_convs, grad_res_w, grad_time_w, grad_rows, *tf_grads)
-    *summed, results = reduce_windows(
-        orders, *cut_grads(places, shard_lengths, window_sizes, grads), results
-    )
+    results, *cuts = whole_step(
+        places, shard_lengths, lengths, place, cells, time_embed, gathered
+    )
+    *summed, results = reduce_windows(orders, *cuts, results)
     results = results.reshape(utts_here, local_len, 2 * C)
     res_share = from_window(summed[0], shard_lengths[0], owner)
     tf_share = from_window(summed[1], shard_lengths[1], owner)

time: 195 us -> 197 us (1.010)
  Pallas kernels: 165 us -> 184 us
  local copies, waits for them, and re-layouts: 19.6 us -> 1.17 us
  other arithmetic: 7.1 us -> 10.5 us
    pallas_call x1, Pallas kernels: 35.4 us -> 52.1 us  [gather_windows(): pl.pallas_call(functools.partial(gather_kernel, orders), out_shape=(jax.S...]
    unnamed x60 -> x20, local copies, waits for them, and re-layouts: 16.7 us -> 0.05 us
    pallas_call x1, Pallas kernels: 35.1 us -> 38 us  [reduce_windows(): pl.pallas_call(functools.partial(reduce_kernel, orders), out_shape=(jax.S...]
    pallas_call x1, Pallas kernels: 8.37 us -> 5.94 us  [prepare(): pl.pallas_call(prepare_kernel, grid_spec=pltpu.PrefetchScalarGridSpec(num...]
    pallas_call x3 -> x1, Pallas kernels: 85.9 us -> 87.6 us  [whole_step(): pl.pallas_call(functools.partial(step_kernel, places, shard_lengths), gri...]
where the time goes in v6:
time: 197 us; the launch traced here: 196 us
  Pallas kernels  184 us (93%)
  other arithmetic  10.5 us (5%)
    pallas_call x1, Pallas kernels, whole_step(): pl.pallas_call(functools.partial(step_kernel, places, shard_lengths), gri...  87.6 us
    pallas_call x1, Pallas kernels, gather_windows(): pl.pallas_call(functools.partial(gather_kernel, orders), out_shape=(jax.S...  52.1 us
    pallas_call x1, Pallas kernels, reduce_windows(): pl.pallas_call(functools.partial(reduce_kernel, orders), out_shape=(jax.S...  38 us
    pallas_call x1, Pallas kernels, prepare(): pl.pallas_call(prepare_kernel, grid_spec=pltpu.PrefetchScalarGridSpec(num...  5.94 us
    convert_element_type x1, other arithmetic, per_device(): results[:, :, C:].astype(jnp.float32)  4 us

profile of v6, /device:TPU:0, one launch (start us, length us, event | category | flops | bytes accessed | tf_op | source)
XLA Modules:
  0.0 196.1 jit_solution(9965907023604237968)
XLA Ops:
  0.7 0.9 convert_element_type.19
  1.6 0.5 dynamic_update_slice.7
  2.1 0.0 copy-start.5
  2.1 0.9 convert_element_type.18
  3.1 0.6 dynamic_update_slice.6
  3.6 0.0 copy-start.4
  3.7 5.9 %shard_map.211.cells = bf16[4,2,256,512]{3,2,1,0:T(8,128)(2,1)} custom-call(s32[8]{0:T(128)} %lengths_ref.3, s32[1]{0:T(128)} %bitcast.place_ref, f32[8,256,256]{2,1,0:T(8,128)} %inputs_ref.1, f32[8,128,256]{2,1,0:T(8,128)} %encoded_ref.1, s32[8,1,128]{2,1,0:T(1,128)} %bitcast.12, f32[8,256,256]{2,1,0:T(8,128)} %cotangent_ref.1), custom_call_target="tpu_custom_call" | custom-call | tf_op jit(solution)/shard_map/pallas_call | solution.py:959
  9.6 0.0 copy-done.5
  9.6 0.0 copy-done.4
  9.6 52.1 %shard_map.212 = (bf16[32,192,128]{2,1,0:T(8,128)(2,1)}, bf16[32,176,128]{2,1,0:T(8,128)(2,1)}, bf16[4,2,256,512]{3,2,1,0:T(8,128)(2,1)}) custom-call(bf16[192,128]{1,0:T(8,128)(2,1)} %bitcast.8, bf16[176,128]{1,0:T(8,128)(2,1)} %bitcast.9, bf16[4,2,256,512]{3,2,1,0:T(8,128)(2,1)} %shard_map.211.cells), custom_call_target="tpu_custom_call" | custom-call | tf_op jit(solution)/shard_map/pallas_call | solution.py:176
  61.7 87.6 %shard_map.213 = (bf16[4,2,256,512]{3,2,1,0:T(8,128)(2,1)}, bf16[32,192,128]{2,1,0:T(8,128)(2,1)}, bf16[32,176,128]{2,1,0:T(8,128)(2,1)}) custom-call(s32[8]{0:T(128)} %lengths_ref.3, s32[1]{0:T(128)} %bitcast.place_ref, bf16[4,2,256,512]{3,2,1,0:T(8,128)(2,1)} %get-tuple-element.21.cells_ref, f32[8,1024]{1,0:T(8,128)} %time_ref.1, ...), custom_call_target="tpu_custom_call" | custom-call | tf_op jit(solution)/shard_map/pallas_call | solution.py:907
  149.3 0.0 copy-start
  149.3 0.0 copy-start.7
  149.3 0.0 copy-start.6
  149.3 0.0 copy-start.2
  149.3 0.0 copy-start.8
  149.4 0.0 copy-start.9
  149.4 38.0 %shard_map.214 = (f32[192,128]{1,0:T(8,128)}, f32[176,128]{1,0:T(8,128)}, bf16[4,2,256,512]{3,2,1,0:T(8,128)(2,1)}) custom-call(bf16[32,192,128]{2,1,0:T(8,128)(2,1)} %get-tuple-element.24.in_a, bf16[32,176,128]{2,1,0:T(8,128)(2,1)} %get-tuple-element.25.in_b, bf16[4,2,256,512]{3,2,1,0:T(8,128)(2,1)} %get-tuple-element.26.cells), custom_call_target="tpu_custom_call" | custom-call | tf_op jit(solution)/shard_map/pallas_call | solution.py:278
  187.4 0.0 copy-done
  187.4 0.0 copy-done.7
  187.4 1.7 fusion.1
  189.1 0.0 copy-start.1
  189.1 0.0 copy-done.6
  189.1 0.7 multiply_add_fusion
  189.7 0.0 copy-done.2
  189.7 0.0 copy-done.8
  189.7 1.7 fusion
  191.4 0.0 copy-done.9
  191.4 0.7 multiply_add_fusion.2
  192.1 4.0 %slice_convert_fusion = (f32[8,256,256]{2,1,0:T(8,128)}, f32[8,256,256]{2,1,0:T(8,128)}) fusion(bf16[8,256,512]{2,1,0:T(8,128)(2,1)} %bitcast.7), kind=kLoop, calls=%fused_computation | loop fusion | flops 1048576 | bytes 6291456 | tf_op jit(solution)/shard_map/convert_element_type | solution.py:1024
  196.1 0.0 copy-done.1
  196.1 0.0 copy-done.3
  (3 shorter events, 0.0 us)
Async XLA Ops:
  2.1 7.5 %copy-start.5 = (bf16[22528]{0:T(1024)(128)(2,1)}, bf16[22528]{0:T(1024)(128)(2,1)S(1)}, u32[]{:S(2)}) copy-start(bf16[22528]{0:T(1024)(128)(2,1)S(1)} %dynamic_update_slice.7) | copy-start | bytes 135172
  3.6 6.0 %copy-start.4 = (bf16[24576]{0:T(1024)(128)(2,1)}, bf16[24576]{0:T(1024)(128)(2,1)S(1)}, u32[]{:S(2)}) copy-start(bf16[24576]{0:T(1024)(128)(2,1)S(1)} %dynamic_update_slice.6) | copy-start | bytes 147460
  149.3 38.0 %copy-start = (f32[22592]{0:T(1024)S(1)}, f32[22592]{0:T(1024)}, u32[]{:S(2)}) copy-start(f32[22592]{0:T(1024)} %param.18) | copy-start | bytes 271108
  149.3 38.0 %copy-start.7 = (f32[22592]{0:T(1024)S(1)}, f32[22592]{0:T(1024)}, u32[]{:S(2)}) copy-start(f32[22592]{0:T(1024)} %param.19) | copy-start | bytes 271108
  149.3 39.7 %copy-start.6 = (f32[22592]{0:T(1024)S(1)}, f32[22592]{0:T(1024)}, u32[]{:S(2)}) copy-start(f32[22592]{0:T(1024)} %param.20) | copy-start | bytes 271108
  149.3 40.4 %copy-start.2 = (f32[20624]{0:T(1024)S(1)}, f32[20624]{0:T(1024)}, u32[]{:S(2)}) copy-start(f32[20624]{0:T(1024)} %param.21) | copy-start | bytes 247492
  149.3 40.4 %copy-start.8 = (f32[20624]{0:T(1024)S(1)}, f32[20624]{0:T(1024)}, u32[]{:S(2)}) copy-start(f32[20624]{0:T(1024)} %param.22) | copy-start | bytes 247492
  149.4 42.0 %copy-start.9 = (f32[20624]{0:T(1024)S(1)}, f32[20624]{0:T(1024)}, u32[]{:S(2)}) copy-start(f32[20624]{0:T(1024)} %param.23) | copy-start | bytes 247492
  189.1 7.0 %copy-start.1 = (f32[22592]{0:T(1024)}, f32[22592]{0:T(1024)S(1)}, u32[]{:S(2)}) copy-start(f32[22592]{0:T(1024)S(1)} %get-tuple-element.35) | copy-start | bytes 271108
  191.4 4.7 %copy-start.3 = (f32[20624]{0:T(1024)}, f32[20624]{0:T(1024)S(1)}, u32[]{:S(2)}) copy-start(f32[20624]{0:T(1024)S(1)} %get-tuple-element.31) | copy-start | bytes 247492

commit v7 on v6

--- a/solution.py
+++ b/solution.py
@@ -114,6 +114,7 @@
     out_a,
     out_b,
     cells_out,
+    bounce,
     local_sem,
     send_sem,
     recv_sem,
@@ -133,41 +134,47 @@
         for part in range(2)
     ]
     place = lax.axis_index("seq")
-    locals_now.append(pltpu.make_async_copy(cells.at[place], cells_out.at[place], local_sem.at[2]))
+    own_in = pltpu.make_async_copy(cells.at[place], bounce, local_sem.at[2])
+    own_out = pltpu.make_async_copy(bounce, cells_out.at[place], local_sem.at[3])
+    own_in.start()
     for copy in locals_now:
         copy.start()
     greet(orders)
     swaps = exchange_copies(cells, cells_out, swap_send, swap_recv)
     for copy in locals_now:
         copy.wait()
-    copies = []
+    copies = {}
+
+    def send(part, step):
+        block = outs[part].at[pl.ds(offsets[part], 1 << step)]
+        copy = pltpu.make_async_remote_copy(
+            src_ref=block,
+            dst_ref=block,
+            send_sem=send_sem.at[part, step],
+            recv_sem=recv_sem.at[part, step],
+            device_id=partner_of(*orders[part][step]),
+            device_id_type=pl.DeviceIdType.MESH,
+        )
+        copy.start()
+        copies[part, step] = copy
+
+    for part in range(2):
+        send(part, 0)
+    for copy in swaps:
+        copy.start()
+    own_in.wait()
+    own_out.start()
     for step in range(stage_count):
-        held = 1 << step
         for part in range(2):
-            name, weight = orders[part][step]
-            start = offsets[part]
-            block = outs[part].at[pl.ds(start, held)]
-            copy = pltpu.make_async_remote_copy(
-                src_ref=block,
-                dst_ref=block,
-                send_sem=send_sem.at[part, step],
-                recv_sem=recv_sem.at[part, step],
-                device_id=partner_of(name, weight),
-                device_id_type=pl.DeviceIdType.MESH,
-            )
-            copy.start()
-            copies.append(copy)
-        if step == 0:
-            for copy in swaps:
-                copy.start()
-        for part in range(2):
-            copies[2 * step + part].wait_recv()
-            name, weight = orders[part][step]
-            offsets[part] = offsets[part] - bit_of(name, weight) * held
-    for copy in copies:
+            copies[part, step].wait_recv()
+            offsets[part] = offsets[part] - bit_of(*orders[part][step]) * (1 << step)
+            if step + 1 < stage_count:
+                send(part, step + 1)
+    for copy in copies.values():
         copy.wait_send()
     for copy in swaps:
         copy.wait()
+    own_out.wait()
 
 
 def gather_windows(orders, win_a, win_b, cells):
@@ -182,9 +189,11 @@
         ),
         in_specs=[pl.BlockSpec(memory_space=pltpu.VMEM)] * 2
         + [pl.BlockSpec(memory_space=pltpu.HBM)],
-        out_specs=[pl.BlockSpec(memory_space=pltpu.HBM)] * 3,
+        out_specs=[pl.BlockSpec(memory_space=pltpu.VMEM)] * 2
+        + [pl.BlockSpec(memory_space=pltpu.HBM)],
         scratch_shapes=[
-            pltpu.SemaphoreType.DMA((3,)),
+            pltpu.VMEM(cells.shape[1:], cells.dtype),
+            pltpu.SemaphoreType.DMA((4,)),
             pltpu.SemaphoreType.DMA((2, stages)),
             pltpu.SemaphoreType.DMA((2, stages)),
             pltpu.SemaphoreType.DMA((cells.shape[0] - 1,)),
@@ -206,6 +215,7 @@
     cells_out,
     land_a,
     land_b,
+    bounce,
     local_sem,
     send_sem,
     recv_sem,
@@ -215,11 +225,12 @@
     ins, outs, lands = (in_a, in_b), (out_a, out_b), (land_a, land_b)
     stage_count = len(orders[0])
     place = lax.axis_index("seq")
-    local = pltpu.make_async_copy(cells.at[place], cells_out.at[place], local_sem.at[0])
-    local.start()
+    own_in = pltpu.make_async_copy(cells.at[place], bounce, local_sem.at[0])
+    own_out = pltpu.make_async_copy(bounce, cells_out.at[place], local_sem.at[1])
+    own_in.start()
     greet(orders)
     swaps = exchange_copies(cells, cells_out, swap_send, swap_recv)
-    copies = []
+    copies = {}
 
     def source(part, step, keep):
         name, weight = orders[part][stage_count - 1 - step]
@@ -231,45 +242,51 @@
         base = (1 << stage_count) - (1 << (stage_count - step + 1))
         return lands[part].at[pl.ds(base + side * held, held)]
 
+    def base_of(step):
+        return (1 << stage_count) - (1 << (stage_count - step))
+
+    def send(part, step):
+        copy = pltpu.make_async_remote_copy(
+            src_ref=source(part, step, False),
+            dst_ref=lands[part].at[pl.ds(base_of(step), 1 << (stage_count - 1 - step))],
+            send_sem=send_sem.at[part, step],
+            recv_sem=recv_sem.at[part, step],
+            device_id=partner_of(*orders[part][stage_count - 1 - step]),
+            device_id_type=pl.DeviceIdType.MESH,
+        )
+        copy.start()
+        copies[part, step] = copy
+
+    for part in range(2):
+        send(part, 0)
+    for copy in swaps:
+        copy.start()
+    own_in.wait()
+    own_out.start()
     for step in range(stage_count):
-        held = 1 << (stage_count - 1 - step)
-        base = (1 << stage_count) - (1 << (stage_count - step))
         for part in range(2):
-            name, weight = orders[part][stage_count - 1 - step]
-            copy = pltpu.make_async_remote_copy(
-                src_ref=source(part, step, False),
-                dst_ref=lands[part].at[pl.ds(base, held)],
-                send_sem=send_sem.at[part, step],
-                recv_sem=recv_sem.at[part, step],
-                device_id=partner_of(name, weight),
-                device_id_type=pl.DeviceIdType.MESH,
-            )
-            copy.start()
-            copies.append(copy)
-        if step == 0:
-            for copy in swaps:
-                copy.start()
-        for part in range(2):
-            copies[2 * step + part].wait_recv()
+            copies[part, step].wait_recv()
             mine = source(part, step, True)
+            base = base_of(step)
             if step == stage_count - 1:
                 outs[part][...] = mine[0].astype(jnp.float32) + lands[part][base].astype(
                     jnp.float32
                 )
-            else:
-
-                def add_one(index, carry, mine=mine, part=part, base=base):
-                    land = lands[part].at[base + index]
-                    total = mine[index].astype(jnp.float32) + land[...].astype(jnp.float32)
-                    land[...] = total.astype(land.dtype)
-                    return carry
-
-                lax.fori_loop(0, held, add_one, 0)
-    for copy in copies:
+                continue
+
+            def add_one(index, carry, mine=mine, part=part, base=base):
+                land = lands[part].at[base + index]
+                total = mine[index].astype(jnp.float32) + land[...].astype(jnp.float32)
+                land[...] = total.astype(land.dtype)
+                return carry
+
+            lax.fori_loop(0, 1 << (stage_count - 1 - step), add_one, 0)
+            send(part, step + 1)
+    for copy in copies.values():
         copy.wait_send()
     for copy in swaps:
         copy.wait()
-    local.wait()
+    own_out.wait()
 
 
 def reduce_windows(orders, rows_a, rows_b, cells):
@@ -289,7 +306,8 @@
         scratch_shapes=[
             pltpu.VMEM((count - 1,) + rows_a.shape[1:], rows_a.dtype),
             pltpu.VMEM((count - 1,) + rows_b.shape[1:], rows_b.dtype),
-            pltpu.SemaphoreType.DMA((1,)),
+            pltpu.VMEM(cells.shape[1:], cells.dtype),
+            pltpu.SemaphoreType.DMA((2,)),
             pltpu.SemaphoreType.DMA((2, stages)),
             pltpu.SemaphoreType.DMA((2, stages)),
             pltpu.SemaphoreType.DMA((cells.shape[0] - 1,)),

time: 197 us -> 178 us (0.904)
  Pallas kernels: 184 us -> 165 us
    pallas_call x1, Pallas kernels: 52.1 us -> 36.8 us  [gather_windows(): pl.pallas_call(functools.partial(gather_kernel, orders), out_shape=(jax.S...]
    pallas_call x1, Pallas kernels: 38 us -> 34.4 us  [reduce_windows(): pl.pallas_call(functools.partial(reduce_kernel, orders), out_shape=(jax.S...]
where the time goes in v7:
time: 178 us; the launch traced here: 177 us
  Pallas kernels  165 us (93%)
  other arithmetic  10.5 us (6%)
    pallas_call x1, Pallas kernels, whole_step(): pl.pallas_call(functools.partial(step_kernel, places, shard_lengths), gri...  87.6 us
    pallas_call x1, Pallas kernels, gather_windows(): pl.pallas_call(functools.partial(gather_kernel, orders), out_shape=(jax.S...  36.8 us
    pallas_call x1, Pallas kernels, reduce_windows(): pl.pallas_call(functools.partial(reduce_kernel, orders), out_shape=(jax.S...  34.4 us
    pallas_call x1, Pallas kernels, prepare(): pl.pallas_call(prepare_kernel, grid_spec=pltpu.PrefetchScalarGridSpec(num...  5.94 us
    convert_element_type x1, other arithmetic, per_device(): results[:, :, C:].astype(jnp.float32)  4 us

profile of v7, /device:TPU:0, one launch (start us, length us, event | category | flops | bytes accessed | tf_op | source)
XLA Modules:
  0.0 177.2 jit_solution(2253367437707286529)
XLA Ops:
  0.7 0.9 convert_element_type.19
  1.6 0.5 dynamic_update_slice.7
  2.1 0.0 copy-start.5
  2.1 0.9 convert_element_type.18
  3.1 0.6 dynamic_update_slice.6
  3.6 0.0 copy-start.4
  3.7 5.9 %shard_map.211.cells = bf16[4,2,256,512]{3,2,1,0:T(8,128)(2,1)} custom-call(s32[8]{0:T(128)} %lengths_ref.3, s32[1]{0:T(128)} %bitcast.place_ref, f32[8,256,256]{2,1,0:T(8,128)} %inputs_ref.1, f32[8,128,256]{2,1,0:T(8,128)} %encoded_ref.1, s32[8,1,128]{2,1,0:T(1,128)} %bitcast.12, f32[8,256,256]{2,1,0:T(8,128)} %cotangent_ref.1), custom_call_target="tpu_custom_call" | custom-call | tf_op jit(solution)/shard_map/pallas_call | solution.py:977
  9.6 0.0 copy-done.5
  9.6 0.0 copy-done.4
  9.6 36.8 %shard_map.212 = (bf16[32,192,128]{2,1,0:T(8,128)(2,1)}, bf16[32,176,128]{2,1,0:T(8,128)(2,1)}, bf16[4,2,256,512]{3,2,1,0:T(8,128)(2,1)}) custom-call(bf16[192,128]{1,0:T(8,128)(2,1)} %bitcast.8, bf16[176,128]{1,0:T(8,128)(2,1)} %bitcast.9, bf16[4,2,256,512]{3,2,1,0:T(8,128)(2,1)} %shard_map.211.cells), custom_call_target="tpu_custom_call" | custom-call | tf_op jit(solution)/shard_map/pallas_call | solution.py:183
  46.4 87.6 %shard_map.213 = (bf16[4,2,256,512]{3,2,1,0:T(8,128)(2,1)}, bf16[32,192,128]{2,1,0:T(8,128)(2,1)}, bf16[32,176,128]{2,1,0:T(8,128)(2,1)}) custom-call(s32[8]{0:T(128)} %lengths_ref.3, s32[1]{0:T(128)} %bitcast.place_ref, bf16[4,2,256,512]{3,2,1,0:T(8,128)(2,1)} %get-tuple-element.21.cells_ref, f32[8,1024]{1,0:T(8,128)} %time_ref.1, ...), custom_call_target="tpu_custom_call" | custom-call | tf_op jit(solution)/shard_map/pallas_call | solution.py:925
  134.0 0.0 copy-start
  134.0 0.0 copy-start.7
  134.0 0.0 copy-start.6
  134.0 0.0 copy-start.2
  134.0 0.0 copy-start.8
  134.1 0.0 copy-start.9
  134.1 34.4 %shard_map.214 = (f32[192,128]{1,0:T(8,128)}, f32[176,128]{1,0:T(8,128)}, bf16[4,2,256,512]{3,2,1,0:T(8,128)(2,1)}) custom-call(bf16[32,192,128]{2,1,0:T(8,128)(2,1)} %get-tuple-element.24.in_a, bf16[32,176,128]{2,1,0:T(8,128)(2,1)} %get-tuple-element.25.in_b, bf16[4,2,256,512]{3,2,1,0:T(8,128)(2,1)} %get-tuple-element.26.cells), custom_call_target="tpu_custom_call" | custom-call | tf_op jit(solution)/shard_map/pallas_call | solution.py:295
  168.5 0.0 copy-done
  168.5 0.0 copy-done.7
  168.5 1.7 fusion.1
  170.2 0.0 copy-start.1
  170.2 0.0 copy-done.6
  170.2 0.7 multiply_add_fusion
  170.8 0.0 copy-done.2
  170.8 0.0 copy-done.8
  170.8 1.7 fusion
  172.5 0.0 copy-done.9
  172.5 0.7 multiply_add_fusion.2
  173.2 4.0 %slice_convert_fusion = (f32[8,256,256]{2,1,0:T(8,128)}, f32[8,256,256]{2,1,0:T(8,128)}) fusion(bf16[8,256,512]{2,1,0:T(8,128)(2,1)} %bitcast.7), kind=kLoop, calls=%fused_computation | loop fusion | flops 1048576 | bytes 6291456 | tf_op jit(solution)/shard_map/convert_element_type | solution.py:1042
  177.2 0.0 copy-done.1
  177.2 0.0 copy-done.3
  (3 shorter events, 0.0 us)
Async XLA Ops:
  2.1 7.5 %copy-start.5 = (bf16[22528]{0:T(1024)(128)(2,1)}, bf16[22528]{0:T(1024)(128)(2,1)S(1)}, u32[]{:S(2)}) copy-start(bf16[22528]{0:T(1024)(128)(2,1)S(1)} %dynamic_update_slice.7) | copy-start | bytes 135172
  3.6 6.0 %copy-start.4 = (bf16[24576]{0:T(1024)(128)(2,1)}, bf16[24576]{0:T(1024)(128)(2,1)S(1)}, u32[]{:S(2)}) copy-start(bf16[24576]{0:T(1024)(128)(2,1)S(1)} %dynamic_update_slice.6) | copy-start | bytes 147460
  134.0 34.4 %copy-start = (f32[22592]{0:T(1024)S(1)}, f32[22592]{0:T(1024)}, u32[]{:S(2)}) copy-start(f32[22592]{0:T(1024)} %param.18) | copy-start | bytes 271108
  134.0 34.5 %copy-start.7 = (f32[22592]{0:T(1024)S(1)}, f32[22592]{0:T(1024)}, u32[]{:S(2)}) copy-start(f32[22592]{0:T(1024)} %param.19) | copy-start | bytes 271108
  134.0 36.1 %copy-start.6 = (f32[22592]{0:T(1024)S(1)}, f32[22592]{0:T(1024)}, u32[]{:S(2)}) copy-start(f32[22592]{0:T(1024)} %param.20) | copy-start | bytes 271108
  134.0 36.8 %copy-start.2 = (f32[20624]{0:T(1024)S(1)}, f32[20624]{0:T(1024)}, u32[]{:S(2)}) copy-start(f32[20624]{0:T(1024)} %param.21) | copy-start | bytes 247492
  134.0 36.8 %copy-start.8 = (f32[20624]{0:T(1024)S(1)}, f32[20624]{0:T(1024)}, u32[]{:S(2)}) copy-start(f32[20624]{0:T(1024)} %param.22) | copy-start | bytes 247492
  134.1 38.4 %copy-start.9 = (f32[20624]{0:T(1024)S(1)}, f32[20624]{0:T(1024)}, u32[]{:S(2)}) copy-start(f32[20624]{0:T(1024)} %param.23) | copy-start | bytes 247492
  170.2 7.0 %copy-start.1 = (f32[22592]{0:T(1024)}, f32[22592]{0:T(1024)S(1)}, u32[]{:S(2)}) copy-start(f32[22592]{0:T(1024)S(1)} %get-tuple-element.35) | copy-start | bytes 271108
  172.5 4.7 %copy-start.3 = (f32[20624]{0:T(1024)}, f32[20624]{0:T(1024)S(1)}, u32[]{:S(2)}) copy-start(f32[20624]{0:T(1024)S(1)} %get-tuple-element.31) | copy-start | bytes 247492
